TPU v7x, 32 devices: a whole 2x2x4 slice. The times are simulated.
32 devices in a mesh: section: 2 (over core), seq: 4 (over z), head: 4 (over y, x).
Axes of the slice: x: 2, y: 2, z: 4, core: 2. Of those that a mesh axis runs over, the one named last changes fastest.
Arguments:
- inputs: bfloat16 [2, 2048, 1024], P(None, 'seq'), may hold values from -6 to 6
- positions: int32 [2, 2048], P(None, 'seq'), may hold values from 0 to 1535, as said below
- cotangent: bfloat16 [2, 2048, 1024], P(None, 'seq'), may hold values from -6 to 6
- qkv_weight: bfloat16 [2, 1024, 3, 1024], P('section', 'seq', None, 'head'), may hold values from -0.1875 to 0.1875
- out_weight: bfloat16 [2, 1024, 1024], P('section', 'seq', 'head'), may hold values from -1.5 to 1.5
- gate_up_weight: bfloat16 [2, 1024, 2, 2816], P('section', 'seq', None, 'head'), may hold values from -0.1875 to 0.1875
- down_weight: bfloat16 [2, 1024, 2816], P('section', 'seq', 'head'), may hold values from -0.109375 to 0.109375
- attn_gain: bfloat16 [2, 1024], P('section', 'seq'), may hold values from 0.5 to 1.5
- ffn_gain: bfloat16 [2, 1024], P('section', 'seq'), may hold values from 0.5 to 1.5
Outputs:
- activations: bfloat16 [2, 2, 2048, 1024], P('section', None, 'seq')
- input_grads: float32 [2, 2, 2048, 1024], P('section', None, 'seq')
- qkv_grad: float32 [2, 1024, 3, 1024], P('section', 'seq', None, 'head')
- out_grad: float32 [2, 1024, 1024], P('section', 'seq', 'head')
- gate_up_grad: float32 [2, 1024, 2, 2816], P('section', 'seq', None, 'head')
- down_grad: float32 [2, 1024, 2816], P('section', 'seq', 'head')
- attn_gain_grad: float32 [2, 1024], P('section', 'seq')
- ffn_gain_grad: float32 [2, 1024], P('section', 'seq')
Inputs may be any that keep to these rules, and one draw needn't show every extreme that they name: Each micro-batch is packed with documents laid end to end: a first document of 1 to 511 tokens, then one document of exactly 1536 tokens, then one or two documents that fill the rest; a token's position is its offset in its document, so positions rise by one inside a document and restart at 0 where the next begins.
All inputs are finite; a program needn't handle non-finite values.
Results may differ from a plain program's by a relative error of at most 0.03.
Values may be sent and summed in bfloat16 or wider, within the bound.
No kernel may reach another device: no remote copies, remote signals or barrier semaphores. Data moves between devices by JAX's collectives and lax.ppermute only.
A program may use at most 256 MiB of HBM per device.

v0:
```python
from functools import partial
import math

import jax
import jax.numpy as jnp
from jax import lax
from jax.sharding import PartitionSpec as P

HEAD_DIM = 64


masked = -1e30


def passed_along(shard, axis, by):
    peers = lax.axis_size(axis)
    pairs = [(i, i + by) for i in range(peers) if 0 <= i + by < peers]
    return lax.ppermute(shard, axis, pairs)


def angles(positions):
    half = HEAD_DIM // 2
    rates = 10000.0 ** (-jnp.arange(half, dtype=jnp.float32) / half)
    turned = positions.astype(jnp.float32)[:, None] * rates[None, :]
    return (jnp.cos(turned)[:, None, :], jnp.sin(turned)[:, None, :])


def rotate(vectors, cosine, sine):
    half = HEAD_DIM // 2
    first = vectors[..., :half]
    second = vectors[..., half:]
    return jnp.concatenate(
        [first * cosine - second * sine, second * cosine + first * sine], axis=-1
    )


def rotate_back(grads, cosine, sine):
    half = HEAD_DIM // 2
    first = grads[..., :half]
    second = grads[..., half:]
    return jnp.concatenate(
        [first * cosine + second * sine, second * cosine - first * sine], axis=-1
    )


def head_sum(partial_sum):
    return lax.psum(partial_sum.astype(jnp.bfloat16), "head").astype(jnp.float32)


def gather_keys(key_value, folder, initial):
    return folder(initial, lax.all_gather(key_value, "seq", axis=0, tiled=True), jnp.int32(0))


def block_rows(count, own_rows):
    return math.gcd(count, max(512, own_rows))


def fold_forward(state, key_value, start, context):
    queries, query_index, lowest = context
    count = key_value.shape[0]
    block = block_rows(count, queries.shape[0])
    heads = queries.shape[1]
    pieces = key_value.reshape(count // block, block, 2, heads, HEAD_DIM)
    offsets = jnp.arange(count // block, dtype=jnp.int32) * block
    scale = HEAD_DIM ** (-0.5)

    def fold_advance(carry, item):
        piece, offset = item
        peak, total, summed = carry
        key_index = offset + jnp.arange(block, dtype=jnp.int32)
        allowed = (
            (key_index[None, :] <= query_index[:, None]) & (key_index[None, :] >= lowest[:, None])
        )[None]
        scores = (
            jnp.einsum("qhd,khd->hqk", queries, piece[:, 0], preferred_element_type=jnp.float32)
            * scale
        )
        scores = jnp.where(allowed, scores, masked)
        fresh = jnp.maximum(peak, jnp.max(scores, axis=-1))
        weights = jnp.where(allowed, jnp.exp(scores - fresh[..., None]), 0.0)
        shrink = jnp.exp(peak - fresh)
        total = total * shrink + jnp.sum(weights, axis=-1)
        summed = summed * shrink[..., None] + jnp.einsum(
            "hqk,khd->hqd",
            weights.astype(jnp.bfloat16),
            piece[:, 1],
            preferred_element_type=jnp.float32,
        )
        return ((fresh, total, summed), None)

    state, unused = lax.scan(fold_advance, state, (pieces, offsets))
    return state


def grad_piece(key_value, context):
    queries, query_index, lowest, grad_out, logsum, delta = context
    count = key_value.shape[0]
    rows = queries.shape[0]
    block = block_rows(count, rows)
    heads = queries.shape[1]
    pieces = key_value.reshape(count // block, block, 2, heads, HEAD_DIM)
    offsets = jnp.arange(count // block, dtype=jnp.int32) * block
    scale = HEAD_DIM ** (-0.5)

    def grad_advance(carry, item):
        piece, offset = item
        key_index = offset + jnp.arange(block, dtype=jnp.int32)
        allowed = (
            (key_index[None, :] <= query_index[:, None]) & (key_index[None, :] >= lowest[:, None])
        )[None]
        keys = piece[:, 0]
        values = piece[:, 1]
        scores = (
            jnp.einsum("qhd,khd->hqk", queries, keys, preferred_element_type=jnp.float32) * scale
        )
        probs = jnp.where(allowed, jnp.exp(scores - logsum[..., None]), 0.0)
        grad_probs = jnp.einsum(
            "qhd,khd->hqk", grad_out, values, preferred_element_type=jnp.float32
        )
        grad_scores = (probs * (grad_probs - delta[..., None])).astype(jnp.bfloat16)
        carry = (
            carry
            + jnp.einsum("hqk,khd->qhd", grad_scores, keys, preferred_element_type=jnp.float32)
            * scale
        )
        grad_keys = (
            jnp.einsum("hqk,qhd->khd", grad_scores, queries, preferred_element_type=jnp.float32)
            * scale
        )
        grad_values = jnp.einsum(
            "hqk,qhd->khd", probs.astype(jnp.bfloat16), grad_out, preferred_element_type=jnp.float32
        )
        return (carry, jnp.stack([grad_keys, grad_values], axis=1))

    initial = jnp.zeros((rows, heads, HEAD_DIM), jnp.float32)
    grad_query, key_grads = lax.scan(grad_advance, initial, (pieces, offsets))
    return (grad_query, key_grads.reshape(count, 2, heads * HEAD_DIM))


def on_device(
    inputs,
    positions,
    cotangent,
    qkv_weight,
    out_weight,
    gate_up_weight,
    down_weight,
    attn_gain,
    ffn_gain,
):
    section_index = lax.axis_index("section")
    on_later = (section_index == 1).astype(jnp.float32)
    gathered = (
        lax.all_gather(qkv_weight, "seq", axis=1, tiled=True),
        lax.all_gather(out_weight, "seq", axis=1, tiled=True),
        lax.all_gather(gate_up_weight, "seq", axis=1, tiled=True),
        lax.all_gather(down_weight, "seq", axis=1, tiled=True),
        lax.all_gather(attn_gain, "seq", axis=1, tiled=True),
        lax.all_gather(ffn_gain, "seq", axis=1, tiled=True),
    )
    w_project = gathered[0][0]
    w_out = gathered[1][0]
    w_gate_up = gathered[2][0]
    w_down = gathered[3][0]
    gain_attn = gathered[4][0].astype(jnp.float32)
    gain_ffn = gathered[5][0].astype(jnp.float32)
    batches, rows, width = inputs.shape
    heads = w_project.shape[2] // HEAD_DIM
    local_width = heads * HEAD_DIM
    devices = lax.axis_size("seq")
    row_start = lax.axis_index("seq") * rows
    query_index = row_start + jnp.arange(rows, dtype=jnp.int32)
    split_shape = (rows, heads, HEAD_DIM)
    carried = jnp.zeros((rows, width + local_width), jnp.bfloat16)
    outputs = []
    kept_list = []
    for tick in range(batches + 1):
        batch = jnp.clip(tick - section_index, 0, batches - 1)
        offsets = lax.dynamic_index_in_dim(positions, batch, 0, keepdims=False)
        own_input = inputs[min(tick, batches - 1)]
        layer_in = jnp.where(section_index == 1, carried[:, :width], own_input).astype(jnp.float32)
        layer_lowest = query_index - offsets
        layer_inverse = lax.rsqrt(jnp.mean(layer_in * layer_in, axis=-1, keepdims=True) + 1e-06)
        layer_normed = (layer_in * layer_inverse * gain_attn).astype(jnp.bfloat16)
        project = jnp.einsum(
            "td,dce->tce", layer_normed, w_project, preferred_element_type=jnp.float32
        )
        layer_cosine, layer_sine = angles(offsets)
        layer_queries = rotate(project[:, 0].reshape(split_shape), layer_cosine, layer_sine).astype(
            jnp.bfloat16
        )
        keys = rotate(project[:, 1].reshape(split_shape), layer_cosine, layer_sine).astype(
            jnp.bfloat16
        )
        values = (
            (1.0 - 0.5 * on_later) * project[:, 2]
            + 0.5 * on_later * carried[:, width:].astype(jnp.float32)
        ).astype(jnp.bfloat16)
        layer_key_value = jnp.stack([keys.reshape(rows, local_width), values], axis=1)
        layer_context = (layer_queries, query_index, layer_lowest)
        layer_initial = (
            jnp.full((heads, rows), masked, jnp.float32),
            jnp.zeros((heads, rows), jnp.float32),
            jnp.zeros((heads, rows, HEAD_DIM), jnp.float32),
        )
        state = gather_keys(
            layer_key_value, partial(fold_forward, context=layer_context), layer_initial
        )
        peak, layer_total, summed = state
        layer_attended_full = jnp.transpose(summed / layer_total[..., None], (1, 0, 2)).reshape(
            rows, local_width
        )
        layer_logsum = peak + jnp.log(layer_total)
        layer_attended = layer_attended_full.astype(jnp.bfloat16)
        layer_hidden = layer_in + head_sum(
            jnp.einsum("ti,oi->to", layer_attended, w_out, preferred_element_type=jnp.float32)
        )
        layer_inverse_ffn = lax.rsqrt(
            jnp.mean(layer_hidden * layer_hidden, axis=-1, keepdims=True) + 1e-06
        )
        layer_normed_ffn = (layer_hidden * layer_inverse_ffn * gain_ffn).astype(jnp.bfloat16)
        layer_gate_up = jnp.einsum(
            "td,dcf->tcf", layer_normed_ffn, w_gate_up, preferred_element_type=jnp.float32
        )
        layer_active = (jax.nn.silu(layer_gate_up[:, 0]) * layer_gate_up[:, 1]).astype(jnp.bfloat16)
        output = layer_hidden + head_sum(
            jnp.einsum("tf,df->td", layer_active, w_down, preferred_element_type=jnp.float32)
        )
        layer_kept = (
            layer_in,
            layer_inverse,
            layer_normed,
            layer_queries,
            layer_key_value,
            layer_attended_full,
            layer_logsum,
            layer_hidden,
            layer_inverse_ffn,
            layer_normed_ffn,
            layer_gate_up,
            layer_active,
        )
        output, values, kept = (output, values, layer_kept)
        output_low = output.astype(jnp.bfloat16)
        outputs.append(output_low)
        kept_list.append(kept)
        if tick < batches:
            carried = passed_along(jnp.concatenate([output_low, values], axis=1), "section", 1)
    stacked = tuple(
        (jnp.stack([entry[index] for entry in kept_list]) for index in range(len(kept_list[0])))
    )
    activations = lax.dynamic_slice_in_dim(jnp.stack(outputs), section_index, batches, 0)[None]
    incoming = jnp.zeros((rows, width + local_width), jnp.bfloat16)
    grad_list = []
    totals = None
    for tick in range(batches + 1):
        order = tick - 1 + section_index
        batch = jnp.clip(order, 0, batches - 1)
        valid = ((order >= 0) & (order < batches)).astype(jnp.float32)
        source = jnp.clip(order + section_index, 0, batches)
        kept = tuple(
            (lax.dynamic_index_in_dim(entry, source, 0, keepdims=False) for entry in stacked)
        )
        offsets = lax.dynamic_index_in_dim(positions, batch, 0, keepdims=False)
        own_grad = cotangent[min(tick, batches - 1)]
        grad_in = (
            jnp.where(section_index == 1, own_grad, incoming[:, :width]).astype(jnp.float32) * valid
        )
        (
            layer_layer_in,
            inverse,
            normed,
            queries,
            key_value,
            attended_full,
            logsum,
            hidden,
            inverse_ffn,
            normed_ffn,
            gate_up,
            active,
        ) = kept
        lowest = query_index - offsets
        cosine, sine = angles(offsets)
        grad_branch = grad_in.astype(jnp.bfloat16)
        gate = gate_up[:, 0]
        upward = gate_up[:, 1]
        sigmoid = jax.nn.sigmoid(gate)
        grad_down = jnp.einsum("td,tf->df", grad_branch, active, preferred_element_type=jnp.float32)
        grad_active = jnp.einsum(
            "td,df->tf", grad_branch, w_down, preferred_element_type=jnp.float32
        )
        grad_gate = grad_active * upward * sigmoid * (1.0 + gate * (1.0 - sigmoid))
        grad_up = grad_active * jax.nn.silu(gate)
        grad_gate_up = jnp.stack([grad_gate, grad_up], axis=1).astype(jnp.bfloat16)
        grad_gate_up_weight = jnp.einsum(
            "td,tcf->dcf", normed_ffn, grad_gate_up, preferred_element_type=jnp.float32
        )
        grad_normed_ffn = head_sum(
            jnp.einsum("tcf,dcf->td", grad_gate_up, w_gate_up, preferred_element_type=jnp.float32)
        )
        scaled_ffn = hidden * inverse_ffn
        grad_gain_ffn = jnp.sum(grad_normed_ffn * scaled_ffn, axis=0)
        grad_scaled_ffn = grad_normed_ffn * gain_ffn
        grad_hidden = grad_in + inverse_ffn * (
            grad_scaled_ffn
            - scaled_ffn * jnp.mean(grad_scaled_ffn * scaled_ffn, axis=-1, keepdims=True)
        )
        grad_attn_branch = grad_hidden.astype(jnp.bfloat16)
        attended = attended_full.astype(jnp.bfloat16)
        grad_out_weight = jnp.einsum(
            "to,ti->oi", grad_attn_branch, attended, preferred_element_type=jnp.float32
        )
        grad_attended = jnp.einsum(
            "to,oi->ti", grad_attn_branch, w_out, preferred_element_type=jnp.float32
        ).astype(jnp.bfloat16)
        grad_out_split = grad_attended.reshape(split_shape)
        delta = jnp.transpose(
            jnp.sum(
                grad_out_split.astype(jnp.float32) * attended_full.reshape(split_shape), axis=-1
            )
        )
        context = (queries, query_index, lowest, grad_out_split, logsum, delta)

        def fold_back(carry, piece, start):
            part_query, part_grads = grad_piece(piece, context)
            return (part_query, part_grads)

        initial = (
            jnp.zeros(split_shape, jnp.float32),
            jnp.zeros((rows * devices, 2, local_width), jnp.float32),
        )
        grad_query, key_grads = gather_keys(key_value, fold_back, initial)
        mine = lax.psum_scatter(
            key_grads.astype(jnp.bfloat16), "seq", scatter_dimension=0, tiled=True
        ).astype(jnp.float32)
        grad_query_raw = (
            rotate_back(grad_query, cosine, sine).reshape(rows, local_width).astype(jnp.bfloat16)
        )
        grad_key_raw = (
            rotate_back(mine[:, 0].reshape(split_shape), cosine, sine)
            .reshape(rows, local_width)
            .astype(jnp.bfloat16)
        )
        grad_mixed = mine[:, 1]
        grad_value_raw = (
            (1.0 - 0.5 * on_later) * grad_mixed + incoming[:, width:].astype(jnp.float32)
        ).astype(jnp.bfloat16)
        grad_first_out = (0.5 * on_later * grad_mixed).astype(jnp.bfloat16)
        grad_project = jnp.stack([grad_query_raw, grad_key_raw, grad_value_raw], axis=1)
        grad_project_weight = jnp.einsum(
            "td,tce->dce", normed, grad_project, preferred_element_type=jnp.float32
        )
        grad_normed = head_sum(
            jnp.einsum("tce,dce->td", grad_project, w_project, preferred_element_type=jnp.float32)
        )
        scaled = layer_layer_in * inverse
        grad_gain_attn = jnp.sum(grad_normed * scaled, axis=0)
        grad_scaled = grad_normed * gain_attn
        grad_layer_in = grad_hidden + inverse * (
            grad_scaled - scaled * jnp.mean(grad_scaled * scaled, axis=-1, keepdims=True)
        )
        terms = (
            grad_project_weight,
            grad_out_weight,
            grad_gate_up_weight,
            grad_down,
            grad_gain_attn,
            grad_gain_ffn,
        )
        grad_layer_in, grad_first_out, terms = (grad_layer_in, grad_first_out, terms)
        grad_list.append(grad_layer_in)
        if totals is None:
            totals = terms
        else:
            totals = tuple((total + term for total, term in zip(totals, terms)))
        if tick < batches:
            incoming = passed_along(
                jnp.concatenate([grad_layer_in.astype(jnp.bfloat16), grad_first_out], axis=1),
                "section",
                -1,
            )
    input_grads = lax.dynamic_slice_in_dim(jnp.stack(grad_list), 1 - section_index, batches, 0)[
        None
    ]
    final = (
        lax.psum_scatter(
            totals[0][None].astype(jnp.bfloat16), "seq", scatter_dimension=1, tiled=True
        ).astype(jnp.float32),
        lax.psum_scatter(
            totals[1][None].astype(jnp.bfloat16), "seq", scatter_dimension=1, tiled=True
        ).astype(jnp.float32),
        lax.psum_scatter(
            totals[2][None].astype(jnp.bfloat16), "seq", scatter_dimension=1, tiled=True
        ).astype(jnp.float32),
        lax.psum_scatter(
            totals[3][None].astype(jnp.bfloat16), "seq", scatter_dimension=1, tiled=True
        ).astype(jnp.float32),
        lax.psum_scatter(
            totals[4][None].astype(jnp.bfloat16), "seq", scatter_dimension=1, tiled=True
        ).astype(jnp.float32),
        lax.psum_scatter(
            totals[5][None].astype(jnp.bfloat16), "seq", scatter_dimension=1, tiled=True
        ).astype(jnp.float32),
    )
    return (activations, input_grads, final[0], final[1], final[2], final[3], final[4], final[5])


def solution(mesh):
    placed = (
        P(None, "seq", None),
        P(None, "seq"),
        P(None, "seq", None),
        P("section", "seq", None, "head"),
        P("section", "seq", "head"),
        P("section", "seq", None, "head"),
        P("section", "seq", "head"),
        P("section", "seq"),
        P("section", "seq"),
    )
    return jax.shard_map(
        on_device,
        mesh=mesh,
        in_specs=placed,
        out_specs=(
            P("section", None, "seq", None),
            P("section", None, "seq", None),
            P("section", "seq", None, "head"),
            P("section", "seq", "head"),
            P("section", "seq", None, "head"),
            P("section", "seq", "head"),
            P("section", "seq"),
            P("section", "seq"),
        ),
        check_vma=False,
    )
```

profile of v0, /device:TPU:0, one launch (start us, length us, event | category | flops | bytes accessed | tf_op | source)
XLA Modules:
  0.0 1741.6 jit_solution(11160887800026842267)
XLA Ops:
  14.2 12.6 all_gather.36
  29.8 20.8 %all-gather.13.cloned.1.call-done = bf16[1,1024,3,256]{1,3,2,0:T(8,128)(2,1)} async-done(((bf16[1,256,3,256]{1,3,2,0:T(8,128)(2,1)}), bf16[1,1024,3,256]{1,3,2,0:T(8,128)(2,1)}) %all-gather.13.cloned.1.call-update) | async-done | bytes 1572880 | tf_op jit(solution)/shard_map/all_gather | solution.py:154
  55.0 17.2 all_gather.39
  72.2 30.7 %all-gather.15.cloned.1.call-done = bf16[2048,2,256]{0,2,1:T(8,128)(2,1)} async-done(((bf16[512,2,256]{0,2,1:T(8,128)(2,1)}), bf16[2048,2,256]{0,2,1:T(8,128)(2,1)}) %all-gather.15.cloned.1.call-update) | async-done | bytes 2097168 | tf_op jit(solution)/shard_map/all_gather | solution.py:51
  103.0 4.5 reshape.1381
  107.4 3.5 copy.143
  110.9 41.5 %while.84 = (s32[]{:T(128)}, f32[4,512]{1,0:T(4,128)S(1)}, f32[4,512]{1,0:T(4,128)S(1)}, f32[4,512,64]{1,2,0:T(8,128)S(1)}, s32[4]{0:T(128)S(1)}, /*index=5*/s32...) while((s32[]{:T(128)}, f32[4,512]{1,0:T(4,128)S(1)}, ...), condition=%wide.region_4.5_spmd.clone, body=%wide.region_1.4_spmd.clone.sunk | while | flops 283257856 | bytes 33433772 | solution.py:91
  156.0 9.4 all_gather.40
  165.4 41.5 %all-reduce.13.cloned.1.call-done = bf16[512,1024]{0,1:T(8,128)(2,1)} async-done(((bf16[512,1024]{0,1:T(8,128)(2,1)}), bf16[512,1024]{0,1:T(8,128)(2,1)}) %all-reduce.13.cloned.1.call-update) | async-done | bytes 1048592 | tf_op jit(solution)/shard_map/psum | solution.py:47
  208.7 58.8 %all-gather.17.cloned.1.call-done = bf16[1,1024,2,704]{1,3,2,0:T(8,128)(2,1)} async-done(((bf16[1,256,2,704]{1,3,2,0:T(8,128)(2,1)}), bf16[1,1024,2,704]{1,3,2,0:T(8,128)(2,1)}) %all-gather.17.cloned.1.call-update) | async-done | bytes 2883600 | tf_op jit(solution)/shard_map/all_gather | solution.py:156
  267.5 5.2 fusion.112
  272.6 30.1 %all-gather.19.cloned.1.call-done = bf16[1,1024,704]{1,2,0:T(8,128)(2,1)} async-done(((bf16[1,256,704]{1,2,0:T(8,128)(2,1)}), bf16[1,1024,704]{1,2,0:T(8,128)(2,1)}) %all-gather.19.cloned.1.call-update) | async-done | bytes 1441808 | tf_op jit(solution)/shard_map/all_gather | solution.py:157
  302.7 4.3 convolution_convert_fusion.5
  307.1 50.9 %all-reduce.15.cloned.1.call-done = bf16[512,1024]{0,1:T(8,128)(2,1)} async-done(((bf16[512,1024]{0,1:T(8,128)(2,1)}), bf16[512,1024]{0,1:T(8,128)(2,1)}) %all-reduce.15.cloned.1.call-update) | async-done | bytes 1048592 | tf_op jit(solution)/shard_map/psum | solution.py:47
  358.0 3.5 fusion.348
  376.6 46.0 %all-gather.21.cloned.1.call-done = bf16[2048,2,256]{0,2,1:T(8,128)(2,1)} async-done(((bf16[512,2,256]{0,2,1:T(8,128)(2,1)}), bf16[2048,2,256]{0,2,1:T(8,128)(2,1)}) %all-gather.21.cloned.1.call-update) | async-done | bytes 2097168 | tf_op jit(solution)/shard_map/all_gather | solution.py:51
  422.6 4.5 reshape.1382
  427.0 3.4 copy.149
  430.5 41.5 %while.85 = (s32[]{:T(128)}, f32[4,512]{1,0:T(4,128)S(1)}, f32[4,512]{1,0:T(4,128)S(1)}, f32[4,512,64]{1,2,0:T(8,128)S(1)}, s32[4]{0:T(128)S(1)}, /*index=5*/s32...) while((s32[]{:T(128)}, f32[4,512]{1,0:T(4,128)S(1)}, ...), condition=%wide.region_12.13_spmd.clone, body=%wide.region_9.12_spmd.clone.sunk | while | flops 283257856 | bytes 33433772 | solution.py:91
  474.8 51.0 %all-reduce.17.cloned.1.call-done = bf16[512,1024]{0,1:T(8,128)(2,1)} async-done(((bf16[512,1024]{0,1:T(8,128)(2,1)}), bf16[512,1024]{0,1:T(8,128)(2,1)}) %all-reduce.17.cloned.1.call-update) | async-done | bytes 1048592 | tf_op jit(solution)/shard_map/psum | solution.py:47
  527.5 3.7 fusion.110
  534.9 52.6 %all-reduce.19.cloned.1.call-done = bf16[512,1024]{0,1:T(8,128)(2,1)} async-done(((bf16[512,1024]{0,1:T(8,128)(2,1)}), bf16[512,1024]{0,1:T(8,128)(2,1)}) %all-reduce.19.cloned.1.call-update) | async-done | bytes 1048592 | tf_op jit(solution)/shard_map/psum | solution.py:47
  587.6 3.9 fusion.346
  601.6 46.0 %all-gather.23.cloned.1.call-done = bf16[2048,2,256]{0,2,1:T(8,128)(2,1)} async-done(((bf16[512,2,256]{0,2,1:T(8,128)(2,1)}), bf16[2048,2,256]{0,2,1:T(8,128)(2,1)}) %all-gather.23.cloned.1.call-update) | async-done | bytes 2097168 | tf_op jit(solution)/shard_map/all_gather | solution.py:51
  647.6 4.5 reshape.1383
  652.1 3.5 copy.154
  655.5 41.5 %while.86 = (s32[]{:T(128)}, f32[4,512]{1,0:T(4,128)S(1)}, f32[4,512]{1,0:T(4,128)S(1)}, f32[4,512,64]{1,2,0:T(8,128)S(1)}, s32[4]{0:T(128)S(1)}, /*index=5*/s32...) while((s32[]{:T(128)}, f32[4,512]{1,0:T(4,128)S(1)}, ...), condition=%wide.region_20.21_spmd.clone, body=%wide.region_17.20_spmd.clone.sunk | while | flops 283257856 | bytes 33433772 | solution.py:91
  708.1 42.7 %all-reduce.21.cloned.1.call-done = bf16[512,1024]{0,1:T(8,128)(2,1)} async-done(((bf16[512,1024]{0,1:T(8,128)(2,1)}), bf16[512,1024]{0,1:T(8,128)(2,1)}) %all-reduce.21.cloned.1.call-update) | async-done | bytes 1048592 | tf_op jit(solution)/shard_map/psum | solution.py:47
  757.6 3.8 dynamic-slice_bitcast_fusion.6
  767.2 30.9 %all-gather.25.cloned.1.call-done = bf16[1,2048,2,256]{1,3,2,0:T(8,128)(2,1)} async-done(((bf16[1,512,2,256]{1,3,2,0:T(8,128)(2,1)}), bf16[1,2048,2,256]{1,3,2,0:T(8,128)(2,1)}) %all-gather.25.cloned.1.call-update) | async-done | bytes 2097168 | tf_op jit(solution)/shard_map/all_gather | solution.py:51
  798.2 4.5 reshape.1384
  802.7 3.6 copy.161
  813.7 39.4 %all-reduce.23.cloned.1.call-done = bf16[512,1024]{0,1:T(8,128)(2,1)} async-done(((bf16[512,1024]{0,1:T(8,128)(2,1)}), bf16[512,1024]{0,1:T(8,128)(2,1)}) %all-reduce.23.cloned.1.call-update) | async-done | bytes 1048592 | tf_op jit(solution)/shard_map/psum | solution.py:47
  861.0 41.3 %while.87 = (s32[]{:T(128)}, f32[512,4,64]{0,2,1:T(8,128)}, bf16[4,512,2,4,64]{1,4,3,2,0:T(8,128)(2,1)}, bf16[4,512,2,4,64]{1,4,3,2,0:T(8,128)(2,1)}, s32[4]{0:T...) while((s32[]{:T(128)}, f32[512,4,64]{0,2,1:T(8,128)}, ...), condition=%wide.region_28.29_spmd.clone, body=%wide.region_27.28_spmd.clone.sunk | while | flops 684065792 | bytes 25201312 | solution.py:136
  908.4 43.9 %reduce-scatter.14.cloned.1.call-done = bf16[512,2,256]{0,2,1:T(8,128)(2,1)} async-done(((bf16[2048,2,256]{0,2,1:T(8,128)(2,1)}), bf16[512,2,256]{0,2,1:T(8,128)(2,1)}) %reduce-scatter.14.cloned.1.call-update) | async-done | bytes 524304 | tf_op jit(solution)/shard_map/reduce_scatter | solution.py:334
  959.1 6.3 pad_maximum_fusion.2
  965.4 44.0 %all-reduce.25.cloned.1.call-done = bf16[512,1024]{0,1:T(8,128)(2,1)} async-done(((bf16[512,1024]{0,1:T(8,128)(2,1)}), bf16[512,1024]{0,1:T(8,128)(2,1)}) %all-reduce.25.cloned.1.call-update) | async-done | bytes 1048592 | tf_op jit(solution)/shard_map/psum | solution.py:47
  1012.8 3.4 fusion.350
  1031.3 25.6 %all-gather.27.cloned.1.call-done = bf16[1,2048,2,256]{1,3,2,0:T(8,128)(2,1)} async-done(((bf16[1,512,2,256]{1,3,2,0:T(8,128)(2,1)}), bf16[1,2048,2,256]{1,3,2,0:T(8,128)(2,1)}) %all-gather.27.cloned.1.call-update) | async-done | bytes 2097168 | tf_op jit(solution)/shard_map/all_gather | solution.py:51
  1056.9 4.5 reshape.1387
  1064.8 47.2 %all-reduce.27.cloned.1.call-done = bf16[512,1024]{0,1:T(8,128)(2,1)} async-done(((bf16[512,1024]{0,1:T(8,128)(2,1)}), bf16[512,1024]{0,1:T(8,128)(2,1)}) %all-reduce.27.cloned.1.call-update) | async-done | bytes 1048592 | tf_op jit(solution)/shard_map/psum | solution.py:47
  1120.7 39.8 %while.88 = (s32[]{:T(128)}, f32[512,4,64]{0,2,1:T(8,128)}, bf16[4,512,2,4,64]{1,4,3,2,0:T(8,128)(2,1)}, bf16[4,512,2,4,64]{1,4,3,2,0:T(8,128)(2,1)}, s32[4]{0:T...) while((s32[]{:T(128)}, f32[512,4,64]{0,2,1:T(8,128)}, ...), condition=%wide.region_36.37_spmd.clone, body=%wide.region_35.36_spmd.clone.sunk | while | flops 684065792 | bytes 26249916 | solution.py:136
  1166.6 44.0 %reduce-scatter.16.cloned.1.call-done = bf16[512,2,256]{0,2,1:T(8,128)(2,1)} async-done(((bf16[2048,2,256]{0,2,1:T(8,128)(2,1)}), bf16[512,2,256]{0,2,1:T(8,128)(2,1)}) %reduce-scatter.16.cloned.1.call-update) | async-done | bytes 524304 | tf_op jit(solution)/shard_map/reduce_scatter | solution.py:334
  1218.4 49.8 %all-reduce.29.cloned.1.call-done = bf16[512,1024]{0,1:T(8,128)(2,1)} async-done(((bf16[512,1024]{0,1:T(8,128)(2,1)}), bf16[512,1024]{0,1:T(8,128)(2,1)}) %all-reduce.29.cloned.1.call-update) | async-done | bytes 1048592 | tf_op jit(solution)/shard_map/psum | solution.py:47
  1271.6 3.5 fusion.352
  1277.5 4.0 collective-permute-done.3
  1289.0 26.5 %all-gather.29.cloned.1.call-done = bf16[1,2048,2,256]{1,3,2,0:T(8,128)(2,1)} async-done(((bf16[1,512,2,256]{1,3,2,0:T(8,128)(2,1)}), bf16[1,2048,2,256]{1,3,2,0:T(8,128)(2,1)}) %all-gather.29.cloned.1.call-update) | async-done | bytes 2097168 | tf_op jit(solution)/shard_map/all_gather | solution.py:51
  1315.5 4.5 reshape.1390
  1320.0 3.4 copy.174
  1323.4 47.1 %all-reduce.31.cloned.1.call-done = bf16[512,1024]{0,1:T(8,128)(2,1)} async-done(((bf16[512,1024]{0,1:T(8,128)(2,1)}), bf16[512,1024]{0,1:T(8,128)(2,1)}) %all-reduce.31.cloned.1.call-update) | async-done | bytes 1048592 | tf_op jit(solution)/shard_map/psum | solution.py:47
  1378.6 33.2 %while.89 = (s32[]{:T(128)}, f32[512,4,64]{0,2,1:T(8,128)S(1)}, bf16[4,512,2,4,64]{1,4,3,2,0:T(8,128)(2,1)}, bf16[4,512,2,4,64]{1,4,3,2,0:T(8,128)(2,1)}, s32[4]...) while((s32[]{:T(128)}, f32[512,4,64]{0,2,1:T(8,128)S(1)}, ...), condition=%wide.region_44.45_spmd.clone, body=%wide.region_43.44_spmd.clone.sunk | while | flops 684065792 | bytes 26249916 | solution.py:136
  1411.8 4.6 copy.175
  1416.4 4.6 convert_element_type.731
  1421.1 3.5 convolution_convert_fusion.3
  1424.5 40.5 %reduce-scatter.18.cloned.1.call-done = bf16[512,2,256]{0,2,1:T(8,128)(2,1)} async-done(((bf16[2048,2,256]{0,2,1:T(8,128)(2,1)}), bf16[512,2,256]{0,2,1:T(8,128)(2,1)}) %reduce-scatter.18.cloned.1.call-update) | async-done | bytes 524304 | tf_op jit(solution)/shard_map/reduce_scatter | solution.py:334
  1489.8 49.9 %all-reduce.33.cloned.1.call-done = (bf16[512,1024]{0,1:T(8,128)(2,1)}, bf16[512,1024]{0,1:T(8,128)(2,1)}) async-done(((bf16[512,1024]{0,1:T(8,128)(2,1)}, bf16[512,1024]{0,1:T(8,128)(2,1)}), (bf16[512,1024]{0,1:T(8,128)(2,1)}, bf16[512,1024]{0,1:T(8,128)(2,1)})) %all-reduce.33.cloned.1.call-update) | async-done | bytes 2097168 | tf_op jit(solution)/shard_map/psum | solution.py:47
  1539.8 4.4 fusion.347
  1553.0 5.4 fusion.181
  1570.2 13.8 reduce-scatter.22.cloned.1.call-done
  1585.5 32.8 %reduce-scatter.26.cloned.1.call-done = bf16[1,256,704]{1,2,0:T(8,128)(2,1)} async-done(((bf16[1,1024,704]{1,2,0:T(8,128)(2,1)}), bf16[1,256,704]{1,2,0:T(8,128)(2,1)}) %reduce-scatter.26.cloned.1.call-update) | async-done | bytes 360464 | tf_op jit(solution)/shard_map/reduce_scatter | solution.py:396
  1625.9 5.5 copy.179
  1633.9 3.9 copy.158
  1640.6 34.4 %reduce-scatter.20.cloned.1.call-done = bf16[1,256,3,256]{3,1,2,0:T(8,128)(2,1)} async-done(((bf16[1,1024,3,256]{3,1,2,0:T(8,128)(2,1)}), bf16[1,256,3,256]{3,1,2,0:T(8,128)(2,1)}) %reduce-scatter.20.cloned.1.call-update) | async-done | bytes 393232 | tf_op jit(solution)/shard_map/reduce_scatter | solution.py:387
  1676.9 55.6 %reduce-scatter.24.cloned.1.call-done = bf16[1,256,2,704]{1,3,2,0:T(8,128)(2,1)} async-done(((bf16[1,1024,2,704]{1,3,2,0:T(8,128)(2,1)}), bf16[1,256,2,704]{1,3,2,0:T(8,128)(2,1)}) %reduce-scatter.24.cloned.1.call-update) | async-done | bytes 720912 | tf_op jit(solution)/shard_map/reduce_scatter | solution.py:393
  (924 shorter events, 470.4 us)
Async XLA Ops:
  7.2 43.4 %all-gather.13.cloned.1.call-start = ((), (), s32[]{:S(2)}) async-start(), calls=%async_computation.9 | async-start | bytes 1966080 | tf_op jit(solution)/shard_map/all_gather | solution.py:154
  9.2 93.8 %all-gather.15.cloned.1.call-start = ((), (), s32[]{:S(2)}) async-start(), calls=%async_computation.10 | async-start | bytes 2621440 | tf_op jit(solution)/shard_map/all_gather | solution.py:51
  14.2 343.8 %copy-start.3 = (bf16[1,512,1024]{1,2,0:T(8,128)(2,1)}, bf16[1,512,1024]{1,2,0:T(8,128)(2,1)S(1)}, u32[]{:S(2)}) copy-start(bf16[1,512,1024]{1,2,0:T(8,128)(2,1)S(1)} %copy.241) | copy-start | bytes 3145732
  26.8 344.6 %copy-start.112 = (f32[1,1024]{1,0:T(1,128)}, f32[1,1024]{1,0:T(1,128)S(1)}, u32[]{:S(2)}) copy-start(f32[1,1024]{1,0:T(1,128)S(1)} %mul.1375) | copy-start | bytes 12292
  53.3 54.1 %copy-start.83 = (bf16[512,4,32]{0,2,1:T(8,128)(2,1)}, bf16[512,4,32]{0,2,1:T(8,128)(2,1)S(1)}, u32[]{:S(2)}) copy-start(bf16[512,4,32]{0,2,1:T(8,128)(2,1)S(1)} %get-tuple-element.976) | copy-start | bytes 393220
  54.9 152.0 %all-reduce.13.cloned.1.call-start = ((), (), s32[]{:S(2)}) async-start(), calls=%async_computation.11 | async-start | bytes 2097152 | tf_op jit(solution)/shard_map/psum | solution.py:47
  72.2 786.7 %copy-start.14 = (bf16[1,1024,256]{2,1,0:T(8,128)(2,1)}, bf16[1,1024,256]{2,1,0:T(8,128)(2,1)S(1)}, u32[]{:S(2)}) copy-start(bf16[1,1024,256]{2,1,0:T(8,128)(2,1)S(1)} %all_gather.39) | copy-start | bytes 1572868
  154.7 112.7 %all-gather.17.cloned.1.call-start = ((), (), s32[]{:S(2)}) async-start(), calls=%async_computation.12 | async-start | bytes 3604480 | tf_op jit(solution)/shard_map/all_gather | solution.py:156
  155.3 147.4 %all-gather.19.cloned.1.call-start = ((), (), s32[]{:S(2)}) async-start(), calls=%async_computation.13 | async-start | bytes 1802240 | tf_op jit(solution)/shard_map/all_gather | solution.py:157
  155.9 202.0 %all-reduce.15.cloned.1.call-start = ((), (), s32[]{:S(2)}) async-start(), calls=%async_computation.14 | async-start | bytes 2097152 | tf_op jit(solution)/shard_map/psum | solution.py:47
  165.4 192.6 %copy-start.103 = (f32[1,1024]{1,0:T(1,128)}, f32[1,1024]{1,0:T(1,128)S(1)}, u32[]{:S(2)}) copy-start(f32[1,1024]{1,0:T(1,128)S(1)} %mul.1376) | copy-start | bytes 12292
  206.9 60.6 %copy-start.66 = (bf16[512,1024]{0,1:T(8,128)(2,1)S(1)}, bf16[512,1024]{0,1:T(8,128)(2,1)}, u32[]{:S(2)}) copy-start(bf16[512,1024]{0,1:T(8,128)(2,1)} %all-reduce.13.cloned.1.call-done) | copy-start | bytes 3145732
  208.7 149.3 %copy-start.166 = (f32[512]{0:T(512)}, f32[512]{0:T(512)S(1)}, u32[]{:S(2)}) copy-start(f32[512]{0:T(512)S(1)} %add_rsqrt_fusion.4) | copy-start | bytes 6148
  307.0 55.5 %copy-start.75 = (bf16[512,1,256]{0,2,1:T(8,128)(2,1)S(1)}, bf16[512,1,256]{0,2,1:T(8,128)(2,1)}, u32[]{:S(2)}) copy-start(bf16[512,1,256]{0,2,1:T(8,128)(2,1)} %copy-done.74) | copy-start | bytes 786436
  307.0 115.5 %all-gather.21.cloned.1.call-start = ((), (), s32[]{:S(2)}) async-start(), calls=%async_computation.15 | async-start | bytes 2621440 | tf_op jit(solution)/shard_map/all_gather | solution.py:51
  363.6 4.7 collective-permute-start
  376.4 149.3 %all-reduce.17.cloned.1.call-start = ((), (), s32[]{:S(2)}) async-start(), calls=%async_computation.16 | async-start | bytes 2097152 | tf_op jit(solution)/shard_map/psum | solution.py:47
  472.9 54.6 %copy-start.104 = (f32[1,1024]{1,0:T(1,128)S(1)}, f32[1,1024]{1,0:T(1,128)}, u32[]{:S(2)}) copy-start(f32[1,1024]{1,0:T(1,128)} %copy-done.103) | copy-start | bytes 12292
  474.3 113.2 %all-reduce.19.cloned.1.call-start = ((), (), s32[]{:S(2)}) async-start(), calls=%async_computation.17 | async-start | bytes 2097152 | tf_op jit(solution)/shard_map/psum | solution.py:47
  527.5 60.1 %copy-start.150 = (f32[512]{0:T(512)}, f32[512]{0:T(512)S(1)}, u32[]{:S(2)}) copy-start(f32[512]{0:T(512)S(1)} %add_rsqrt_fusion.2) | copy-start | bytes 6148
  532.7 54.8 %copy-start.113 = (f32[1,1024]{1,0:T(1,128)S(1)}, f32[1,1024]{1,0:T(1,128)}, u32[]{:S(2)}) copy-start(f32[1,1024]{1,0:T(1,128)} %copy-done.112) | copy-start | bytes 12292
  532.7 54.8 %copy-start.148 = (f32[512]{0:T(512)S(1)}, f32[512]{0:T(512)}, u32[]{:S(2)}) copy-start(f32[512]{0:T(512)} %copy-done.147) | copy-start | bytes 6148
  534.9 56.6 %copy-start.73 = (bf16[512,256]{0,1:T(8,128)(2,1)S(1)}, bf16[512,256]{0,1:T(8,128)(2,1)}, u32[]{:S(2)}) copy-start(bf16[512,256]{0,1:T(8,128)(2,1)} %copy-done.72) | copy-start | bytes 786436
  534.9 112.7 %all-gather.23.cloned.1.call-start = ((), (), s32[]{:S(2)}) async-start(), calls=%async_computation.18 | async-start | bytes 2621440 | tf_op jit(solution)/shard_map/all_gather | solution.py:51
  591.6 4.7 collective-permute-start.1
  597.8 156.1 %copy-start.19 = (bf16[512,1024]{0,1:T(8,128)(2,1)}, bf16[512,1024]{0,1:T(8,128)(2,1)S(1)}, u32[]{:S(2)}) copy-start(bf16[512,1024]{0,1:T(8,128)(2,1)S(1)} %get-tuple-element.883) | copy-start | bytes 3145732
  601.5 149.3 %all-reduce.21.cloned.1.call-start = ((), (), s32[]{:S(2)}) async-start(), calls=%async_computation.19 | async-start | bytes 2097152 | tf_op jit(solution)/shard_map/psum | solution.py:47
  699.4 98.8 %all-gather.25.cloned.1.call-start = ((), (), s32[]{:S(2)}) async-start(), calls=%async_computation.32 | async-start | bytes 2621440 | tf_op jit(solution)/shard_map/all_gather | solution.py:51
  706.9 146.2 %all-reduce.23.cloned.1.call-start = ((), (), s32[]{:S(2)}) async-start(), calls=%async_computation.20 | async-start | bytes 2097152 | tf_op jit(solution)/shard_map/psum | solution.py:47
  708.1 45.8 %copy-start.105 = (f32[1,1024]{1,0:T(1,128)S(1)}, f32[1,1024]{1,0:T(1,128)}, u32[]{:S(2)}) copy-start(f32[1,1024]{1,0:T(1,128)} %copy-done.103) | copy-start | bytes 12292
  753.9 54.3 %copy-start.145 = (f32[512]{0:T(512)}, f32[512]{0:T(512)S(1)}, u32[]{:S(2)}) copy-start(f32[512]{0:T(512)S(1)} %add_rsqrt_fusion) | copy-start | bytes 6148
  766.7 185.6 %reduce-scatter.14.cloned.1.call-start = ((), (), s32[]{:S(2)}) async-start(), calls=%async_computation.21 | async-start | bytes 2621440 | tf_op jit(solution)/shard_map/reduce_scatter | solution.py:334
  808.2 50.7 %copy-start.50 = (f32[1,512,256]{1,2,0:T(8,128)}, f32[1,512,256]{1,2,0:T(8,128)S(1)}, u32[]{:S(2)}) copy-start(f32[1,512,256]{1,2,0:T(8,128)S(1)} %get-tuple-element.937) | copy-start | bytes 1572868
  908.3 45.4 %copy-start.16 = (f32[512,4,64]{0,2,1:T(8,128)S(1)}, f32[512,4,64]{0,2,1:T(8,128)}, u32[]{:S(2)}) copy-start(f32[512,4,64]{0,2,1:T(8,128)} %get-tuple-element.338) | copy-start | bytes 1572868
  908.3 45.4 %copy-start.134 = (f32[512,32]{0,1:T(8,128)S(1)}, f32[512,32]{0,1:T(8,128)}, u32[]{:S(2)}) copy-start(f32[512,32]{0,1:T(8,128)} %get-tuple-element.1030) | copy-start | bytes 196612
  908.3 101.1 %all-reduce.25.cloned.1.call-start = ((), (), s32[]{:S(2)}) async-start(), calls=%async_computation.22 | async-start | bytes 2097152 | tf_op jit(solution)/shard_map/psum | solution.py:47
  957.4 99.5 %all-gather.27.cloned.1.call-start = ((), (), s32[]{:S(2)}) async-start(), calls=%async_computation.33 | async-start | bytes 2621440 | tf_op jit(solution)/shard_map/all_gather | solution.py:51
  958.9 153.1 %all-reduce.27.cloned.1.call-start = ((), (), s32[]{:S(2)}) async-start(), calls=%async_computation.23 | async-start | bytes 2097152 | tf_op jit(solution)/shard_map/psum | solution.py:47
  959.1 50.3 %copy-start.115 = (f32[1,1024]{1,0:T(1,128)S(1)}, f32[1,1024]{1,0:T(1,128)}, u32[]{:S(2)}) copy-start(f32[1,1024]{1,0:T(1,128)} %copy-done.112) | copy-start | bytes 12292
  959.1 50.3 %copy-start.163 = (f32[1,512,1]{1,2,0:T(1,128)S(1)}, f32[1,512,1]{1,2,0:T(1,128)}, u32[]{:S(2)}) copy-start(f32[1,512,1]{1,2,0:T(1,128)} %get-tuple-element.1002) | copy-start | bytes 6148
  965.4 47.4 %copy-start.6 = (f32[512,1024]{0,1:T(8,128)S(1)}, f32[512,1024]{0,1:T(8,128)}, u32[]{:S(2)}) copy-start(f32[512,1024]{0,1:T(8,128)} %copy-done.5) | copy-start | bytes 6291460
  1017.4 5.3 collective-permute-start.2
  1024.0 91.4 %copy-start.21 = (bf16[512,1024]{0,1:T(8,128)(2,1)}, bf16[512,1024]{0,1:T(8,128)(2,1)S(1)}, u32[]{:S(2)}) copy-start(bf16[512,1024]{0,1:T(8,128)(2,1)S(1)} %slice_select_fusion.1) | copy-start | bytes 3145732
  1031.2 179.3 %reduce-scatter.16.cloned.1.call-start = ((), (), s32[]{:S(2)}) async-start(), calls=%async_computation.24 | async-start | bytes 2621440 | tf_op jit(solution)/shard_map/reduce_scatter | solution.py:334
  1061.4 50.6 %copy-start.162 = (f32[1,512,1]{1,2,0:T(1,128)S(1)}, f32[1,512,1]{1,2,0:T(1,128)}, u32[]{:S(2)}) copy-start(f32[1,512,1]{1,2,0:T(1,128)} %get-tuple-element.1043) | copy-start | bytes 6148
  1166.5 101.6 %all-reduce.29.cloned.1.call-start = ((), (), s32[]{:S(2)}) async-start(), calls=%async_computation.25 | async-start | bytes 2097152 | tf_op jit(solution)/shard_map/psum | solution.py:47
  1216.1 99.4 %all-gather.29.cloned.1.call-start = ((), (), s32[]{:S(2)}) async-start(), calls=%async_computation.34 | async-start | bytes 2621440 | tf_op jit(solution)/shard_map/all_gather | solution.py:51
  1216.7 54.9 %copy-start.9 = (f32[512,1024]{0,1:T(8,128)S(1)}, f32[512,1024]{0,1:T(8,128)}, u32[]{:S(2)}) copy-start(f32[512,1024]{0,1:T(8,128)} %copy-done.8) | copy-start | bytes 6291460
  1216.7 153.8 %all-reduce.31.cloned.1.call-start = ((), (), s32[]{:S(2)}) async-start(), calls=%async_computation.26 | async-start | bytes 2097152 | tf_op jit(solution)/shard_map/psum | solution.py:47
  1276.2 5.3 collective-permute-start.3
  1282.8 90.5 %copy-start.33 = (bf16[512,1024]{0,1:T(8,128)(2,1)}, bf16[512,1024]{0,1:T(8,128)(2,1)S(1)}, u32[]{:S(2)}) copy-start(bf16[512,1024]{0,1:T(8,128)(2,1)S(1)} %slice_select_fusion) | copy-start | bytes 3145732
  1288.9 176.1 %reduce-scatter.18.cloned.1.call-start = ((), (), s32[]{:S(2)}) async-start(), calls=%async_computation.27 | async-start | bytes 2621440 | tf_op jit(solution)/shard_map/reduce_scatter | solution.py:334
  1421.0 118.8 %all-reduce.33.cloned.1.call-start = ((), (), s32[]{:S(2)}) async-start(), calls=%async_computation.37 | async-start | bytes 4194304 | tf_op jit(solution)/shard_map/psum | solution.py:47
  1470.4 98.1 %reduce-scatter.30.cloned.1.call-start = ((), (), s32[]{:S(2)}) async-start(), calls=%async_computation.36 | async-start | bytes 327680
  1481.5 102.4 %reduce-scatter.22.cloned.1.call-start = ((), (), s32[]{:S(2)}) async-start(), calls=%async_computation.29 | async-start | bytes 655360 | tf_op jit(solution)/shard_map/reduce_scatter | solution.py:390
  1484.1 134.2 %reduce-scatter.26.cloned.1.call-start = ((), (), s32[]{:S(2)}) async-start(), calls=%async_computation.31 | async-start | bytes 1802240 | tf_op jit(solution)/shard_map/reduce_scatter | solution.py:396
  1487.7 52.1 %copy-start.141 = (f32[1,512,1]{1,2,0:T(1,128)S(1)}, f32[1,512,1]{1,2,0:T(1,128)}, u32[]{:S(2)}) copy-start(f32[1,512,1]{1,2,0:T(1,128)} %get-tuple-element.1000) | copy-start | bytes 6148
  1487.7 52.1 %copy-start.144 = (f32[512]{0:T(512)S(1)}, f32[512]{0:T(512)}, u32[]{:S(2)}) copy-start(f32[512]{0:T(512)} %copy-done.142) | copy-start | bytes 6148
  1487.7 52.1 %copy-start.146 = (f32[512]{0:T(512)S(1)}, f32[512]{0:T(512)}, u32[]{:S(2)}) copy-start(f32[512]{0:T(512)} %copy-done.145) | copy-start | bytes 6148
  1489.8 50.0 %copy-start.20 = (bf16[512,1024]{0,1:T(8,128)(2,1)S(1)}, bf16[512,1024]{0,1:T(8,128)(2,1)}, u32[]{:S(2)}) copy-start(bf16[512,1024]{0,1:T(8,128)(2,1)} %copy-done.19) | copy-start | bytes 3145732
  1489.8 149.3 %reduce-scatter.28.cloned.1.call-start = ((), (), s32[]{:S(2)}) async-start(), calls=%async_computation.35 | async-start | bytes 327680
  1552.9 122.1 %reduce-scatter.20.cloned.1.call-start = ((), (), s32[]{:S(2)}) async-start(), calls=%async_computation.28 | async-start | bytes 1966080 | tf_op jit(solution)/shard_map/reduce_scatter | solution.py:387
  1558.4 174.1 %reduce-scatter.24.cloned.1.call-start = ((), (), s32[]{:S(2)}) async-start(), calls=%async_computation.30 | async-start | bytes 3604480 | tf_op jit(solution)/shard_map/reduce_scatter | solution.py:393
  1568.5 51.7 %copy-start.57 = (bf16[512,1024]{0,1:T(8,128)(2,1)S(1)}, bf16[512,1024]{0,1:T(8,128)(2,1)}, u32[]{:S(2)}) copy-start(bf16[512,1024]{0,1:T(8,128)(2,1)} %get-tuple-element.873) | copy-start | bytes 3145732
  (184 other events, 768.2 us)
Sparse Core Ops, SparseCore 0:
  10.1 40.3 all-gather.12
  55.0 47.8 all-gather.14
  154.8 52.0 all-reduce.12
  208.3 59.1 all-gather.16
  268.9 33.7 all-gather.18
  307.1 50.7 all-reduce.14
  376.6 45.9 all-gather.20
  474.4 51.2 all-reduce.16
  535.0 52.5 all-reduce.18
  601.6 45.9 all-gather.22
  699.5 51.2 all-reduce.20
  752.2 45.9 all-gather.24
  801.8 51.2 all-reduce.22
  908.4 43.8 reduce-scatter.13
  957.5 51.8 all-reduce.24
  1010.9 45.9 all-gather.26
  1060.7 51.2 all-reduce.26
  1166.6 43.8 reduce-scatter.15
  1216.2 51.8 all-reduce.28
  1269.6 45.8 all-gather.28
  1319.1 51.3 all-reduce.30
  1421.1 43.8 reduce-scatter.17
  1470.6 69.1 all-reduce.32
  1541.9 19.6 reduce-scatter.29
  1563.9 19.9 reduce-scatter.21
  1586.8 31.5 reduce-scatter.25
  1620.5 18.5 reduce-scatter.27
  1641.4 33.5 reduce-scatter.19
  1677.3 55.1 reduce-scatter.23
where the time goes:
time: 1750 us; the launch traced here: 1740 us
  waiting for transfers between devices  1110 us (63%)
  matrix products  201 us (11%)
  other arithmetic  190 us (11%)
  local copies, waits for them, and re-layouts  172 us (10%)
  blocking collectives  39.2 us (2%)
    psum x11, waiting for transfers between devices, head_sum(): lax.psum(partial_sum.astype(jnp.bfloat16), 'head').astype(jnp.float32)  516 us
    all_gather x6, waiting for transfers between devices, gather_keys(): lax.all_gather(key_value, 'seq', axis=0, tiled=True)  206 us
    reduce_scatter x3, waiting for transfers between devices, on_device(): lax.psum_scatter(key_grads.astype(jnp.bfloat16), 'seq', scatter_dimension...  128 us
    all_gather x1, waiting for transfers between devices, on_device(): lax.all_gather(gate_up_weight, 'seq', axis=1, tiled=True)  58.8 us
    reduce_scatter x1, waiting for transfers between devices, on_device(): lax.psum_scatter(totals[2][None].astype(jnp.bfloat16), 'seq', scatter_dim...  55.6 us
    unnamed x405, local copies, waits for them, and re-layouts  50.5 us
    reduce_sum x12, other arithmetic, fold_advance(): total = total * shrink + jnp.sum(weights, axis=-1)  40.7 us
    another operation x23, other arithmetic, on_device(): jnp.stack([entry[index] for entry in kept_list])  40.3 us
  transfers between devices with their start and end apart: 33, of which 32 were waited for; matrix products, arithmetic and copies ran while one was open for 10% of the time, Pallas kernels for 0%

commit v1 on v0

v1 whole, which is shorter than its diff:
```python
import jax
import jax.numpy as jnp
from jax import lax
from jax.experimental import pallas as pl
from jax.experimental.pallas import tpu as pltpu
from jax.sharding import PartitionSpec as P

HEAD_DIM = 64
HALF = HEAD_DIM // 2
EPS = 1e-06
MASKED = -1e30
SCALE = HEAD_DIM ** (-0.5)
BF16 = jnp.bfloat16
F32 = jnp.float32


def dot(a, b, dims):
    return lax.dot_general(a, b, (dims, ((), ())), preferred_element_type=F32)


def head_peer(x, k):
    n = lax.axis_size("head")
    return lax.ppermute(x, "head", [(i, i ^ k) for i in range(n)])


def seq_shift(x, k):
    n = lax.axis_size("seq")
    return lax.ppermute(x, "seq", [(i, (i + k) % n) for i in range(n)])


def core_swap(x):
    return lax.ppermute(x, "section", [(0, 1), (1, 0)])


def reduce_tokens(partial_sum):
    n = lax.axis_size("head")
    part = partial_sum.shape[0] // n
    low = partial_sum.astype(BF16)
    total = partial_sum[:part]
    for k in range(1, n):
        total = total + head_peer(low[k * part : (k + 1) * part], k).astype(F32)
    return total


def gather_tokens(own):
    n = lax.axis_size("head")
    return jnp.concatenate([own] + [head_peer(own, k) for k in range(1, n)], axis=0)


def peer_order(x):
    n = lax.axis_size("head")
    me = lax.axis_index("head")
    part = x.shape[0] // n
    return jnp.concatenate(
        [lax.dynamic_slice_in_dim(x, (me ^ k) * part, part, 0) for k in range(n)], axis=0
    )


def seq_slots(x):
    n = lax.axis_size("seq")
    return jnp.stack([x] + [seq_shift(x, k) for k in range(1, n)], axis=0)


def to_heads(x):
    n = lax.axis_size("seq")
    me = lax.axis_index("seq")

    def block(k):
        return lax.dynamic_index_in_dim(x, (me + k) % n, 0, keepdims=False)

    return jnp.stack([block(0)] + [seq_shift(block(k), k) for k in range(1, n)], axis=0)


def to_tokens(x):
    n = lax.axis_size("seq")
    me = lax.axis_index("seq")
    parts = jnp.stack([x[0]] + [seq_shift(x[k], -k) for k in range(1, n)], axis=0)
    return jnp.stack(
        [lax.dynamic_index_in_dim(parts, (h - me) % n, 0, keepdims=False) for h in range(n)],
        axis=0,
    )


def visible(block, xor, lo_token, queries, size):
    rows = lax.broadcasted_iota(jnp.int32, (size, 1), 0)
    keys = block * size + (rows ^ xor)
    return (keys <= queries) & (keys >= lo_token)


def attend_kernel(lo, qslot, kslot, base, q_ref, k_ref, v_ref, pos_ref, o_ref, ob_ref, lse_ref, kt_ref):
    i = pl.program_id(1)
    size = q_ref.shape[-1]
    blocks = k_ref.shape[1]

    @pl.when(i == 0)
    def _():
        for j in range(blocks):
            kt_ref[j] = jnp.transpose(k_ref[0, j, 0])

    xor = base[1]
    here = base[0] + i
    query = (q_ref[0, 0, 0].astype(F32) * SCALE).astype(BF16)
    lanes = lax.broadcasted_iota(jnp.int32, (1, size), 1)
    index = here * size + (lanes ^ xor)
    first = index - pos_ref[0]

    def step(j, carry):
        peak, total, acc = carry
        slot = kslot[j]
        s = dot(kt_ref[slot], query, ((1,), (0,)))
        s = jnp.where(visible(j, xor, first, index, size), s, MASKED)
        fresh = jnp.maximum(peak, jnp.max(s, axis=0, keepdims=True))
        p = jnp.exp(s - fresh)
        shrink = jnp.exp(peak - fresh)
        total = total * shrink + jnp.sum(p, axis=0, keepdims=True)
        acc = acc * shrink + dot(v_ref[0, slot, 0], p.astype(BF16), ((1,), (0,)))
        return fresh, total, acc

    peak, total, acc = lax.fori_loop(
        lo[i],
        here + 1,
        step,
        (
            jnp.full((1, size), MASKED, F32),
            jnp.zeros((1, size), F32),
            jnp.zeros((HEAD_DIM, size), F32),
        ),
    )
    out = acc / total
    o_ref[0, 0] = out
    ob_ref[0, 0] = out.astype(BF16)
    lse_ref[0, 0] = peak + jnp.log(total)


def grad_kernel(
    lo, qslot, kslot, base,
    q_ref, k_ref, v_ref, pos_ref, o_ref, dob_ref, lse_ref,
    dq_ref, dk_ref, dv_ref, kt_ref, vt_ref,
):
    i = pl.program_id(1)
    size = q_ref.shape[-1]
    blocks = k_ref.shape[1]

    @pl.when(i == 0)
    def _():
        for j in range(blocks):
            kt_ref[j] = jnp.transpose(k_ref[0, j, 0])
            vt_ref[j] = jnp.transpose(v_ref[0, j, 0])
        dk_ref[...] = jnp.zeros_like(dk_ref)
        dv_ref[...] = jnp.zeros_like(dv_ref)

    xor = base[1]
    here = base[0] + i
    query = (q_ref[0, 0, 0].astype(F32) * SCALE).astype(BF16)
    dob = dob_ref[0, 0]
    lse = lse_ref[0, 0]
    delta = jnp.sum(dob.astype(F32) * o_ref[0, 0], axis=0, keepdims=True)
    lanes = lax.broadcasted_iota(jnp.int32, (1, size), 1)
    index = here * size + (lanes ^ xor)
    first = index - pos_ref[0]

    def step(j, dq):
        slot = kslot[j]
        s = dot(kt_ref[slot], query, ((1,), (0,)))
        p = jnp.where(visible(j, xor, first, index, size), jnp.exp(s - lse), 0.0)
        dp = dot(vt_ref[slot], dob, ((1,), (0,)))
        ds = (p * (dp - delta)).astype(BF16)
        dv_ref[0, slot] += dot(dob, p.astype(BF16), ((1,), (1,)))
        dk_ref[0, slot] += dot(query, ds, ((1,), (1,)))
        return dq + dot(k_ref[0, slot, 0], ds, ((1,), (0,)))

    dq = lax.fori_loop(lo[i], here + 1, step, jnp.zeros((HEAD_DIM, size), F32))
    dq_ref[0, 0] = dq * SCALE


def attention_specs(heads, queries, keys, size):
    def q_at(h, i, lo, qslot, kslot, base):
        return (h, qslot[i], 0, 0, 0)

    def k_at(h, i, *_):
        return (h, 0, 1, 0, 0)

    def v_at(h, i, *_):
        return (h, 0, 2, 0, 0)

    def row_at(h, i, lo, qslot, kslot, base):
        return (qslot[i], 0, 0)

    def own_at(h, i, lo, qslot, kslot, base):
        return (h, qslot[i], 0, 0)

    q_spec = pl.BlockSpec((1, 1, 1, HEAD_DIM, size), q_at)
    k_spec = pl.BlockSpec((1, keys, 1, HEAD_DIM, size), k_at)
    v_spec = pl.BlockSpec((1, keys, 1, HEAD_DIM, size), v_at)
    pos_spec = pl.BlockSpec((1, 1, size), row_at)
    wide = pl.BlockSpec((1, 1, HEAD_DIM, size), own_at)
    thin = pl.BlockSpec((1, 1, 1, size), own_at)
    full = pl.BlockSpec((1, keys, HEAD_DIM, size), lambda h, i, *_: (h, 0, 0, 0))
    return q_spec, k_spec, v_spec, pos_spec, wide, thin, full


def attend(scalars, q, kv, pos):
    heads, queries, _, _, size = q.shape
    keys = kv.shape[1]
    q_spec, k_spec, v_spec, pos_spec, wide, thin, full = attention_specs(heads, queries, keys, size)
    pairs = heads * queries * keys * size * size
    return pl.pallas_call(
        attend_kernel,
        grid_spec=pltpu.PrefetchScalarGridSpec(
            num_scalar_prefetch=4,
            grid=(heads, queries),
            in_specs=[q_spec, k_spec, v_spec, pos_spec],
            out_specs=[wide, wide, thin],
            scratch_shapes=[pltpu.VMEM((keys, size, HEAD_DIM), BF16)],
        ),
        out_shape=[
            jax.ShapeDtypeStruct((heads, queries, HEAD_DIM, size), F32),
            jax.ShapeDtypeStruct((heads, queries, HEAD_DIM, size), BF16),
            jax.ShapeDtypeStruct((heads, queries, 1, size), F32),
        ],
        compiler_params=pltpu.CompilerParams(vmem_limit_bytes=40 << 20),
        cost_estimate=pl.CostEstimate(
            flops=4 * pairs * HEAD_DIM, bytes_accessed=4 * q.size, transcendentals=pairs
        ),
        name="attend",
    )(*scalars, q, kv, kv, pos)


def attend_grad(scalars, q, kv, pos, o, dob, lse):
    heads, queries, _, _, size = q.shape
    keys = kv.shape[1]
    q_spec, k_spec, v_spec, pos_spec, wide, thin, full = attention_specs(heads, queries, keys, size)
    pairs = heads * queries * keys * size * size
    return pl.pallas_call(
        grad_kernel,
        grid_spec=pltpu.PrefetchScalarGridSpec(
            num_scalar_prefetch=4,
            grid=(heads, queries),
            in_specs=[q_spec, k_spec, v_spec, pos_spec, wide, wide, thin],
            out_specs=[wide, full, full],
            scratch_shapes=[pltpu.VMEM((keys, size, HEAD_DIM), BF16)] * 2,
        ),
        out_shape=[
            jax.ShapeDtypeStruct((heads, queries, HEAD_DIM, size), F32),
            jax.ShapeDtypeStruct((heads, keys, HEAD_DIM, size), F32),
            jax.ShapeDtypeStruct((heads, keys, HEAD_DIM, size), F32),
        ],
        compiler_params=pltpu.CompilerParams(vmem_limit_bytes=48 << 20),
        cost_estimate=pl.CostEstimate(
            flops=10 * pairs * HEAD_DIM, bytes_accessed=8 * q.size, transcendentals=pairs
        ),
        name="attend_grad",
    )(*scalars, q, kv, kv, pos, o, dob, lse)


def turn(w, cosine, sine):
    first, second = w[..., :HALF, :], w[..., HALF:, :]
    return jnp.concatenate(
        [first * cosine - second * sine, second * cosine + first * sine], axis=-2
    )


def turn_back(w, cosine, sine):
    first, second = w[..., :HALF, :], w[..., HALF:, :]
    return jnp.concatenate(
        [first * cosine + second * sine, second * cosine - first * sine], axis=-2
    )


def gather_layers(shard):
    core = lax.axis_index("section")
    half = shard.shape[0] // 2
    mine = lax.dynamic_slice_in_dim(shard, core * half, half, 0)
    got = core_swap(lax.dynamic_slice_in_dim(shard, (1 - core) * half, half, 0))
    halves = (jnp.where(core == 0, mine, got), jnp.where(core == 0, got, mine))
    return [lax.all_gather(h, ("seq", "section"), axis=0, tiled=True) for h in halves]


def on_device(
    inputs, positions, cotangent, qkv_weight, out_weight, gate_up_weight, down_weight,
    attn_gain, ffn_gain,
):
    core = lax.axis_index("section")
    seq = lax.axis_index("seq")
    devices = lax.axis_size("seq")
    peers = lax.axis_size("head")
    _, rows, width = inputs.shape
    part = rows // peers
    heads = qkv_weight.shape[3] // HEAD_DIM
    local = heads * HEAD_DIM
    hidden = down_weight.shape[2]
    by_head = devices == heads

    own = width // devices
    w_qkv = gather_layers(
        qkv_weight[0].reshape(own, 3, heads, HEAD_DIM).transpose(0, 2, 1, 3).reshape(own, 3 * local)
    )
    w_out = gather_layers(out_weight[0])
    w_gate_up = gather_layers(gate_up_weight[0].reshape(own, 2 * hidden))
    w_down = gather_layers(down_weight[0])
    gain = jnp.stack([attn_gain[0], ffn_gain[0]])
    gain_other = core_swap(gain)
    gain = jnp.where(core == 0, jnp.stack([gain, gain_other]), jnp.stack([gain_other, gain]))
    gain = seq_slots(gain)
    gain = jnp.stack(
        [
            lax.dynamic_index_in_dim(gain, (seq - j) % devices, 0, keepdims=False)
            for j in range(devices)
        ],
        axis=2,
    ).reshape(2, 2, width)
    gain = gain.astype(F32)

    x0 = peer_order(lax.dynamic_index_in_dim(inputs, core, 0, keepdims=False))
    gy1 = peer_order(lax.dynamic_index_in_dim(cotangent, core, 0, keepdims=False))
    pos = peer_order(lax.dynamic_index_in_dim(positions, core, 0, keepdims=False))
    pos = seq_slots(pos)
    xor = lax.axis_index("head") * part
    slots = (seq - jnp.arange(devices, dtype=jnp.int32)) % devices
    token = slots[:, None] * rows + (jnp.arange(rows, dtype=jnp.int32) ^ xor)[None, :]
    lowest = jnp.min(token - pos, axis=1) // rows
    rates = 10000.0 ** (-jnp.arange(HALF, dtype=F32) / HALF)
    theta = pos.astype(F32)[:, None, :] * rates[None, :, None]
    cosine, sine = jnp.cos(theta), jnp.sin(theta)
    own_cos, own_sin = cosine[0], sine[0]
    if by_head:
        scalars = (
            lowest[slots],
            slots,
            slots,
            jnp.stack([jnp.zeros((), jnp.int32), xor]),
        )
        pos_rows = pos[:, None, :]
        back_cos, back_sin = cosine, sine
    else:
        scalars = (
            lowest[:1],
            jnp.zeros((1,), jnp.int32),
            jnp.arange(devices, dtype=jnp.int32),
            jnp.stack([seq, xor]),
        )
        pos_rows = pos[:1, None, :]
        back_cos, back_sin = own_cos, own_sin

    def norm(v, g):
        inverse = lax.rsqrt(jnp.mean(v * v, axis=-1, keepdims=True) + EPS)
        return inverse, (v * inverse * g).astype(BF16)

    def forward(layer, x, first_value):
        x_full = x.astype(F32)
        _, n1 = norm(x_full, gain[layer, 0])
        p = dot(w_qkv[layer], n1, ((0,), (1,))).reshape(heads, 3, HEAD_DIM, rows)
        q = turn(p[:, 0], own_cos, own_sin).astype(BF16)
        k = turn(p[:, 1], own_cos, own_sin).astype(BF16)
        v = p[:, 2]
        if first_value is not None:
            v = 0.5 * v + 0.5 * first_value.astype(F32)
        v = v.astype(BF16)
        packed = jnp.stack([q, k, v], axis=1)
        if by_head:
            query = to_heads(packed)[None]
            key_value = query
        else:
            query = packed[:, None]
            key_value = jnp.transpose(lax.all_gather(packed, "seq"), (1, 0, 2, 3, 4))
        o, ob, lse = attend(scalars, query, key_value, pos_rows)
        ob = (to_tokens(ob[0]) if by_head else ob[:, 0]).reshape(local, rows)
        x_own = x_full[:part]
        hid = x_own + reduce_tokens(dot(ob, w_out[layer], ((0,), (1,))))
        r2, n2_own = norm(hid, gain[layer, 1])
        n2 = gather_tokens(n2_own)
        gate_up = dot(n2, w_gate_up[layer], ((1,), (0,)))
        gate, up = gate_up[:, :hidden], gate_up[:, hidden:]
        act = (jax.nn.silu(gate) * up).astype(BF16)
        y_own = hid + reduce_tokens(dot(act, w_down[layer], ((1,), (1,))))
        y = gather_tokens(y_own.astype(BF16))
        kept = (x_own, n1, query, key_value, o, lse, ob, hid, r2, n2, gate, up, act)
        return y, v, kept

    def backward(layer, gyb, gfirst, kept):
        x_own, n1, query, key_value, o, lse, ob, hid, r2, n2, gate, up, act = kept
        sigmoid = jax.nn.sigmoid(gate)
        da = dot(gyb, w_down[layer], ((1,), (0,)))
        dgate = da * up * sigmoid * (1.0 + gate * (1.0 - sigmoid))
        dup = da * (gate * sigmoid)
        dgu = jnp.concatenate([dgate, dup], axis=1).astype(BF16)
        dn2 = reduce_tokens(dot(dgu, w_gate_up[layer], ((1,), (1,))))
        g_down = dot(gyb, act, ((0,), (0,))).astype(BF16)
        g_gate_up = dot(n2, dgu, ((0,), (0,))).astype(BF16)
        c2 = hid * r2
        g_ffn_gain = jnp.sum(dn2 * c2, axis=0)
        e2 = dn2 * gain[layer, 1]
        gh = gyb[:part].astype(F32) + r2 * (e2 - c2 * jnp.mean(e2 * c2, axis=-1, keepdims=True))
        ghb = gather_tokens(gh.astype(BF16))
        g_out = dot(ghb, ob, ((0,), (1,))).astype(BF16)
        dob = dot(w_out[layer], ghb, ((0,), (1,))).astype(BF16).reshape(heads, HEAD_DIM, rows)
        dob = to_heads(dob)[None] if by_head else dob[:, None]
        dq, dk, dv = attend_grad(scalars, query, key_value, pos_rows, o, dob, lse)
        if by_head:
            dq, dk, dv = dq[0], dk[0], dv[0]
        else:
            dq = dq[:, 0]
            dkv = jnp.stack([dk, dv], axis=1).transpose(2, 0, 1, 3, 4).astype(BF16)
            dkv = lax.psum_scatter(dkv, "seq", scatter_dimension=0, tiled=False).astype(F32)
            dk, dv = dkv[:, 0], dkv[:, 1]
        dq = turn_back(dq, back_cos, back_sin).astype(BF16)
        dk = turn_back(dk, back_cos, back_sin).astype(BF16)
        if gfirst is None:
            dv = (0.5 * dv).astype(BF16)
        else:
            dv = (dv + gfirst.astype(F32)).astype(BF16)
        packed = jnp.stack([dq, dk, dv], axis=1)
        if by_head:
            packed = to_tokens(packed)
        dqkv = packed.reshape(3 * local, rows)
        dn1 = reduce_tokens(dot(dqkv, w_qkv[layer], ((0,), (1,))))
        g_qkv = dot(n1, dqkv, ((0,), (1,))).astype(BF16)
        r1 = lax.rsqrt(jnp.mean(x_own * x_own, axis=-1, keepdims=True) + EPS)
        c1 = x_own * r1
        g_attn_gain = jnp.sum(dn1 * c1, axis=0)
        e1 = dn1 * gain[layer, 0]
        gx = gh + r1 * (e1 - c1 * jnp.mean(e1 * c1, axis=-1, keepdims=True))
        gx = gather_tokens(gx.astype(BF16))
        scattered = [
            lax.psum_scatter(g, ("seq", "section"), scatter_dimension=0, tiled=True)
            for g in (g_down, g_gate_up, g_out, g_qkv)
        ]
        return gx, dv, scattered, jnp.stack([g_attn_gain, g_ffn_gain])

    y0, v0, kept0 = forward(0, x0, None)
    y1, _, kept1 = forward(1, y0, v0)
    gx1, gfirst, grads1, gains1 = backward(1, gy1, None, kept1)
    gx0, _, grads0, gains0 = backward(0, gx1, gfirst, kept0)

    def place(first_layer, second_layer):
        other_first = lax.ppermute(first_layer, "section", [(1, 0)])
        other_second = lax.ppermute(second_layer, "section", [(0, 1)])
        return (
            jnp.where(core == 0, first_layer, other_second),
            jnp.where(core == 0, other_first, second_layer),
        )

    def place_tokens(first_layer, second_layer, dtype):
        pair = place(first_layer, second_layer)
        return jnp.stack([peer_order(m).astype(dtype) for m in pair])[None]

    def place_rows(first_layer, second_layer):
        pair = place(first_layer, second_layer)
        return jnp.concatenate(pair, axis=0).astype(F32)[None]

    activations = place_tokens(y0, y1, BF16)
    input_grads = place_tokens(gx0, gx1, F32)
    down_grad, gate_up_grad, out_grad, qkv_grad = [
        place_rows(a, b) for a, b in zip(grads0, grads1)
    ]
    qkv_grad = (
        qkv_grad.reshape(1, own, heads, 3, HEAD_DIM)
        .transpose(0, 1, 3, 2, 4)
        .reshape(1, own, 3, local)
    )
    gate_up_grad = gate_up_grad.reshape(1, own, 2, hidden)
    gains = jnp.stack([gains0, gains1])
    for axis, count in (("section", 2), ("head", peers), ("seq", devices)):
        k = 1
        while k < count:
            gains = gains + lax.ppermute(gains, axis, [(i, i ^ k) for i in range(count)])
            k *= 2
    gains = lax.dynamic_index_in_dim(gains, core, 0, keepdims=False)
    gains = lax.dynamic_slice_in_dim(gains, seq * own, own, 1)
    return (
        activations,
        input_grads,
        qkv_grad,
        out_grad,
        gate_up_grad,
        down_grad,
        gains[0][None],
        gains[1][None],
    )


def solution(mesh):
    placed = (
        P(None, "seq", None),
        P(None, "seq"),
        P(None, "seq", None),
        P("section", "seq", None, "head"),
        P("section", "seq", "head"),
        P("section", "seq", None, "head"),
        P("section", "seq", "head"),
        P("section", "seq"),
        P("section", "seq"),
    )
    return jax.shard_map(
        on_device,
        mesh=mesh,
        in_specs=placed,
        out_specs=(
            P("section", None, "seq", None),
            P("section", None, "seq", None),
            P("section", "seq", None, "head"),
            P("section", "seq", "head"),
            P("section", "seq", None, "head"),
            P("section", "seq", "head"),
            P("section", "seq"),
            P("section", "seq"),
        ),
        check_vma=False,
    )
```

time: 1750 us -> 682 us (0.39)
  waiting for transfers between devices: 1110 us -> 317 us
  other arithmetic: 190 us -> 37.6 us
  local copies, waits for them, and re-layouts: 172 us -> 29.3 us
  matrix products: 201 us -> 60.1 us
  starting transfers between devices: 10.6 us -> 146 us
  Pallas kernels: 0 us -> 35.7 us
    psum x11 -> x0, waiting for transfers between devices: 516 us -> none  [head_sum(): lax.psum(partial_sum.astype(jnp.bfloat16), 'head').astype(jnp.float32)]
    all_gather x9 -> x6, waiting for transfers between devices: 315 us -> 6.05 us  [gather_layers(): lax.all_gather(h, ('seq', 'section'), axis=0, tiled=True)]
    ppermute x4 -> x100, waiting for transfers between devices: 11.3 us -> 259 us  [the longest x48 151 us: head_peer(): return lax.ppermute(x, 'head', [(i, i ^ k) for i in range(n)])]
    reduce_scatter x7 -> x6, waiting for transfers between devices: 265 us -> 51.9 us  [backward(): lax.psum_scatter(g, ('seq', 'section'), scatter_dimension=0, tiled=True)]
    dot_general x120 -> x24, matrix products: 201 us -> 60.1 us  [dot(): return lax.dot_general(a, b, (dims, ((), ())), preferred_element_type=F32)]
    ppermute x4 -> x100, starting transfers between devices: 7.45 us -> 145 us  [the longest x48 60.2 us: head_peer(): return lax.ppermute(x, 'head', [(i, i ^ k) for i in range(n)])]
    reduce_sum x22 -> x8, other arithmetic: 61.4 us -> 4.79 us  [the longest x4 2.14 us: norm(): inverse = lax.rsqrt(jnp.mean(v * v, axis=-1, keepdims=True) + EPS)]
    another operation x37 -> x23, other arithmetic: 58.1 us -> 2.21 us  [the longest x4 1.15 us: to_tokens(): jnp.stack([x[0]] + [seq_shift(x[k], -k) for k in range(1, n)], axis=0)]
  transfers between devices with their start and end apart: 33 -> 114, of which waited for: 32 -> 60; matrix products, arithmetic and copies ran while one was open for 10% -> 15% of each run, Pallas kernels for 0% -> 4%
where the time goes in v1:
time: 682 us; the launch traced here: 673 us
  waiting for transfers between devices  317 us (46%)
  starting transfers between devices  146 us (21%)
  matrix products  60.1 us (9%)
  other arithmetic  37.6 us (6%)
  Pallas kernels  35.7 us (5%)
  blocking collectives  31.3 us (5%)
  local copies, waits for them, and re-layouts  29.3 us (4%)
  between operations  16.4 us (2%)
    ppermute x48, waiting for transfers between devices, head_peer(): return lax.ppermute(x, 'head', [(i, i ^ k) for i in range(n)])  151 us
    ppermute x30, waiting for transfers between devices, seq_shift(): return lax.ppermute(x, 'seq', [(i, (i + k) % n) for i in range(n)])  87.2 us
    ppermute x48, starting transfers between devices, head_peer(): return lax.ppermute(x, 'head', [(i, i ^ k) for i in range(n)])  60.2 us
    dot_general x24, matrix products, dot(): return lax.dot_general(a, b, (dims, ((), ())), preferred_element_type=F32)  60.1 us
    reduce_scatter x6, waiting for transfers between devices, backward(): lax.psum_scatter(g, ('seq', 'section'), scatter_dimension=0, tiled=True)  51.9 us
    ppermute x30, starting transfers between devices, seq_shift(): return lax.ppermute(x, 'seq', [(i, (i + k) % n) for i in range(n)])  51.2 us
    all_gather x2, blocking collectives, gather_layers(): lax.all_gather(h, ('seq', 'section'), axis=0, tiled=True)  31.3 us
    unnamed x178, local copies, waits for them, and re-layouts  20.6 us
  transfers between devices with their start and end apart: 114, of which 60 were waited for; matrix products, arithmetic and copies ran while one was open for 15% of the time, Pallas kernels for 4%

profile of v1, /device:TPU:0, one launch (start us, length us, event | category | flops | bytes accessed | tf_op | source)
XLA Modules:
  0.0 673.5 jit_solution(2974401002124337580)
XLA Ops:
  14.4 5.0 collective-permute-start.2
  33.1 6.0 all-gather.7.cloned.1.call-done
  46.8 4.7 collective-permute-done.10
  51.5 25.1 %collective-permute-done.9 = bf16[3,64,512]{2,1,0:T(8,128)(2,1)S(1)} collective-permute-done((bf16[3,64,512]{2,1,0:T(8,128)(2,1)S(1)}, bf16[3,64,512]{2,1,0:T(8,128)(2,1)S(1)}, u32[]{:S(2)}, u32[]{:S(2)}) %collective-permute-start.9) | collective-permute-done | bytes 196640 | tf_op jit(solution)/shard_map/ppermute | solution.py:28
  76.7 7.8 %attend.2 = (f32[1,4,64,512]{3,2,1,0:T(8,128)S(1)}, bf16[1,4,64,512]{3,2,1,0:T(8,128)(2,1)S(1)}, f32[1,4,1,512]{3,2,1,0:T(1,128)S(1)}) custom-call(s32[4]{0:T(128)S(1)} %gather_fusion, s32[4]{0:T(128)S(1)} %get-tuple-element.267.qslot.kslot, s32[4]{0:T(128)S(1)} %get-tuple-element.267.qslot.kslot, s32[2]{0:T(128)S(1)} %pad_add_fusion.2.base, ...), custom_call_target="tpu_custom_call" | custom-call | flops 1073741824 | bytes 1572864 | tf_op jit(solution)/shard_map/attend/pallas_call | solution.py:207
  84.5 4.1 collective-permute-start.13
  88.6 3.0 collective-permute-start.12
  91.7 2.9 collective-permute-start.11
  94.5 16.3 %all_gather.25 = bf16[1024,256]{1,0:T(8,128)(2,1)S(1)} all-gather(bf16[128,256]{1,0:T(8,128)(2,1)S(1)} %get-tuple-element.223), channel_id=1, replica_groups=mesh['section'=2,'seq'=4,'head'=4] {'seq','section'}, dimensions={0}, use_global_device_ids=true | all-gather | bytes 589824 | tf_op jit(solution)/shard_map/all_gather | solution.py:276
  115.5 6.3 collective-permute-done.17
  121.8 5.1 collective-permute-done.16
  131.5 6.4 collective-permute-done.20
  137.9 4.3 collective-permute-done.19
  143.2 3.6 fusion.66
  155.3 6.6 collective-permute-done.25
  161.9 4.5 collective-permute-done.24
  170.5 6.6 collective-permute-done.28
  177.1 4.4 collective-permute-done.27
  191.3 4.1 collective-permute-done.31
  195.4 11.5 %collective-permute-done.30 = bf16[3,64,512]{2,1,0:T(8,128)(2,1)S(1)} collective-permute-done((bf16[3,64,512]{2,1,0:T(8,128)(2,1)S(1)}, bf16[3,64,512]{2,1,0:T(8,128)(2,1)S(1)}, u32[]{:S(2)}, u32[]{:S(2)}) %collective-permute-start.30) | collective-permute-done | bytes 196640 | tf_op jit(solution)/shard_map/ppermute | solution.py:28
  206.9 7.8 %attend.3 = (f32[1,4,64,512]{3,2,1,0:T(8,128)S(1)}, bf16[1,4,64,512]{3,2,1,0:T(8,128)(2,1)S(1)}, f32[1,4,1,512]{3,2,1,0:T(1,128)S(1)}) custom-call(s32[4]{0:T(128)S(1)} %gather_fusion, s32[4]{0:T(128)S(1)} %get-tuple-element.267.qslot.kslot, s32[4]{0:T(128)S(1)} %get-tuple-element.267.qslot.kslot, s32[2]{0:T(128)S(1)} %pad_add_fusion.2.base, ...), custom_call_target="tpu_custom_call" | custom-call | flops 1073741824 | bytes 1572864 | tf_op jit(solution)/shard_map/attend/pallas_call | solution.py:207
  217.5 2.9 collective-permute-start.32
  220.4 14.9 %all_gather.29 = bf16[1024,256]{1,0:T(8,128)(2,1)S(1)} all-gather(bf16[128,256]{1,0:T(8,128)(2,1)S(1)} %get-tuple-element.222), channel_id=1, replica_groups=mesh['section'=2,'seq'=4,'head'=4] {'seq','section'}, dimensions={0}, use_global_device_ids=true | all-gather | bytes 589824 | tf_op jit(solution)/shard_map/all_gather | solution.py:276
  241.1 6.6 collective-permute-done.37
  247.6 5.0 collective-permute-done.36
  259.4 5.8 collective-permute-done.40
  265.3 4.8 collective-permute-done.39
  270.0 5.5 fusion.65
  275.5 4.1 multiply_convert_fusion.5
  285.2 6.6 collective-permute-done.51
  291.8 4.6 collective-permute-done.50
  300.6 6.6 collective-permute-done.54
  307.2 4.6 collective-permute-done.53
  317.4 3.2 collective-permute-done.56
  320.7 10.1 %attend_grad.2 = (f32[1,4,64,512]{3,2,1,0:T(8,128)S(1)}, f32[1,4,64,512]{3,2,1,0:T(8,128)S(1)}, f32[1,4,64,512]{3,2,1,0:T(8,128)S(1)}) custom-call(s32[4]{0:T(128)S(1)} %gather_fusion, s32[4]{0:T(128)S(1)} %get-tuple-element.267.qslot.kslot, s32[4]{0:T(128)S(1)} %get-tuple-element.267.qslot.kslot, s32[2]{0:T(128)S(1)} %pad_add_fusion.2.base, ...), custom_call_target="tpu_custom_call" | custom-call | flops 2684354560 | bytes 3145728 | tf_op jit(solution)/shard_map/attend_grad/pallas_call | solution.py:234
  341.8 5.5 collective-permute-done.59
  362.6 2.9 collective-permute-start.41
  365.6 2.9 collective-permute-done.62
  370.1 3.9 collective-permute-done.43
  374.0 4.5 collective-permute-done.42
  391.2 4.6 collective-permute-done.65
  395.8 3.9 multiply_convert_fusion.3
  405.3 6.6 collective-permute-done.69
  412.0 4.6 collective-permute-done.68
  421.2 6.6 collective-permute-done.72
  427.8 4.7 collective-permute-done.71
  435.4 3.5 convolution_convert_fusion.2
  439.2 3.5 convolution_convert_fusion.5
  447.3 6.2 collective-permute-start.75
  456.0 5.2 collective-permute-done.74
  461.3 10.1 %attend_grad.3 = (f32[1,4,64,512]{3,2,1,0:T(8,128)S(1)}, f32[1,4,64,512]{3,2,1,0:T(8,128)S(1)}, f32[1,4,64,512]{3,2,1,0:T(8,128)S(1)}) custom-call(s32[4]{0:T(128)S(1)} %gather_fusion, s32[4]{0:T(128)S(1)} %get-tuple-element.267.qslot.kslot, s32[4]{0:T(128)S(1)} %get-tuple-element.267.qslot.kslot, s32[2]{0:T(128)S(1)} %pad_add_fusion.2.base, ...), custom_call_target="tpu_custom_call" | custom-call | flops 2684354560 | bytes 3145728 | tf_op jit(solution)/shard_map/attend_grad/pallas_call | solution.py:234
  477.7 7.5 %collective-permute-done.78 = bf16[3,64,512]{2,1,0:T(8,128)(2,1)S(1)} collective-permute-done((bf16[3,64,512]{2,1,0:T(8,128)(2,1)S(1)}, bf16[3,64,512]{2,1,0:T(8,128)(2,1)S(1)}, u32[]{:S(2)}, u32[]{:S(2)}) %collective-permute-start.78) | collective-permute-done | bytes 196640 | tf_op jit(solution)/shard_map/ppermute | solution.py:28
  485.2 11.0 %collective-permute-done.77 = bf16[3,64,512]{2,1,0:T(8,128)(2,1)S(1)} collective-permute-done((bf16[3,64,512]{2,1,0:T(8,128)(2,1)S(1)}, bf16[3,64,512]{2,1,0:T(8,128)(2,1)S(1)}, u32[]{:S(2)}, u32[]{:S(2)}) %collective-permute-start.77) | collective-permute-done | bytes 196640 | tf_op jit(solution)/shard_map/ppermute | solution.py:28
  500.0 4.9 convolution_convert_fusion
  509.9 6.6 collective-permute-done.46
  516.5 5.7 collective-permute-done.45
  522.3 2.8 pad_maximum_fusion.5
  525.1 2.9 collective-permute-start.47
  531.6 3.5 convolution_convert_fusion.1
  541.7 5.8 collective-permute-done.81
  557.6 10.7 %collective-permute-done.97 = f32[2,2,1024]{2,1,0:T(2,128)S(1)} collective-permute-done((f32[2,2,1024]{2,1,0:T(2,128)S(1)}, f32[2,2,1024]{2,1,0:T(2,128)S(1)}, u32[]{:S(2)}, u32[]{:S(2)}) %collective-permute-start.97) | collective-permute-done | bytes 16416 | tf_op jit(solution)/shard_map/ppermute | solution.py:466
  568.3 7.1 %collective-permute-start.98 = (f32[2,2,1024]{2,1,0:T(2,128)S(1)}, f32[2,2,1024]{2,1,0:T(2,128)S(1)}, u32[]{:S(2)}, u32[]{:S(2)}) collective-permute-start(f32[2,2,1024]{2,1,0:T(2,128)S(1)} %add.599), channel_id=1, source_target_pairs={{0,4},{4,0},{8,12},{12,8},{1,5},{5,1},{9,13},{13,9},{2,6},{6,2},{1... | collective-permute-start | bytes 49160 | tf_op jit(solution)/shard_map/ppermute | solution.py:466
  606.6 14.2 %reduce-scatter.23.cloned.1.call-done = bf16[128,1408]{1,0:T(8,128)(2,1)} async-done(((bf16[1024,1408]{1,0:T(8,128)(2,1)}), bf16[128,1408]{1,0:T(8,128)(2,1)}) %reduce-scatter.23.cloned.1.call-update) | async-done | bytes 360464 | tf_op jit(solution)/shard_map/reduce_scatter | solution.py:425
  623.6 37.6 %reduce-scatter.21.cloned.1.call-done = bf16[128,1408]{1,0:T(8,128)(2,1)} async-done(((bf16[1024,1408]{1,0:T(8,128)(2,1)}), bf16[128,1408]{1,0:T(8,128)(2,1)}) %reduce-scatter.21.cloned.1.call-update) | async-done | bytes 360464 | tf_op jit(solution)/shard_map/reduce_scatter | solution.py:425
  (539 shorter events, 225.5 us)
Async XLA Ops:
  7.2 31.9 %all-gather.7.cloned.1.call-start = ((), (), s32[]{:S(2)}) async-start(), calls=%async_computation.8 | async-start | bytes 1769472 | tf_op jit(solution)/shard_map/all_gather | solution.py:276
  11.1 131.4 %all-gather.9.cloned.1.call-start = ((), (), s32[]{:S(2)}) async-start(), calls=%async_computation.9 | async-start | bytes 3244032 | tf_op jit(solution)/shard_map/all_gather | solution.py:276
  14.2 134.8 %all-gather.11.cloned.1.call-start = ((), (), s32[]{:S(2)}) async-start(), calls=%async_computation.10 | async-start | bytes 1622016 | tf_op jit(solution)/shard_map/all_gather | solution.py:276
  20.5 26.2 %collective-permute-start.14 = (bf16[128,256]{1,0:T(8,128)(2,1)S(1)}, bf16[128,256]{1,0:T(8,128)(2,1)S(1)}, u32[]{:S(2)}, u32[]{:S(2)}) collective-permute-start(bf16[128,256]{1,0:T(8,128)(2,1)S(1)} %dynamic-slice_bitcast_fusion.29), channel_id=1, source_target_pairs={{0,16},{16,0},{1,17},{17,1},{2,18},{18,2},{3,19},{19,3},{4,20},{20... | collective-permute-start | bytes 196616 | tf_op jit(solution)/shard_map/ppermute | solution.py:32
  29.4 154.4 %all-gather.13.cloned.1.call-start = ((), (), s32[]{:S(2)}) async-start(), calls=%async_computation.11 | async-start | bytes 1769472 | tf_op jit(solution)/shard_map/all_gather | solution.py:276
  44.9 31.7 %collective-permute-start.9 = (bf16[3,64,512]{2,1,0:T(8,128)(2,1)S(1)}, bf16[3,64,512]{2,1,0:T(8,128)(2,1)S(1)}, u32[]{:S(2)}, u32[]{:S(2)}) collective-permute-start(bf16[3,64,512]{2,1,0:T(8,128)(2,1)S(1)} %get-tuple-element.168), channel_id=1, source_target_pairs={{0,8},{4,12},{8,0},{12,4},{1,9},{5,13},{9,1},{13,5},{2,10},{6,14},... | collective-permute-start | bytes 589832 | tf_op jit(solution)/shard_map/ppermute | solution.py:28
  45.9 30.8 %collective-permute-start.8 = (bf16[3,64,512]{2,1,0:T(8,128)(2,1)S(1)}, bf16[3,64,512]{2,1,0:T(8,128)(2,1)S(1)}, u32[]{:S(2)}, u32[]{:S(2)}) collective-permute-start(bf16[3,64,512]{2,1,0:T(8,128)(2,1)S(1)} %get-tuple-element.169), channel_id=1, source_target_pairs={{0,4},{4,8},{8,12},{12,0},{1,5},{5,9},{9,13},{13,1},{2,6},{6,10},{... | collective-permute-start | bytes 589832 | tf_op jit(solution)/shard_map/ppermute | solution.py:28
  46.8 212.7 %all-gather.15.cloned.1.call-start = ((), (), s32[]{:S(2)}) async-start(), calls=%async_computation.12 | async-start | bytes 3244032 | tf_op jit(solution)/shard_map/all_gather | solution.py:276
  84.5 26.3 %collective-permute-start.13 = (bf16[64,512]{1,0:T(8,128)(2,1)S(1)}, bf16[64,512]{1,0:T(8,128)(2,1)S(1)}, u32[]{:S(2)}, u32[]{:S(2)}) collective-permute-start(bf16[64,512]{1,0:T(8,128)(2,1)S(1)} %get-tuple-element.219), channel_id=1, source_target_pairs={{0,4},{4,8},{8,12},{12,0},{1,5},{5,9},{9,13},{13,1},{2,6},{6,10},{... | collective-permute-start | bytes 196616 | tf_op jit(solution)/shard_map/ppermute | solution.py:28
  88.6 22.2 %collective-permute-start.12 = (bf16[64,512]{1,0:T(8,128)(2,1)S(1)}, bf16[64,512]{1,0:T(8,128)(2,1)S(1)}, u32[]{:S(2)}, u32[]{:S(2)}) collective-permute-start(bf16[64,512]{1,0:T(8,128)(2,1)S(1)} %get-tuple-element.220), channel_id=1, source_target_pairs={{0,8},{4,12},{8,0},{12,4},{1,9},{5,13},{9,1},{13,5},{2,10},{6,14},... | collective-permute-start | bytes 196616 | tf_op jit(solution)/shard_map/ppermute | solution.py:28
  91.7 19.2 %collective-permute-start.11 = (bf16[64,512]{1,0:T(8,128)(2,1)S(1)}, bf16[64,512]{1,0:T(8,128)(2,1)S(1)}, u32[]{:S(2)}, u32[]{:S(2)}) collective-permute-start(bf16[64,512]{1,0:T(8,128)(2,1)S(1)} %get-tuple-element.221), channel_id=1, source_target_pairs={{0,12},{4,0},{8,4},{12,8},{1,13},{5,1},{9,5},{13,9},{2,14},{6,2},{... | collective-permute-start | bytes 196616 | tf_op jit(solution)/shard_map/ppermute | solution.py:28
  114.5 12.4 %collective-permute-start.16 = (bf16[128,1024]{1,0:T(8,128)(2,1)S(1)}, bf16[128,1024]{1,0:T(8,128)(2,1)S(1)}, u32[]{:S(2)}, u32[]{:S(2)}) collective-permute-start(bf16[128,1024]{1,0:T(8,128)(2,1)S(1)} %get-tuple-element.145), channel_id=1, source_target_pairs={{0,2},{1,3},{2,0},{3,1},{4,6},{5,7},{6,4},{7,5},{8,10},{9,11},{10,... | collective-permute-start | bytes 786440 | tf_op jit(solution)/shard_map/ppermute | solution.py:23
  115.1 12.2 %collective-permute-start.15 = (bf16[128,1024]{1,0:T(8,128)(2,1)S(1)}, bf16[128,1024]{1,0:T(8,128)(2,1)S(1)}, u32[]{:S(2)}, u32[]{:S(2)}) collective-permute-start(bf16[128,1024]{1,0:T(8,128)(2,1)S(1)} %get-tuple-element.143), channel_id=1, source_target_pairs={{0,1},{1,0},{2,3},{3,2},{4,5},{5,4},{6,7},{7,6},{8,9},{9,8},{10,11... | collective-permute-start | bytes 786440 | tf_op jit(solution)/shard_map/ppermute | solution.py:23
  129.3 12.9 %collective-permute-start.19 = (bf16[128,1024]{1,0:T(8,128)(2,1)S(1)}, bf16[128,1024]{1,0:T(8,128)(2,1)S(1)}, u32[]{:S(2)}, u32[]{:S(2)}) collective-permute-start(bf16[128,1024]{1,0:T(8,128)(2,1)S(1)} %multiply_convert_fusion.10), channel_id=1, source_target_pairs={{0,2},{1,3},{2,0},{3,1},{4,6},{5,7},{6,4},{7,5},{8,10},{9,11},{10,... | collective-permute-start | bytes 786440 | tf_op jit(solution)/shard_map/ppermute | solution.py:23
  131.3 144.3 %all-gather.17.cloned.1.call-start = ((), (), s32[]{:S(2)}) async-start(), calls=%async_computation.13 | async-start | bytes 1622016 | tf_op jit(solution)/shard_map/all_gather | solution.py:276
  153.2 13.2 %collective-permute-start.24 = (bf16[128,1024]{1,0:T(8,128)(2,1)S(1)}, bf16[128,1024]{1,0:T(8,128)(2,1)S(1)}, u32[]{:S(2)}, u32[]{:S(2)}) collective-permute-start(bf16[128,1024]{1,0:T(8,128)(2,1)S(1)} %get-tuple-element.142), channel_id=1, source_target_pairs={{0,2},{1,3},{2,0},{3,1},{4,6},{5,7},{6,4},{7,5},{8,10},{9,11},{10,... | collective-permute-start | bytes 786440 | tf_op jit(solution)/shard_map/ppermute | solution.py:23
  168.4 13.1 %collective-permute-start.27 = (bf16[128,1024]{1,0:T(8,128)(2,1)S(1)}, bf16[128,1024]{1,0:T(8,128)(2,1)S(1)}, u32[]{:S(2)}, u32[]{:S(2)}) collective-permute-start(bf16[128,1024]{1,0:T(8,128)(2,1)S(1)} %fusion.25), channel_id=1, source_target_pairs={{0,2},{1,3},{2,0},{3,1},{4,6},{5,7},{6,4},{7,5},{8,10},{9,11},{10,... | collective-permute-start | bytes 786440 | tf_op jit(solution)/shard_map/ppermute | solution.py:23
  188.5 18.3 %collective-permute-start.30 = (bf16[3,64,512]{2,1,0:T(8,128)(2,1)S(1)}, bf16[3,64,512]{2,1,0:T(8,128)(2,1)S(1)}, u32[]{:S(2)}, u32[]{:S(2)}) collective-permute-start(bf16[3,64,512]{2,1,0:T(8,128)(2,1)S(1)} %get-tuple-element.164), channel_id=1, source_target_pairs={{0,8},{4,12},{8,0},{12,4},{1,9},{5,13},{9,1},{13,5},{2,10},{6,14},... | collective-permute-start | bytes 589832 | tf_op jit(solution)/shard_map/ppermute | solution.py:28
  189.3 17.5 %collective-permute-start.29 = (bf16[3,64,512]{2,1,0:T(8,128)(2,1)S(1)}, bf16[3,64,512]{2,1,0:T(8,128)(2,1)S(1)}, u32[]{:S(2)}, u32[]{:S(2)}) collective-permute-start(bf16[3,64,512]{2,1,0:T(8,128)(2,1)S(1)} %get-tuple-element.165), channel_id=1, source_target_pairs={{0,4},{4,8},{8,12},{12,0},{1,5},{5,9},{9,13},{13,1},{2,6},{6,10},{... | collective-permute-start | bytes 589832 | tf_op jit(solution)/shard_map/ppermute | solution.py:28
  215.3 20.5 %collective-permute-start.34 = (bf16[64,512]{1,0:T(8,128)(2,1)}, bf16[64,512]{1,0:T(8,128)(2,1)S(1)}, u32[]{:S(2)}, u32[]{:S(2)}) collective-permute-start(bf16[64,512]{1,0:T(8,128)(2,1)} %get-tuple-element.211), channel_id=1, source_target_pairs={{0,4},{4,8},{8,12},{12,0},{1,5},{5,9},{9,13},{13,1},{2,6},{6,10},{... | collective-permute-start | bytes 196616 | tf_op jit(solution)/shard_map/ppermute | solution.py:28
  215.6 20.3 %collective-permute-start.33 = (bf16[64,512]{1,0:T(8,128)(2,1)S(1)}, bf16[64,512]{1,0:T(8,128)(2,1)}, u32[]{:S(2)}, u32[]{:S(2)}) collective-permute-start(bf16[64,512]{1,0:T(8,128)(2,1)S(1)} %get-tuple-element.212), channel_id=1, source_target_pairs={{0,8},{4,12},{8,0},{12,4},{1,9},{5,13},{9,1},{13,5},{2,10},{6,14},... | collective-permute-start | bytes 196616 | tf_op jit(solution)/shard_map/ppermute | solution.py:28
  217.5 18.4 %collective-permute-start.32 = (bf16[64,512]{1,0:T(8,128)(2,1)S(1)}, bf16[64,512]{1,0:T(8,128)(2,1)}, u32[]{:S(2)}, u32[]{:S(2)}) collective-permute-start(bf16[64,512]{1,0:T(8,128)(2,1)S(1)} %get-tuple-element.213), channel_id=1, source_target_pairs={{0,12},{4,0},{8,4},{12,8},{1,13},{5,1},{9,5},{13,9},{2,14},{6,2},{... | collective-permute-start | bytes 196616 | tf_op jit(solution)/shard_map/ppermute | solution.py:28
  235.4 341.5 %reduce-scatter.19.cloned.1.call-start = ((), (), s32[]{:S(2)}) async-start(), calls=%async_computation.17 | async-start | bytes 589824 | tf_op jit(solution)/shard_map/reduce_scatter | solution.py:425
  239.2 13.5 %collective-permute-start.36 = (bf16[128,1024]{1,0:T(8,128)(2,1)S(1)}, bf16[128,1024]{1,0:T(8,128)(2,1)S(1)}, u32[]{:S(2)}, u32[]{:S(2)}) collective-permute-start(bf16[128,1024]{1,0:T(8,128)(2,1)S(1)} %get-tuple-element.139), channel_id=1, source_target_pairs={{0,2},{1,3},{2,0},{3,1},{4,6},{5,7},{6,4},{7,5},{8,10},{9,11},{10,... | collective-permute-start | bytes 786440 | tf_op jit(solution)/shard_map/ppermute | solution.py:23
  240.3 12.3 %collective-permute-start.35 = (bf16[128,1024]{1,0:T(8,128)(2,1)S(1)}, bf16[128,1024]{1,0:T(8,128)(2,1)S(1)}, u32[]{:S(2)}, u32[]{:S(2)}) collective-permute-start(bf16[128,1024]{1,0:T(8,128)(2,1)S(1)} %get-tuple-element.137), channel_id=1, source_target_pairs={{0,1},{1,0},{2,3},{3,2},{4,5},{5,4},{6,7},{7,6},{8,9},{9,8},{10,11... | collective-permute-start | bytes 786440 | tf_op jit(solution)/shard_map/ppermute | solution.py:23
  256.4 13.6 %collective-permute-start.39 = (bf16[128,1024]{1,0:T(8,128)(2,1)}, bf16[128,1024]{1,0:T(8,128)(2,1)}, u32[]{:S(2)}, u32[]{:S(2)}) collective-permute-start(bf16[128,1024]{1,0:T(8,128)(2,1)} %multiply_convert_fusion.9), channel_id=1, source_target_pairs={{0,2},{1,3},{2,0},{3,1},{4,6},{5,7},{6,4},{7,5},{8,10},{9,11},{10,... | collective-permute-start | bytes 786440 | tf_op jit(solution)/shard_map/ppermute | solution.py:23
  257.6 12.5 %collective-permute-start.38 = (bf16[128,1024]{1,0:T(8,128)(2,1)}, bf16[128,1024]{1,0:T(8,128)(2,1)}, u32[]{:S(2)}, u32[]{:S(2)}) collective-permute-start(bf16[128,1024]{1,0:T(8,128)(2,1)} %multiply_convert_fusion.9), channel_id=1, source_target_pairs={{0,1},{1,0},{2,3},{3,2},{4,5},{5,4},{6,7},{7,6},{8,9},{9,8},{10,11... | collective-permute-start | bytes 786440 | tf_op jit(solution)/shard_map/ppermute | solution.py:23
  283.3 13.2 %collective-permute-start.50 = (bf16[128,1024]{1,0:T(8,128)(2,1)S(1)}, bf16[128,1024]{1,0:T(8,128)(2,1)S(1)}, u32[]{:S(2)}, u32[]{:S(2)}) collective-permute-start(bf16[128,1024]{1,0:T(8,128)(2,1)S(1)} %get-tuple-element.123), channel_id=1, source_target_pairs={{0,2},{1,3},{2,0},{3,1},{4,6},{5,7},{6,4},{7,5},{8,10},{9,11},{10,... | collective-permute-start | bytes 786440 | tf_op jit(solution)/shard_map/ppermute | solution.py:23
  284.4 12.0 %collective-permute-start.49 = (bf16[128,1024]{1,0:T(8,128)(2,1)S(1)}, bf16[128,1024]{1,0:T(8,128)(2,1)S(1)}, u32[]{:S(2)}, u32[]{:S(2)}) collective-permute-start(bf16[128,1024]{1,0:T(8,128)(2,1)S(1)} %get-tuple-element.121), channel_id=1, source_target_pairs={{0,1},{1,0},{2,3},{3,2},{4,5},{5,4},{6,7},{7,6},{8,9},{9,8},{10,11... | collective-permute-start | bytes 786440 | tf_op jit(solution)/shard_map/ppermute | solution.py:23
  298.7 13.1 %collective-permute-start.53 = (bf16[128,1024]{1,0:T(8,128)(2,1)S(1)}, bf16[128,1024]{1,0:T(8,128)(2,1)S(1)}, u32[]{:S(2)}, u32[]{:S(2)}) collective-permute-start(bf16[128,1024]{1,0:T(8,128)(2,1)S(1)} %fusion.106), channel_id=1, source_target_pairs={{0,2},{1,3},{2,0},{3,1},{4,6},{5,7},{6,4},{7,5},{8,10},{9,11},{10,... | collective-permute-start | bytes 786440 | tf_op jit(solution)/shard_map/ppermute | solution.py:23
  299.8 12.0 %collective-permute-start.52 = (bf16[128,1024]{1,0:T(8,128)(2,1)S(1)}, bf16[128,1024]{1,0:T(8,128)(2,1)S(1)}, u32[]{:S(2)}, u32[]{:S(2)}) collective-permute-start(bf16[128,1024]{1,0:T(8,128)(2,1)S(1)} %fusion.106), channel_id=1, source_target_pairs={{0,1},{1,0},{2,3},{3,2},{4,5},{5,4},{6,7},{7,6},{8,9},{9,8},{10,11... | collective-permute-start | bytes 786440 | tf_op jit(solution)/shard_map/ppermute | solution.py:23
  332.3 15.1 %collective-permute-start.59 = (bf16[3,64,512]{2,1,0:T(8,128)(2,1)S(1)}, bf16[3,64,512]{2,1,0:T(8,128)(2,1)S(1)}, u32[]{:S(2)}, u32[]{:S(2)}) collective-permute-start(bf16[3,64,512]{2,1,0:T(8,128)(2,1)S(1)} %get-tuple-element.161), channel_id=1, source_target_pairs={{0,8},{4,12},{8,0},{12,4},{1,9},{5,13},{9,1},{13,5},{2,10},{6,14},... | collective-permute-start | bytes 589832 | tf_op jit(solution)/shard_map/ppermute | solution.py:28
  334.4 13.0 %collective-permute-start.58 = (bf16[3,64,512]{2,1,0:T(8,128)(2,1)S(1)}, bf16[3,64,512]{2,1,0:T(8,128)(2,1)S(1)}, u32[]{:S(2)}, u32[]{:S(2)}) collective-permute-start(bf16[3,64,512]{2,1,0:T(8,128)(2,1)S(1)} %get-tuple-element.159), channel_id=1, source_target_pairs={{0,12},{4,0},{8,4},{12,8},{1,13},{5,1},{9,5},{13,9},{2,14},{6,2},{... | collective-permute-start | bytes 589832 | tf_op jit(solution)/shard_map/ppermute | solution.py:28
  353.9 14.5 %collective-permute-start.62 = (bf16[128,1024]{1,0:T(8,128)(2,1)}, bf16[128,1024]{1,0:T(8,128)(2,1)}, u32[]{:S(2)}, u32[]{:S(2)}) collective-permute-start(bf16[128,1024]{1,0:T(8,128)(2,1)} %get-tuple-element.120), channel_id=1, source_target_pairs={{0,2},{1,3},{2,0},{3,1},{4,6},{5,7},{6,4},{7,5},{8,10},{9,11},{10,... | collective-permute-start | bytes 786440 | tf_op jit(solution)/shard_map/ppermute | solution.py:23
  357.6 16.4 %collective-permute-start.43 = (bf16[128,1024]{1,0:T(8,128)(2,1)}, bf16[128,1024]{1,0:T(8,128)(2,1)}, u32[]{:S(2)}, u32[]{:S(2)}) collective-permute-start(bf16[128,1024]{1,0:T(8,128)(2,1)} %get-tuple-element.135), channel_id=1, source_target_pairs={{0,3},{1,2},{2,1},{3,0},{4,7},{5,6},{6,5},{7,4},{8,11},{9,10},{10,... | collective-permute-start | bytes 786440 | tf_op jit(solution)/shard_map/ppermute | solution.py:23
  359.1 19.4 %collective-permute-start.42 = (bf16[128,1024]{1,0:T(8,128)(2,1)}, bf16[128,1024]{1,0:T(8,128)(2,1)}, u32[]{:S(2)}, u32[]{:S(2)}) collective-permute-start(bf16[128,1024]{1,0:T(8,128)(2,1)} %get-tuple-element.136), channel_id=1, source_target_pairs={{0,2},{1,3},{2,0},{3,1},{4,6},{5,7},{6,4},{7,5},{8,10},{9,11},{10,... | collective-permute-start | bytes 786440 | tf_op jit(solution)/shard_map/ppermute | solution.py:23
  362.4 222.2 %reduce-scatter.27.cloned.1.call-start = ((), (), s32[]{:S(2)}) async-start(), calls=%async_computation.21 | async-start | bytes 1769472
  362.6 15.9 %collective-permute-start.41 = (bf16[128,1024]{1,0:T(8,128)(2,1)}, bf16[128,1024]{1,0:T(8,128)(2,1)S(1)}, u32[]{:S(2)}, u32[]{:S(2)}) collective-permute-start(bf16[128,1024]{1,0:T(8,128)(2,1)} %get-tuple-element.134), channel_id=1, source_target_pairs={{0,1},{1,0},{2,3},{3,2},{4,5},{5,4},{6,7},{7,6},{8,9},{9,8},{10,11... | collective-permute-start | bytes 786440 | tf_op jit(solution)/shard_map/ppermute | solution.py:23
  382.7 13.2 %collective-permute-start.65 = (bf16[128,1024]{1,0:T(8,128)(2,1)S(1)}, bf16[128,1024]{1,0:T(8,128)(2,1)S(1)}, u32[]{:S(2)}, u32[]{:S(2)}) collective-permute-start(bf16[128,1024]{1,0:T(8,128)(2,1)S(1)} %get-tuple-element.192), channel_id=1, source_target_pairs={{0,2},{1,3},{2,0},{3,1},{4,6},{5,7},{6,4},{7,5},{8,10},{9,11},{10,... | collective-permute-start | bytes 786440 | tf_op jit(solution)/shard_map/ppermute | solution.py:23
  383.8 12.0 %collective-permute-start.64 = (bf16[128,1024]{1,0:T(8,128)(2,1)S(1)}, bf16[128,1024]{1,0:T(8,128)(2,1)S(1)}, u32[]{:S(2)}, u32[]{:S(2)}) collective-permute-start(bf16[128,1024]{1,0:T(8,128)(2,1)S(1)} %get-tuple-element.192), channel_id=1, source_target_pairs={{0,1},{1,0},{2,3},{3,2},{4,5},{5,4},{6,7},{7,6},{8,9},{9,8},{10,11... | collective-permute-start | bytes 786440 | tf_op jit(solution)/shard_map/ppermute | solution.py:23
  389.2 199.4 %reduce-scatter.17.cloned.1.call-start = ((), (), s32[]{:S(2)}) async-start(), calls=%async_computation.16 | async-start | bytes 589824 | tf_op jit(solution)/shard_map/reduce_scatter | solution.py:425
  403.4 13.2 %collective-permute-start.68 = (bf16[128,1024]{1,0:T(8,128)(2,1)S(1)}, bf16[128,1024]{1,0:T(8,128)(2,1)S(1)}, u32[]{:S(2)}, u32[]{:S(2)}) collective-permute-start(bf16[128,1024]{1,0:T(8,128)(2,1)S(1)} %get-tuple-element.117), channel_id=1, source_target_pairs={{0,2},{1,3},{2,0},{3,1},{4,6},{5,7},{6,4},{7,5},{8,10},{9,11},{10,... | collective-permute-start | bytes 786440 | tf_op jit(solution)/shard_map/ppermute | solution.py:23
  404.6 12.0 %collective-permute-start.67 = (bf16[128,1024]{1,0:T(8,128)(2,1)S(1)}, bf16[128,1024]{1,0:T(8,128)(2,1)S(1)}, u32[]{:S(2)}, u32[]{:S(2)}) collective-permute-start(bf16[128,1024]{1,0:T(8,128)(2,1)S(1)} %get-tuple-element.115), channel_id=1, source_target_pairs={{0,1},{1,0},{2,3},{3,2},{4,5},{5,4},{6,7},{7,6},{8,9},{9,8},{10,11... | collective-permute-start | bytes 786440 | tf_op jit(solution)/shard_map/ppermute | solution.py:23
  419.3 13.3 %collective-permute-start.71 = (bf16[128,1024]{1,0:T(8,128)(2,1)S(1)}, bf16[128,1024]{1,0:T(8,128)(2,1)S(1)}, u32[]{:S(2)}, u32[]{:S(2)}) collective-permute-start(bf16[128,1024]{1,0:T(8,128)(2,1)S(1)} %fusion.107), channel_id=1, source_target_pairs={{0,2},{1,3},{2,0},{3,1},{4,6},{5,7},{6,4},{7,5},{8,10},{9,11},{10,... | collective-permute-start | bytes 786440 | tf_op jit(solution)/shard_map/ppermute | solution.py:23
  420.5 12.1 %collective-permute-start.70 = (bf16[128,1024]{1,0:T(8,128)(2,1)S(1)}, bf16[128,1024]{1,0:T(8,128)(2,1)S(1)}, u32[]{:S(2)}, u32[]{:S(2)}) collective-permute-start(bf16[128,1024]{1,0:T(8,128)(2,1)S(1)} %fusion.107), channel_id=1, source_target_pairs={{0,1},{1,0},{2,3},{3,2},{4,5},{5,4},{6,7},{7,6},{8,9},{9,8},{10,11... | collective-permute-start | bytes 786440 | tf_op jit(solution)/shard_map/ppermute | solution.py:23
  435.4 161.3 %reduce-scatter.15.cloned.1.call-start = ((), (), s32[]{:S(2)}) async-start(), calls=%async_computation.15 | async-start | bytes 1769472 | tf_op jit(solution)/shard_map/reduce_scatter | solution.py:425
  439.0 159.8 %reduce-scatter.25.cloned.1.call-start = ((), (), s32[]{:S(2)}) async-start(), calls=%async_computation.20 | async-start | bytes 1769472
  445.4 158.8 %reduce-scatter.13.cloned.1.call-start = ((), (), s32[]{:S(2)}) async-start(), calls=%async_computation.14 | async-start | bytes 1769472 | tf_op jit(solution)/shard_map/reduce_scatter | solution.py:425
  472.9 12.3 %collective-permute-start.78 = (bf16[3,64,512]{2,1,0:T(8,128)(2,1)S(1)}, bf16[3,64,512]{2,1,0:T(8,128)(2,1)S(1)}, u32[]{:S(2)}, u32[]{:S(2)}) collective-permute-start(bf16[3,64,512]{2,1,0:T(8,128)(2,1)S(1)} %get-tuple-element.152), channel_id=1, source_target_pairs={{0,4},{4,8},{8,12},{12,0},{1,5},{5,9},{9,13},{13,1},{2,6},{6,10},{... | collective-permute-start | bytes 589832 | tf_op jit(solution)/shard_map/ppermute | solution.py:28
  473.3 22.9 %collective-permute-start.77 = (bf16[3,64,512]{2,1,0:T(8,128)(2,1)S(1)}, bf16[3,64,512]{2,1,0:T(8,128)(2,1)S(1)}, u32[]{:S(2)}, u32[]{:S(2)}) collective-permute-start(bf16[3,64,512]{2,1,0:T(8,128)(2,1)S(1)} %get-tuple-element.153), channel_id=1, source_target_pairs={{0,8},{4,12},{8,0},{12,4},{1,9},{5,13},{9,1},{13,5},{2,10},{6,14},... | collective-permute-start | bytes 589832 | tf_op jit(solution)/shard_map/ppermute | solution.py:28
  475.4 20.8 %collective-permute-start.76 = (bf16[3,64,512]{2,1,0:T(8,128)(2,1)S(1)}, bf16[3,64,512]{2,1,0:T(8,128)(2,1)S(1)}, u32[]{:S(2)}, u32[]{:S(2)}) collective-permute-start(bf16[3,64,512]{2,1,0:T(8,128)(2,1)S(1)} %get-tuple-element.151), channel_id=1, source_target_pairs={{0,12},{4,0},{8,4},{12,8},{1,13},{5,1},{9,5},{13,9},{2,14},{6,2},{... | collective-permute-start | bytes 589832 | tf_op jit(solution)/shard_map/ppermute | solution.py:28
  499.9 120.9 %reduce-scatter.23.cloned.1.call-start = ((), (), s32[]{:S(2)}) async-start(), calls=%async_computation.19 | async-start | bytes 3244032 | tf_op jit(solution)/shard_map/reduce_scatter | solution.py:425
  504.9 156.3 %reduce-scatter.21.cloned.1.call-start = ((), (), s32[]{:S(2)}) async-start(), calls=%async_computation.18 | async-start | bytes 3244032 | tf_op jit(solution)/shard_map/reduce_scatter | solution.py:425
  507.3 14.9 %collective-permute-start.45 = (bf16[128,1024]{1,0:T(8,128)(2,1)}, bf16[128,1024]{1,0:T(8,128)(2,1)S(1)}, u32[]{:S(2)}, u32[]{:S(2)}) collective-permute-start(bf16[128,1024]{1,0:T(8,128)(2,1)} %get-tuple-element.193), channel_id=1, source_target_pairs={{0,2},{1,3},{2,0},{3,1},{4,6},{5,7},{6,4},{7,5},{8,10},{9,11},{10,... | collective-permute-start | bytes 786440 | tf_op jit(solution)/shard_map/ppermute | solution.py:23
  509.1 13.2 %collective-permute-start.44 = (bf16[128,1024]{1,0:T(8,128)(2,1)}, bf16[128,1024]{1,0:T(8,128)(2,1)S(1)}, u32[]{:S(2)}, u32[]{:S(2)}) collective-permute-start(bf16[128,1024]{1,0:T(8,128)(2,1)} %get-tuple-element.193), channel_id=1, source_target_pairs={{0,1},{1,0},{2,3},{3,2},{4,5},{5,4},{6,7},{7,6},{8,9},{9,8},{10,11... | collective-permute-start | bytes 786440 | tf_op jit(solution)/shard_map/ppermute | solution.py:23
  525.1 16.4 %collective-permute-start.47 = (bf16[512,1024]{1,0:T(8,128)(2,1)}, bf16[512,1024]{1,0:T(8,128)(2,1)}, u32[]{:S(2)}, u32[]{:S(2)}) collective-permute-start(bf16[512,1024]{1,0:T(8,128)(2,1)} %get-tuple-element.128), channel_id=1, source_target_pairs={{0,16},{1,17},{2,18},{3,19},{4,20},{5,21},{6,22},{7,23},{8,24},{9,... | collective-permute-start | bytes 3145736 | tf_op jit(solution)/shard_map/ppermute | solution.py:437
  529.1 50.1 %collective-permute-start.85 = (bf16[512,1024]{1,0:T(8,128)(2,1)}, bf16[512,1024]{1,0:T(8,128)(2,1)}, u32[]{:S(2)}, u32[]{:S(2)}) collective-permute-start(bf16[512,1024]{1,0:T(8,128)(2,1)} %pad_maximum_fusion.8), channel_id=1, source_target_pairs={{0,16},{1,17},{2,18},{3,19},{4,20},{5,21},{6,22},{7,23},{8,24},{9,... | collective-permute-start | bytes 3145736 | tf_op jit(solution)/shard_map/ppermute | solution.py:437
  553.3 27.2 %collective-permute-start.84 = (bf16[128,1024]{1,0:T(8,128)(2,1)S(1)}, bf16[128,1024]{1,0:T(8,128)(2,1)S(1)}, u32[]{:S(2)}, u32[]{:S(2)}) collective-permute-start(bf16[128,1024]{1,0:T(8,128)(2,1)S(1)} %add_convert_fusion), channel_id=1, source_target_pairs={{0,3},{1,2},{2,1},{3,0},{4,7},{5,6},{6,5},{7,4},{8,11},{9,10},{10,... | collective-permute-start | bytes 786440 | tf_op jit(solution)/shard_map/ppermute | solution.py:23
  554.8 25.7 %collective-permute-start.83 = (bf16[128,1024]{1,0:T(8,128)(2,1)S(1)}, bf16[128,1024]{1,0:T(8,128)(2,1)S(1)}, u32[]{:S(2)}, u32[]{:S(2)}) collective-permute-start(bf16[128,1024]{1,0:T(8,128)(2,1)S(1)} %add_convert_fusion), channel_id=1, source_target_pairs={{0,2},{1,3},{2,0},{3,1},{4,6},{5,7},{6,4},{7,5},{8,10},{9,11},{10,... | collective-permute-start | bytes 786440 | tf_op jit(solution)/shard_map/ppermute | solution.py:23
  555.5 25.0 %collective-permute-start.82 = (bf16[128,1024]{1,0:T(8,128)(2,1)S(1)}, bf16[128,1024]{1,0:T(8,128)(2,1)S(1)}, u32[]{:S(2)}, u32[]{:S(2)}) collective-permute-start(bf16[128,1024]{1,0:T(8,128)(2,1)S(1)} %add_convert_fusion), channel_id=1, source_target_pairs={{0,1},{1,0},{2,3},{3,2},{4,5},{5,4},{6,7},{7,6},{8,9},{9,8},{10,11... | collective-permute-start | bytes 786440 | tf_op jit(solution)/shard_map/ppermute | solution.py:23
  577.1 12.8 %collective-permute-start.89 = (bf16[128,256]{1,0:T(8,128)(2,1)}, bf16[128,256]{1,0:T(8,128)(2,1)}, u32[]{:S(2)}, u32[]{:S(2)}) collective-permute-start(bf16[128,256]{1,0:T(8,128)(2,1)} %reduce-scatter.19.cloned.1.call-done), channel_id=1, source_target_pairs={{0,16},{1,17},{2,18},{3,19},{4,20},{5,21},{6,22},{7,23},{8,24},{9,... | collective-permute-start | bytes 196616 | tf_op jit(solution)/shard_map/ppermute | solution.py:437
  586.4 14.8 %collective-permute-start.93 = (bf16[128,704]{0,1:T(8,128)(2,1)}, bf16[128,704]{0,1:T(8,128)(2,1)}, u32[]{:S(2)}, u32[]{:S(2)}) collective-permute-start(bf16[128,704]{0,1:T(8,128)(2,1)} %copy.169), channel_id=1, source_target_pairs={{0,16},{1,17},{2,18},{3,19},{4,20},{5,21},{6,22},{7,23},{8,24},{9,... | collective-permute-start | bytes 540680 | tf_op jit(solution)/shard_map/ppermute | solution.py:437
  604.2 18.0 %collective-permute-start.88 = (bf16[128,768]{1,0:T(8,128)(2,1)}, bf16[128,768]{1,0:T(8,128)(2,1)S(1)}, u32[]{:S(2)}, u32[]{:S(2)}) collective-permute-start(bf16[128,768]{1,0:T(8,128)(2,1)} %reduce-scatter.13.cloned.1.call-done), channel_id=1, source_target_pairs={{16,0},{17,1},{18,2},{19,3},{20,4},{21,5},{22,6},{23,7},{24,8},{25... | collective-permute-start | bytes 589832 | tf_op jit(solution)/shard_map/ppermute | solution.py:436
  620.8 41.7 %collective-permute-start.91 = (bf16[128,1408]{1,0:T(8,128)(2,1)}, bf16[128,1408]{1,0:T(8,128)(2,1)S(1)}, u32[]{:S(2)}, u32[]{:S(2)}) collective-permute-start(bf16[128,1408]{1,0:T(8,128)(2,1)} %reduce-scatter.23.cloned.1.call-done), channel_id=1, source_target_pairs={{0,16},{1,17},{2,18},{3,19},{4,20},{5,21},{6,22},{7,23},{8,24},{9,... | collective-permute-start | bytes 1081352 | tf_op jit(solution)/shard_map/ppermute | solution.py:437
  (133 other events, 1561.4 us)
Sparse Core Ops, SparseCore 0:
  11.2 27.8 all-gather.6
  41.3 47.6 all-gather.8
  91.1 28.6 all-gather.10
  121.9 23.8 all-gather.12
  147.8 35.6 all-gather.14
  235.5 23.9 all-gather.16
  362.5 32.9 reduce-scatter.18
  398.5 32.2 reduce-scatter.26
  435.5 34.2 reduce-scatter.16
  471.9 38.1 reduce-scatter.14
  512.4 34.4 reduce-scatter.24
  549.0 32.6 reduce-scatter.12
  584.0 36.7 reduce-scatter.22
  623.0 38.2 reduce-scatter.20

commit v2 on v1

--- a/solution.py
+++ b/solution.py
@@ -2,6 +2,7 @@
 import jax.numpy as jnp
 from jax import lax
 from jax.experimental import pallas as pl
+from jax.experimental.layout import Layout, with_layout_constraint
 from jax.experimental.pallas import tpu as pltpu
 from jax.sharding import PartitionSpec as P
 
@@ -32,19 +33,69 @@
     return lax.ppermute(x, "section", [(0, 1), (1, 0)])
 
 
-def reduce_tokens(partial_sum):
+barrier = lax.optimization_barrier
+
+
+def beside(exchange, value, work, operands):
+    value, operands = barrier((value, operands))
+    got = exchange(value)
+    done = work(*operands)
+    return barrier((got, done))
+
+
+def reduce_tokens(partial_sum, work=None, operands=()):
     n = lax.axis_size("head")
     part = partial_sum.shape[0] // n
+
+    def exchange(low):
+        return [head_peer(low[k * part : (k + 1) * part], k) for k in range(1, n)]
+
     low = partial_sum.astype(BF16)
-    total = partial_sum[:part]
-    for k in range(1, n):
-        total = total + head_peer(low[k * part : (k + 1) * part], k).astype(F32)
-    return total
-
-
-def gather_tokens(own):
+    if work is None:
+        got = exchange(low)
+    else:
+        got, done = beside(exchange, low, work, operands)
+    total = low[:part].astype(F32)
+    for g in got:
+        total = total + g.astype(F32)
+    return total if work is None else (total, done)
+
+
+def gather_tokens(own, work=None, operands=(), second=None, second_operands=()):
     n = lax.axis_size("head")
-    return jnp.concatenate([own] + [head_peer(own, k) for k in range(1, n)], axis=0)
+
+    def exchange(x):
+        return [head_peer(x, k) for k in range(1, n)]
+
+    if work is None:
+        return jnp.concatenate([own] + exchange(own), axis=0)
+    if second is None:
+        got, done = beside(exchange, own, work, operands)
+        return jnp.concatenate([own] + got, axis=0), done
+    own, operands = barrier((own, operands))
+    got = exchange(own)
+    done = work(*operands)
+    got[0], second_operands = barrier((got[0], second_operands))
+    got, done, also = barrier((got, done, second(*second_operands)))
+    return jnp.concatenate([own] + got, axis=0), done, also
+
+
+def gather_features(own, work=lambda: (), operands=()):
+    n = lax.axis_size("head")
+    part = own.shape[1] // n
+
+    def exchange(x):
+        return [head_peer(x, k) for k in range(1, n)]
+
+    received, done = beside(exchange, own, work, operands)
+    out = [own]
+    for k, got in enumerate(received, 1):
+        out.append(
+            jnp.concatenate(
+                [got[:, (j ^ k) * part : ((j ^ k) + 1) * part] for j in range(n)], axis=1
+            )
+        )
+    return jnp.concatenate(out, axis=0), done
 
 
 def peer_order(x):
@@ -56,29 +107,47 @@
     )
 
 
+def seq_blocks(x):
+    n = lax.axis_size("seq")
+    return [x] + [seq_shift(x, k) for k in range(1, n)]
+
+
 def seq_slots(x):
-    n = lax.axis_size("seq")
-    return jnp.stack([x] + [seq_shift(x, k) for k in range(1, n)], axis=0)
-
-
-def to_heads(x):
+    return jnp.stack(seq_blocks(x), axis=0)
+
+
+def to_heads(x, work, operands=(), held=()):
     n = lax.axis_size("seq")
     me = lax.axis_index("seq")
 
-    def block(k):
-        return lax.dynamic_index_in_dim(x, (me + k) % n, 0, keepdims=False)
-
-    return jnp.stack([block(0)] + [seq_shift(block(k), k) for k in range(1, n)], axis=0)
-
-
-def to_tokens(x):
+    def exchange(x):
+        def block(k):
+            return lax.dynamic_index_in_dim(x, (me + k) % n, 0, keepdims=False)
+
+        return [block(0)] + [seq_shift(block(k), k) for k in range(1, n)]
+
+    x, operands = barrier((x, operands))
+    got = exchange(x)
+    got[1], held = barrier((got[1], held))
+    got, done = barrier((got, work(*operands)))
+    return jnp.stack(got, axis=0), done, held
+
+
+def to_tokens(x, work, operands=(), second=lambda: (), second_operands=()):
     n = lax.axis_size("seq")
     me = lax.axis_index("seq")
-    parts = jnp.stack([x[0]] + [seq_shift(x[k], -k) for k in range(1, n)], axis=0)
-    return jnp.stack(
-        [lax.dynamic_index_in_dim(parts, (h - me) % n, 0, keepdims=False) for h in range(n)],
-        axis=0,
-    )
+
+    def exchange(x):
+        return [x[0]] + [seq_shift(x[k], -k) for k in range(1, n)]
+
+    x, operands = barrier((x, operands))
+    got = exchange(x)
+    done = work(*operands)
+    got[1], second_operands = barrier((got[1], second_operands))
+    got, done, also = barrier((got, done, second(*second_operands)))
+    parts = jnp.stack(got, axis=0)
+    out = [lax.dynamic_index_in_dim(parts, (h - me) % n, 0, keepdims=False) for h in range(n)]
+    return jnp.stack(out, axis=0), done, also
 
 
 def visible(block, xor, lo_token, queries, size):
@@ -267,13 +336,82 @@
     )
 
 
-def gather_layers(shard):
+def half_rows(x, which):
+    half = x.shape[0] // 2
+    return lax.dynamic_slice_in_dim(x, which * half, half, 0)
+
+
+def split_layers(shard):
     core = lax.axis_index("section")
-    half = shard.shape[0] // 2
-    mine = lax.dynamic_slice_in_dim(shard, core * half, half, 0)
-    got = core_swap(lax.dynamic_slice_in_dim(shard, (1 - core) * half, half, 0))
-    halves = (jnp.where(core == 0, mine, got), jnp.where(core == 0, got, mine))
-    return [lax.all_gather(h, ("seq", "section"), axis=0, tiled=True) for h in halves]
+    mine = half_rows(shard, core)
+    got = core_swap(half_rows(shard, 1 - core))
+    return jnp.where(core == 0, mine, got), jnp.where(core == 0, got, mine)
+
+
+def gather_rows(half):
+    return lax.all_gather(by_rows(half), ("seq", "section"), axis=0, tiled=True)
+
+
+def join_halves(mine, in_slots):
+    core = lax.axis_index("section")
+    seq = lax.axis_index("seq")
+    n = mine.shape[0]
+    both = jnp.stack([mine, core_swap(mine)], axis=1).reshape(2 * n, *mine.shape[1:])
+    return jnp.concatenate(
+        [
+            lax.dynamic_index_in_dim(
+                both, ((seq - j) % n if in_slots else j) * 2 + (core ^ h), 0, keepdims=False
+            )
+            for j in range(n)
+            for h in range(2)
+        ],
+        axis=0,
+    )
+
+
+def gather_peers(mine):
+    n = lax.axis_size("head")
+    return jnp.concatenate([mine] + [head_peer(mine, k) for k in range(1, n)], axis=-1)
+
+
+def by_rows(x):
+    return with_layout_constraint(x, Layout(tuple(range(x.ndim))))
+
+
+def columns(x, *widths):
+    out = []
+    at = 0
+    for w in widths:
+        out.append(x[:, at : at + w])
+        at += w
+    return out
+
+
+def scatter_rows(grad):
+    return lax.psum_scatter(by_rows(grad), ("seq", "section"), scatter_dimension=0, tiled=True)
+
+
+def add_cores(grad):
+    core = lax.axis_index("section")
+    n = lax.axis_size("seq")
+    grad = grad.reshape(n, 2, grad.shape[0] // (2 * n), grad.shape[1])
+    mine = lax.dynamic_index_in_dim(grad, core, 1, keepdims=False)
+    other = core_swap(lax.dynamic_index_in_dim(grad, 1 - core, 1, keepdims=False))
+    return (mine.astype(F32) + other.astype(F32)).astype(BF16)
+
+
+def scatter_devices(total):
+    seq = lax.axis_index("seq")
+    n = lax.axis_size("seq")
+
+    def block(k):
+        return lax.dynamic_index_in_dim(total, (seq + k) % n, 0, keepdims=False)
+
+    return [block(0)] + [seq_shift(block(k), k) for k in range(1, n)]
+
+
+def add_up(parts):
+    return sum((p.astype(F32) for p in parts[1:]), parts[0].astype(F32)).astype(BF16)
 
 
 def on_device(
@@ -292,16 +430,29 @@
     by_head = devices == heads
 
     own = width // devices
-    w_qkv = gather_layers(
+    qkv_shard = (
         qkv_weight[0].reshape(own, 3, heads, HEAD_DIM).transpose(0, 2, 1, 3).reshape(own, 3 * local)
     )
-    w_out = gather_layers(out_weight[0])
-    w_gate_up = gather_layers(gate_up_weight[0].reshape(own, 2 * hidden))
-    w_down = gather_layers(down_weight[0])
-    gain = jnp.stack([attn_gain[0], ffn_gain[0]])
+    attn_shard = jnp.concatenate([qkv_shard, out_weight[0]], axis=1)
+    attn_half, attn_later = split_layers(attn_shard)
+    pos = lax.dynamic_index_in_dim(positions, core, 0, keepdims=False)
+    gain = jnp.stack([attn_gain[0], ffn_gain[0]]).astype(F32)
     gain_other = core_swap(gain)
-    gain = jnp.where(core == 0, jnp.stack([gain, gain_other]), jnp.stack([gain_other, gain]))
-    gain = seq_slots(gain)
+    small = jnp.where(core == 0, jnp.stack([gain, gain_other]), jnp.stack([gain_other, gain]))
+    small = jnp.concatenate([peer_order(pos).astype(F32), small.reshape(4 * own)])
+    small = seq_slots(small)
+    attn_half, inputs, cotangent, gate_up_weight, down_weight = barrier(
+        (attn_half, inputs, cotangent, gate_up_weight, down_weight)
+    )
+    first = seq_blocks(attn_half)
+    ffn_shard = jnp.concatenate(
+        [gate_up_weight[0].reshape(own, 2 * hidden), down_weight[0]], axis=1
+    )
+    ffn_half, ffn_later = split_layers(by_rows(ffn_shard))
+    first = jnp.stack(first, axis=0)
+    w_qkv_first = join_halves(first[:, :, : 3 * local], True)
+    out_first = first[:, :, 3 * local :]
+    gain = small[:, rows:].reshape(devices, 2, 2, own)
     gain = jnp.stack(
         [
             lax.dynamic_index_in_dim(gain, (seq - j) % devices, 0, keepdims=False)
@@ -309,12 +460,10 @@
         ],
         axis=2,
     ).reshape(2, 2, width)
-    gain = gain.astype(F32)
 
     x0 = peer_order(lax.dynamic_index_in_dim(inputs, core, 0, keepdims=False))
     gy1 = peer_order(lax.dynamic_index_in_dim(cotangent, core, 0, keepdims=False))
-    pos = peer_order(lax.dynamic_index_in_dim(positions, core, 0, keepdims=False))
-    pos = seq_slots(pos)
+    pos = small[:, :rows].astype(jnp.int32)
     xor = lax.axis_index("head") * part
     slots = (seq - jnp.arange(devices, dtype=jnp.int32)) % devices
     token = slots[:, None] * rows + (jnp.arange(rows, dtype=jnp.int32) ^ xor)[None, :]
@@ -346,56 +495,125 @@
         inverse = lax.rsqrt(jnp.mean(v * v, axis=-1, keepdims=True) + EPS)
         return inverse, (v * inverse * g).astype(BF16)
 
-    def forward(layer, x, first_value):
+    def project(layer, x, w_qkv, first_value):
         x_full = x.astype(F32)
         _, n1 = norm(x_full, gain[layer, 0])
-        p = dot(w_qkv[layer], n1, ((0,), (1,))).reshape(heads, 3, HEAD_DIM, rows)
+        p = dot(w_qkv, n1, ((0,), (1,))).reshape(heads, 3, HEAD_DIM, rows)
         q = turn(p[:, 0], own_cos, own_sin).astype(BF16)
         k = turn(p[:, 1], own_cos, own_sin).astype(BF16)
         v = p[:, 2]
         if first_value is not None:
             v = 0.5 * v + 0.5 * first_value.astype(F32)
         v = v.astype(BF16)
-        packed = jnp.stack([q, k, v], axis=1)
+        return n1, jnp.stack([q, k, v], axis=1), v
+
+    def mix(packed, out_mine, in_slots, held):
         if by_head:
-            query = to_heads(packed)[None]
+            query, out_all, _ = to_heads(packed, gather_peers, (out_mine,))
+            query = query[None]
             key_value = query
         else:
+            out_all = gather_peers(out_mine)
             query = packed[:, None]
             key_value = jnp.transpose(lax.all_gather(packed, "seq"), (1, 0, 2, 3, 4))
+        key_value, held = barrier((key_value, held))
+        query = key_value if by_head else query
         o, ob, lse = attend(scalars, query, key_value, pos_rows)
-        ob = (to_tokens(ob[0]) if by_head else ob[:, 0]).reshape(local, rows)
-        x_own = x_full[:part]
-        hid = x_own + reduce_tokens(dot(ob, w_out[layer], ((0,), (1,))))
-        r2, n2_own = norm(hid, gain[layer, 1])
-        n2 = gather_tokens(n2_own)
-        gate_up = dot(n2, w_gate_up[layer], ((1,), (0,)))
+
+        def join(out_all):
+            return join_halves(out_all, in_slots)
+
+        if by_head:
+            ob, w_out, _ = to_tokens(ob[0], join, (out_all,))
+        else:
+            ob, w_out = ob[:, 0], join(out_all)
+        return ob.reshape(local, rows), w_out, (query, key_value, o, lse), held
+
+    def feed(layer, x, ob_all, w_out, w_gate_up, w_down):
+        hid = x.astype(F32) + dot(ob_all, w_out, ((0,), (1,)))
+        r2, n2 = norm(hid, gain[layer, 1])
+        gate_up = dot(n2, w_gate_up, ((1,), (0,)))
         gate, up = gate_up[:, :hidden], gate_up[:, hidden:]
         act = (jax.nn.silu(gate) * up).astype(BF16)
-        y_own = hid + reduce_tokens(dot(act, w_down[layer], ((1,), (1,))))
-        y = gather_tokens(y_own.astype(BF16))
-        kept = (x_own, n1, query, key_value, o, lse, ob, hid, r2, n2, gate, up, act)
-        return y, v, kept
-
-    def backward(layer, gyb, gfirst, kept):
-        x_own, n1, query, key_value, o, lse, ob, hid, r2, n2, gate, up, act = kept
+        y_part = dot(act, w_down, ((1,), (1,))).astype(BF16)
+        return y_part, (hid[:part], r2[:part], n2, gate, up, act)
+
+    def to_first(value):
+        return lax.ppermute(value, "section", [(1, 0)])
+
+    def to_second(value):
+        return lax.ppermute(value, "section", [(0, 1)])
+
+    def to_second_all(*values):
+        return [to_second(v) for v in values]
+
+    def settle(first_layer, first_other, second_layer, second_other):
+        return (
+            jnp.where(core == 0, first_layer, second_other),
+            jnp.where(core == 0, first_other, second_layer),
+        )
+
+    def place(first_layer, second_layer):
+        return settle(first_layer, to_first(first_layer), second_layer, to_second(second_layer))
+
+    def add_peers(gains):
+        return sum((head_peer(gains, k) for k in range(1, peers)), gains)
+
+    def backward(layer, gyb, gfirst, kept, late, before):
+        x_own, n1, (query, key_value, o, lse), ob, w_out, fed, w_qkv, w_gate_up, w_down = kept
+        hid, r2, n2, gate, up, act = fed
         sigmoid = jax.nn.sigmoid(gate)
-        da = dot(gyb, w_down[layer], ((1,), (0,)))
+        da = dot(gyb, w_down, ((1,), (0,)))
         dgate = da * up * sigmoid * (1.0 + gate * (1.0 - sigmoid))
         dup = da * (gate * sigmoid)
         dgu = jnp.concatenate([dgate, dup], axis=1).astype(BF16)
-        dn2 = reduce_tokens(dot(dgu, w_gate_up[layer], ((1,), (1,))))
-        g_down = dot(gyb, act, ((0,), (0,))).astype(BF16)
-        g_gate_up = dot(n2, dgu, ((0,), (0,))).astype(BF16)
+
+        def grad_rows(a, b):
+            return dot(a, b, ((0,), (0,))).astype(BF16)
+
+        def gain_rows(dn, n, g):
+            return jnp.sum(dn.astype(F32) * n.astype(F32), axis=0) / g
+
+        def beside_ffn(dn, n2, dgu):
+            g_gate_up, g_gain = grad_rows(n2, dgu), gain_rows(dn, n2, gain[layer, 1])
+            if layer:
+                return g_gate_up, g_gain
+            g_gate_up = by_rows(jnp.concatenate([g_gate_up, before[1]], axis=1))
+            return g_gate_up, g_gain, to_second(before[3])
+
+        dn2 = dot(dgu, w_gate_up, ((1,), (1,))).astype(BF16)
+        dn2, (g_gate_up, g_ffn_gain, *y_other) = reduce_tokens(dn2, beside_ffn, (dn2, n2, dgu))
         c2 = hid * r2
-        g_ffn_gain = jnp.sum(dn2 * c2, axis=0)
         e2 = dn2 * gain[layer, 1]
         gh = gyb[:part].astype(F32) + r2 * (e2 - c2 * jnp.mean(e2 * c2, axis=-1, keepdims=True))
-        ghb = gather_tokens(gh.astype(BF16))
-        g_out = dot(ghb, ob, ((0,), (1,))).astype(BF16)
-        dob = dot(w_out[layer], ghb, ((0,), (1,))).astype(BF16).reshape(heads, HEAD_DIM, rows)
-        dob = to_heads(dob)[None] if by_head else dob[:, None]
+        ghb, g_gate_up = barrier((gh.astype(BF16), g_gate_up))
+        gate_up_rows = scatter_rows(g_gate_up)
+
+        def beside_ghb(gyb, act):
+            return (grad_rows(gyb, act), *(() if layer else (to_second(gyb),)))
+
+        ghb, (g_down, *gx_other) = gather_tokens(ghb, beside_ghb, (gyb, act))
+        dob = dot(w_out[:, :local], ghb, ((0,), (1,))).astype(BF16)
+        dob = dob.reshape(heads, HEAD_DIM, rows)
+
+        def grad_rest(ghb, ob, g_down):
+            g_out = dot(ghb, ob, ((0,), (1,))).astype(BF16)
+            return jnp.concatenate([g_out, g_down], axis=1)
+
+        if by_head:
+            dob, g_rest, late = to_heads(dob, grad_rest, (ghb, ob, g_down), late)
+            dob = dob[None]
+        else:
+            g_rest = grad_rest(ghb, ob, g_down)
+            dob = dob[:, None]
+        dob, g_rest = barrier((dob, g_rest))
+        rest_rows = scatter_rows(g_rest)
+        if layer:
+            y_part, y_hid = late
+            y_own = (y_hid + reduce_tokens(y_part)).astype(BF16)
         dq, dk, dv = attend_grad(scalars, query, key_value, pos_rows, o, dob, lse)
+        if layer:
+            dq, y_own = barrier((dq, y_own))
         if by_head:
             dq, dk, dv = dq[0], dk[0], dv[0]
         else:
@@ -410,63 +628,126 @@
         else:
             dv = (dv + gfirst.astype(F32)).astype(BF16)
         packed = jnp.stack([dq, dk, dv], axis=1)
-        if by_head:
-            packed = to_tokens(packed)
+        if by_head and layer:
+            packed, _, y = to_tokens(packed, lambda: (), (), gather_tokens, (y_own,))
+        elif by_head:
+            packed, _, rows_other = to_tokens(packed, lambda: (), (), to_second_all, before[0])
+        elif layer:
+            y = gather_tokens(y_own)
+        else:
+            rows_other = to_second_all(*before[0])
         dqkv = packed.reshape(3 * local, rows)
-        dn1 = reduce_tokens(dot(dqkv, w_qkv[layer], ((0,), (1,))))
-        g_qkv = dot(n1, dqkv, ((0,), (1,))).astype(BF16)
+
+        dn1 = dot(dqkv, w_qkv, ((0,), (1,))).astype(BF16)
+        g_attn_gain = gain_rows(dn1, n1, gain[layer, 0])
+        gains = jnp.stack([g_attn_gain, g_ffn_gain])
+
+        def grad_qkv(n1, dqkv):
+            g_qkv = dot(n1, dqkv, ((0,), (1,))).astype(BF16)
+            return g_qkv if layer else scatter_devices(add_cores(g_qkv))
+
+        if layer:
+            dn1, g_qkv = reduce_tokens(dn1, grad_qkv, (n1, dqkv))
+        else:
+            gains = jnp.concatenate([gains, before[2]], axis=0)
+            high = gains.astype(BF16)
+            low = (gains - high.astype(F32)).astype(BF16)
+            tail = jnp.concatenate([high, low, jnp.zeros((8, width), BF16)], axis=0)
+            dn1 = jnp.concatenate([dn1.reshape(peers, part, width)] + [
+                jnp.broadcast_to(tail[None], (peers, 16, width))
+            ], axis=1).reshape(peers * (part + 16), width)
+            dn1, n1, dqkv = barrier((dn1, n1, dqkv))
+            qkv_parts = grad_qkv(n1, dqkv)
+            dn1 = reduce_tokens(dn1)
+            gains = dn1[part : part + 4] + dn1[part + 4 : part + 8]
+            dn1 = dn1[:part]
         r1 = lax.rsqrt(jnp.mean(x_own * x_own, axis=-1, keepdims=True) + EPS)
         c1 = x_own * r1
-        g_attn_gain = jnp.sum(dn1 * c1, axis=0)
         e1 = dn1 * gain[layer, 0]
         gx = gh + r1 * (e1 - c1 * jnp.mean(e1 * c1, axis=-1, keepdims=True))
-        gx = gather_tokens(gx.astype(BF16))
-        scattered = [
-            lax.psum_scatter(g, ("seq", "section"), scatter_dimension=0, tiled=True)
-            for g in (g_down, g_gate_up, g_out, g_qkv)
-        ]
-        return gx, dv, scattered, jnp.stack([g_attn_gain, g_ffn_gain])
-
-    y0, v0, kept0 = forward(0, x0, None)
-    y1, _, kept1 = forward(1, y0, v0)
-    gx1, gfirst, grads1, gains1 = backward(1, gy1, None, kept1)
-    gx0, _, grads0, gains0 = backward(0, gx1, gfirst, kept0)
-
-    def place(first_layer, second_layer):
-        other_first = lax.ppermute(first_layer, "section", [(1, 0)])
-        other_second = lax.ppermute(second_layer, "section", [(0, 1)])
-        return (
-            jnp.where(core == 0, first_layer, other_second),
-            jnp.where(core == 0, other_first, second_layer),
+        gx = gx.astype(BF16)
+        if layer:
+            return gather_tokens(gx), dv, (gate_up_rows, rest_rows), g_qkv, gains, y
+
+        def beside_last(gate_up_rows, gains):
+            gains = gains.reshape(2, 2, width)
+            mine = lax.dynamic_index_in_dim(gains, core, 0, keepdims=False)
+            other = lax.dynamic_index_in_dim(gains, 1 - core, 0, keepdims=False)
+            gate_up, qkv = columns(gate_up_rows, 2 * hidden, 3 * local)
+            gate_up = settle(gate_up, to_first(gate_up), before[0][0], rows_other[0])
+            return rows_of(gate_up), qkv, to_second(qkv), mine + core_swap(other)
+
+        def then(qkv_parts, gains):
+            qkv = add_up(qkv_parts)
+            return qkv, to_first(qkv), add_devices(gains)
+
+        n = peers
+        gx, gate_up_rows, gains = barrier((gx, gate_up_rows, gains))
+        got = [head_peer(gx, k) for k in range(1, n)]
+        gate_up, qkv1, qkv1_other, gains = beside_last(gate_up_rows, gains)
+        got[0], qkv_parts, gains = barrier((got[0], qkv_parts, gains))
+        qkv0, qkv0_other, gains = then(qkv_parts, gains)
+        got, gate_up, qkv, gains, rest_rows = barrier(
+            (got, gate_up, (qkv0, qkv0_other, qkv1, qkv1_other), gains, rest_rows)
         )
-
-    def place_tokens(first_layer, second_layer, dtype):
-        pair = place(first_layer, second_layer)
+        gx = jnp.concatenate([gx] + got, axis=0)
+        return gx, gate_up, qkv, gains, rest_rows, y_other[0], gx_other[0], rows_other[1]
+
+    def rows_of(pair):
+        return jnp.concatenate(pair, axis=0).astype(F32)
+
+    def add_devices(gains):
+        gains = gains.reshape(2, devices, own)
+        mine = lax.dynamic_index_in_dim(gains, seq, 1, keepdims=False)
+        for k in range(1, devices):
+            block = lax.dynamic_index_in_dim(gains, (seq + k) % devices, 1, keepdims=False)
+            mine = mine + seq_shift(block, k)
+        return mine
+
+    n1_0, packed, v0 = project(0, x0, w_qkv_first, None)
+    ob0, w_out0, attn0, ffn_half = mix(packed, out_first, True, ffn_half)
+    gate_up0, down0 = columns(gather_rows(ffn_half), 2 * hidden, hidden)
+    ob0, attn_later = barrier((ob0, attn_later))
+    attn_later = gather_rows(attn_later)
+    y_part, fed0 = feed(0, x0, gather_features(ob0)[0], w_out0, gate_up0, down0)
+    y0 = gather_tokens((fed0[0] + reduce_tokens(y_part)).astype(BF16))
+    qkv1, out1 = columns(attn_later, 3 * local, local)
+    out1 = lax.dynamic_index_in_dim(
+        out1.reshape(devices, 2, own // 2, local), core, 1, keepdims=False
+    )
+    n1_1, packed, _ = project(1, y0, qkv1, v0)
+    ob1, w_out1, attn1, ffn_later = mix(packed, out1, False, ffn_later)
+    gate_up1, down1 = columns(gather_rows(ffn_later), 2 * hidden, hidden)
+    ob_all, y0_first = gather_features(ob1, to_first, (y0,))
+    y_part, fed1 = feed(1, y0, ob_all, w_out1, gate_up1, down1)
+    kept0 = (x0[:part].astype(F32), n1_0, attn0, ob0, w_out0, fed0, w_qkv_first, gate_up0, down0)
+    kept1 = (y0[:part].astype(F32), n1_1, attn1, ob1, w_out1, fed1, qkv1, gate_up1, down1)
+    gx1, gfirst, rows1, g_qkv1, gains1, y1 = backward(
+        1, gy1, None, kept1, (y_part, fed1[0]), ()
+    )
+    gx0, gate_up_grad, qkv, gains, rest_rows, y1_second, gx1_second, rest_second = backward(
+        0, gx1, gfirst, kept0, (), (rows1, g_qkv1, gains1, y1)
+    )
+
+    def tokens_of(pair, dtype):
         return jnp.stack([peer_order(m).astype(dtype) for m in pair])[None]
 
-    def place_rows(first_layer, second_layer):
-        pair = place(first_layer, second_layer)
-        return jnp.concatenate(pair, axis=0).astype(F32)[None]
-
-    activations = place_tokens(y0, y1, BF16)
-    input_grads = place_tokens(gx0, gx1, F32)
-    down_grad, gate_up_grad, out_grad, qkv_grad = [
-        place_rows(a, b) for a, b in zip(grads0, grads1)
-    ]
+    activations = tokens_of(settle(y0, y0_first, y1, y1_second), BF16)
+    gx0_first, rest_first = to_first(gx0), to_first(rest_rows)
+    input_grads = tokens_of(settle(gx0, gx0_first, gx1, gx1_second), F32)
+    gate_up_grad = gate_up_grad.reshape(1, own, 2, hidden)
     qkv_grad = (
-        qkv_grad.reshape(1, own, heads, 3, HEAD_DIM)
+        rows_of(settle(*qkv))
+        .reshape(1, own, heads, 3, HEAD_DIM)
         .transpose(0, 1, 3, 2, 4)
         .reshape(1, own, 3, local)
     )
-    gate_up_grad = gate_up_grad.reshape(1, own, 2, hidden)
-    gains = jnp.stack([gains0, gains1])
-    for axis, count in (("section", 2), ("head", peers), ("seq", devices)):
-        k = 1
-        while k < count:
-            gains = gains + lax.ppermute(gains, axis, [(i, i ^ k) for i in range(count)])
-            k *= 2
-    gains = lax.dynamic_index_in_dim(gains, core, 0, keepdims=False)
-    gains = lax.dynamic_slice_in_dim(gains, seq * own, own, 1)
+    out_grad, down_grad = [
+        g[None]
+        for g in columns(
+            rows_of(settle(rest_rows, rest_first, rows1[1], rest_second)), local, hidden
+        )
+    ]
     return (
         activations,
         input_grads,

time: 682 us -> 568 us (0.83)
  waiting for transfers between devices: 317 us -> 223 us
  blocking collectives: 31.3 us -> 0 us
  other arithmetic: 37.6 us -> 57.4 us
  matrix products: 60.1 us -> 45.9 us
  local copies, waits for them, and re-layouts: 29.3 us -> 41.5 us
  starting transfers between devices: 146 us -> 138 us
    reduce_scatter x6 -> x4, waiting for transfers between devices: 51.9 us -> 0.03 us  [scatter_rows(): lax.psum_scatter(by_rows(grad), ('seq', 'section'), scatter_dimension=0,...]
    ppermute x48, waiting for transfers between devices: 151 us -> 104 us  [head_peer(): return lax.ppermute(x, 'head', [(i, i ^ k) for i in range(n)])]
    all_gather x2 -> x0, blocking collectives: 31.3 us -> none  [gather_layers(): lax.all_gather(h, ('seq', 'section'), axis=0, tiled=True)]
    ppermute x17 -> x10, waiting for transfers between devices: 18 us -> 0.03 us  [the longest x5 0.01 us: to_first(): return lax.ppermute(value, 'section', [(1, 0)])]
    ppermute x17 -> x10, starting transfers between devices: 31.6 us -> 15.2 us  [the longest x5 8.2 us: to_second(): return lax.ppermute(value, 'section', [(0, 1)])]
    ppermute x30 -> x36, waiting for transfers between devices: 87.2 us -> 103 us  [seq_shift(): return lax.ppermute(x, 'seq', [(i, (i + k) % n) for i in range(n)])]
    dot_general x24, matrix products: 60.1 us -> 45.9 us  [dot(): return lax.dot_general(a, b, (dims, ((), ())), preferred_element_type=F32)]
    ppermute x30 -> x36, starting transfers between devices: 51.2 us -> 64.1 us  [seq_shift(): return lax.ppermute(x, 'seq', [(i, (i + k) % n) for i in range(n)])]
  transfers between devices with their start and end apart: 114 -> 109, of which waited for: 60 -> 49; matrix products, arithmetic and copies ran while one was open for 15% -> 19% of each run, Pallas kernels for 4% -> 6%
where the time goes in v2:
time: 568 us; the launch traced here: 558 us
  waiting for transfers between devices  223 us (39%)
  starting transfers between devices  138 us (24%)
  other arithmetic  57.4 us (10%)
  matrix products  45.9 us (8%)
  local copies, waits for them, and re-layouts  41.5 us (7%)
  Pallas kernels  35.7 us (6%)
  between operations  17.3 us (3%)
    ppermute x48, waiting for transfers between devices, head_peer(): return lax.ppermute(x, 'head', [(i, i ^ k) for i in range(n)])  104 us
    ppermute x36, waiting for transfers between devices, seq_shift(): return lax.ppermute(x, 'seq', [(i, (i + k) % n) for i in range(n)])  103 us
    ppermute x36, starting transfers between devices, seq_shift(): return lax.ppermute(x, 'seq', [(i, (i + k) % n) for i in range(n)])  64.1 us
    ppermute x48, starting transfers between devices, head_peer(): return lax.ppermute(x, 'head', [(i, i ^ k) for i in range(n)])  56.9 us
    dot_general x24, matrix products, dot(): return lax.dot_general(a, b, (dims, ((), ())), preferred_element_type=F32)  45.9 us
    pallas_call x2, Pallas kernels, attend_grad(): pl.pallas_call(grad_kernel, grid_spec=pltpu.PrefetchScalarGridSpec(num_sc...  20.2 us
    unnamed x240, local copies, waits for them, and re-layouts  18.7 us
    all_gather x3, waiting for transfers between devices, gather_rows(): return lax.all_gather(by_rows(half), ('seq', 'section'), axis=0, tiled=True)  15.9 us
  transfers between devices with their start and end apart: 109, of which 49 were waited for; matrix products, arithmetic and copies ran while one was open for 19% of the time, Pallas kernels for 6%

profile of v2, /device:TPU:0, one launch (start us, length us, event | category | flops | bytes accessed | tf_op | source)
XLA Modules:
  0.0 558.4 jit_solution(15069392255171912240)
XLA Ops:
  10.3 3.1 collective-permute-start.2
  13.3 2.6 collective-permute-start.3
  22.3 3.6 collective-permute-start.6
  29.1 4.3 collective-permute-done.5
  33.4 8.7 %collective-permute-done.6 = bf16[128,1024]{1,0:T(8,128)(2,1)S(1)} collective-permute-done((bf16[128,1024]{1,0:T(8,128)(2,1)S(1)}, bf16[128,1024]{1,0:T(8,128)(2,1)S(1)}, u32[]{:S(2)}, u32[]{:S(2)}) %collective-permute-start.6) | collective-permute-done | bytes 262176 | tf_op jit(solution)/shard_map/ppermute | solution.py:29
  49.6 5.9 %collective-permute-start.9 = (bf16[3,64,512]{2,1,0:T(8,128)(2,1)}, bf16[3,64,512]{2,1,0:T(8,128)(2,1)S(1)}, u32[]{:S(2)}, u32[]{:S(2)}) collective-permute-start(bf16[3,64,512]{2,1,0:T(8,128)(2,1)} %get-tuple-element.469), channel_id=1, source_target_pairs={{0,4},{4,8},{8,12},{12,0},{1,5},{5,9},{9,13},{13,1},{2,6},{6,10},{... | collective-permute-start | bytes 589832 | tf_op jit(solution)/shard_map/ppermute | solution.py:29
  66.0 6.1 %collective-permute-done.13 = bf16[4,128,256]{2,1,0:T(8,128)(2,1)S(1)} collective-permute-done((bf16[4,128,256]{2,1,0:T(8,128)(2,1)S(1)}, bf16[4,128,256]{2,1,0:T(8,128)(2,1)S(1)}, u32[]{:S(2)}, u32[]{:S(2)}) %collective-permute-start.13) | collective-permute-done | bytes 262176 | tf_op jit(solution)/shard_map/ppermute | solution.py:24
  74.2 7.8 %attend.2 = (f32[1,4,64,512]{3,2,1,0:T(8,128)S(1)}, bf16[1,4,64,512]{3,2,1,0:T(8,128)(2,1)S(1)}, f32[1,4,1,512]{3,2,1,0:T(1,128)S(1)}) custom-call(s32[4]{0:T(128)S(1)} %gather_fusion, s32[4]{0:T(128)S(1)} %get-tuple-element.571.qslot.kslot, s32[4]{0:T(128)S(1)} %get-tuple-element.571.qslot.kslot, s32[2]{0:T(128)S(1)} %pad_add_fusion.base, ...), custom_call_target="tpu_custom_call" | custom-call | flops 1073741824 | bytes 1572864 | tf_op jit(solution)/shard_map/attend/pallas_call | solution.py:276
  82.7 3.2 collective-permute-start.16
  87.5 4.9 collective-permute-done.16
  94.3 7.8 %collective-permute-done.17 = bf16[64,512]{1,0:T(8,128)(2,1)S(1)} collective-permute-done((bf16[64,512]{1,0:T(8,128)(2,1)}, bf16[64,512]{1,0:T(8,128)(2,1)S(1)}, u32[]{:S(2)}, u32[]{:S(2)}) %collective-permute-start.17) | collective-permute-done | bytes 65568 | tf_op jit(solution)/shard_map/ppermute | solution.py:29
  107.0 5.4 collective-permute-done.20
  112.4 5.5 collective-permute-done.21
  118.0 3.1 multiply_reduce_fusion.5
  122.7 6.6 %all-gather.4.cloned.1.call-done = bf16[1024,2112]{1,0:T(8,128)(2,1)} async-done(((bf16[128,2112]{1,0:T(8,128)(2,1)}), bf16[1024,2112]{1,0:T(8,128)(2,1)}) %all-gather.4.cloned.1.call-update) | async-done | bytes 4325392 | tf_op jit(solution)/shard_map/all_gather | solution.py:352
  129.3 3.6 fusion.6
  133.5 3.2 convolution_convert_fusion.9
  140.3 5.6 %collective-permute-done.23 = bf16[128,1024]{1,0:T(8,128)(2,1)S(1)} collective-permute-done((bf16[128,1024]{1,0:T(8,128)(2,1)S(1)}, bf16[128,1024]{1,0:T(8,128)(2,1)S(1)}, u32[]{:S(2)}, u32[]{:S(2)}) %collective-permute-start.23) | collective-permute-done | bytes 262176 | tf_op jit(solution)/shard_map/ppermute | solution.py:24
  146.0 6.1 %collective-permute-done.24 = bf16[128,1024]{1,0:T(8,128)(2,1)S(1)} collective-permute-done((bf16[128,1024]{1,0:T(8,128)(2,1)S(1)}, bf16[128,1024]{1,0:T(8,128)(2,1)S(1)}, u32[]{:S(2)}, u32[]{:S(2)}) %collective-permute-start.24) | collective-permute-done | bytes 262176 | tf_op jit(solution)/shard_map/ppermute | solution.py:24
  160.4 2.8 collective-permute-done.26
  163.2 5.0 collective-permute-done.27
  176.7 8.1 %collective-permute-done.29 = bf16[3,64,512]{2,1,0:T(8,128)(2,1)S(1)} collective-permute-done((bf16[3,64,512]{2,1,0:T(8,128)(2,1)S(1)}, bf16[3,64,512]{2,1,0:T(8,128)(2,1)S(1)}, u32[]{:S(2)}, u32[]{:S(2)}) %collective-permute-start.29) | collective-permute-done | bytes 196640 | tf_op jit(solution)/shard_map/ppermute | solution.py:29
  186.0 3.6 collective-permute-done.30
  191.2 7.8 %attend.3 = (f32[1,4,64,512]{3,2,1,0:T(8,128)S(1)}, bf16[1,4,64,512]{3,2,1,0:T(8,128)(2,1)S(1)}, f32[1,4,1,512]{3,2,1,0:T(1,128)S(1)}) custom-call(s32[4]{0:T(128)S(1)} %gather_fusion, s32[4]{0:T(128)S(1)} %get-tuple-element.571.qslot.kslot, s32[4]{0:T(128)S(1)} %get-tuple-element.571.qslot.kslot, s32[2]{0:T(128)S(1)} %pad_add_fusion.base, ...), custom_call_target="tpu_custom_call" | custom-call | flops 1073741824 | bytes 1572864 | tf_op jit(solution)/shard_map/attend/pallas_call | solution.py:276
  199.1 2.8 collective-permute-start.35
  208.1 8.5 %collective-permute-done.36 = bf16[64,512]{1,0:T(8,128)(2,1)S(1)} collective-permute-done((bf16[64,512]{1,0:T(8,128)(2,1)S(1)}, bf16[64,512]{1,0:T(8,128)(2,1)S(1)}, u32[]{:S(2)}, u32[]{:S(2)}) %collective-permute-start.36) | collective-permute-done | bytes 65568 | tf_op jit(solution)/shard_map/ppermute | solution.py:29
  223.5 4.0 collective-permute-done.39
  227.5 6.8 %collective-permute-done.40 = bf16[256,512]{1,0:T(8,128)(2,1)S(1)} collective-permute-done((bf16[256,512]{1,0:T(8,128)(2,1)S(1)}, bf16[256,512]{1,0:T(8,128)(2,1)S(1)}, u32[]{:S(2)}, u32[]{:S(2)}) %collective-permute-start.40) | collective-permute-done | bytes 262176 | tf_op jit(solution)/shard_map/ppermute | solution.py:24
  239.3 7.4 %all-gather.8.cloned.1.call-done = bf16[1024,2112]{1,0:T(8,128)(2,1)} async-done(((bf16[128,2112]{1,0:T(8,128)(2,1)}), bf16[1024,2112]{1,0:T(8,128)(2,1)}) %all-gather.8.cloned.1.call-update) | async-done | bytes 4325392 | tf_op jit(solution)/shard_map/all_gather | solution.py:352
  246.7 4.1 fusion.2
  256.7 3.4 convolution_convert_fusion.1
  264.9 3.8 convolution_convert_fusion.8
  270.5 6.0 %collective-permute-done.44 = bf16[128,1024]{1,0:T(8,128)(2,1)S(1)} collective-permute-done((bf16[128,1024]{1,0:T(8,128)(2,1)S(1)}, bf16[128,1024]{1,0:T(8,128)(2,1)S(1)}, u32[]{:S(2)}, u32[]{:S(2)}) %collective-permute-start.44) | collective-permute-done | bytes 262176 | tf_op jit(solution)/shard_map/ppermute | solution.py:24
  283.2 4.7 collective-permute-done.46
  287.9 5.0 collective-permute-done.47
  296.2 2.4 collective-permute-start.51
  306.2 10.1 %attend_grad.2 = (f32[1,4,64,512]{3,2,1,0:T(8,128)S(1)}, f32[1,4,64,512]{3,2,1,0:T(8,128)S(1)}, f32[1,4,64,512]{3,2,1,0:T(8,128)S(1)}) custom-call(s32[4]{0:T(128)S(1)} %gather_fusion, s32[4]{0:T(128)S(1)} %get-tuple-element.571.qslot.kslot, s32[4]{0:T(128)S(1)} %get-tuple-element.571.qslot.kslot, s32[2]{0:T(128)S(1)} %pad_add_fusion.base, ...), custom_call_target="tpu_custom_call" | custom-call | flops 2684354560 | bytes 3145728 | tf_op jit(solution)/shard_map/attend_grad/pallas_call | solution.py:303
  319.6 3.3 collective-permute-start.55
  322.9 7.0 %collective-permute-done.55 = bf16[3,64,512]{2,1,0:T(8,128)(2,1)} collective-permute-done((bf16[3,64,512]{2,1,0:T(8,128)(2,1)S(1)}, bf16[3,64,512]{2,1,0:T(8,128)(2,1)}, u32[]{:S(2)}, u32[]{:S(2)}) %collective-permute-start.55) | collective-permute-done | bytes 196640 | tf_op jit(solution)/shard_map/ppermute | solution.py:29
  335.4 2.3 collective-permute-start.57
  340.2 8.3 %collective-permute-done.56 = bf16[3,64,512]{2,1,0:T(8,128)(2,1)} collective-permute-done((bf16[3,64,512]{2,1,0:T(8,128)(2,1)}, bf16[3,64,512]{2,1,0:T(8,128)(2,1)}, u32[]{:S(2)}, u32[]{:S(2)}) %collective-permute-start.56) | collective-permute-done | bytes 196640 | tf_op jit(solution)/shard_map/ppermute | solution.py:29
  356.4 4.7 collective-permute-done.61
  361.1 4.3 collective-permute-done.62
  370.3 2.7 collective-permute-start.70
  375.0 3.9 collective-permute-done.65
  378.9 3.0 multiply_convert_fusion.3
  390.9 2.4 pad_maximum_fusion
  393.3 3.3 collective-permute-done.68
  398.1 2.3 fusion.166
  412.1 3.9 collective-permute-done.72
  422.9 6.2 %collective-permute-done.75 = bf16[64,512]{1,0:T(8,128)(2,1)} collective-permute-done((bf16[64,512]{1,0:T(8,128)(2,1)}, bf16[64,512]{1,0:T(8,128)(2,1)}, u32[]{:S(2)}, u32[]{:S(2)}) %collective-permute-start.75) | collective-permute-done | bytes 65568 | tf_op jit(solution)/shard_map/ppermute | solution.py:29
  430.0 10.1 %attend_grad.3 = (f32[1,4,64,512]{3,2,1,0:T(8,128)S(1)}, f32[1,4,64,512]{3,2,1,0:T(8,128)S(1)}, f32[1,4,64,512]{3,2,1,0:T(8,128)S(1)}) custom-call(s32[4]{0:T(128)S(1)} %gather_fusion, s32[4]{0:T(128)S(1)} %get-tuple-element.571.qslot.kslot, s32[4]{0:T(128)S(1)} %get-tuple-element.571.qslot.kslot, s32[2]{0:T(128)S(1)} %pad_add_fusion.base, ...), custom_call_target="tpu_custom_call" | custom-call | flops 2684354560 | bytes 3145728 | tf_op jit(solution)/shard_map/attend_grad/pallas_call | solution.py:303
  443.3 9.3 %collective-permute-done.78 = bf16[3,64,512]{2,1,0:T(8,128)(2,1)S(1)} collective-permute-done((bf16[3,64,512]{2,1,0:T(8,128)(2,1)S(1)}, bf16[3,64,512]{2,1,0:T(8,128)(2,1)S(1)}, u32[]{:S(2)}, u32[]{:S(2)}) %collective-permute-start.78) | collective-permute-done | bytes 196640 | tf_op jit(solution)/shard_map/ppermute | solution.py:29
  455.1 3.9 collective-permute-start.80
  461.9 8.9 %collective-permute-done.79 = bf16[3,64,512]{2,1,0:T(8,128)(2,1)S(1)} collective-permute-done((bf16[3,64,512]{2,1,0:T(8,128)(2,1)}, bf16[3,64,512]{2,1,0:T(8,128)(2,1)S(1)}, u32[]{:S(2)}, u32[]{:S(2)}) %collective-permute-start.79) | collective-permute-done | bytes 196640 | tf_op jit(solution)/shard_map/ppermute | solution.py:29
  479.0 4.7 collective-permute-done.83
  483.6 4.0 collective-permute-done.84
  490.9 2.8 collective-permute-start.90
  498.9 3.8 collective-permute-done.88
  504.0 7.2 %collective-permute-done.89 = bf16[128,768]{1,0:T(8,128)(2,1)S(1)} collective-permute-done((bf16[128,768]{1,0:T(8,128)(2,1)S(1)}, bf16[128,768]{1,0:T(8,128)(2,1)S(1)}, u32[]{:S(2)}, u32[]{:S(2)}) %collective-permute-start.89) | collective-permute-done | bytes 196640 | tf_op jit(solution)/shard_map/ppermute | solution.py:29
  511.3 7.3 %collective-permute-start.97 = (f32[2,256]{1,0:T(2,128)S(1)}, f32[2,256]{1,0:T(2,128)S(1)}, u32[]{:S(2)}, u32[]{:S(2)}) collective-permute-start(f32[2,256]{1,0:T(2,128)S(1)} %get-tuple-element.553), channel_id=1, source_target_pairs={{0,4},{4,8},{8,12},{12,0},{1,5},{5,9},{9,13},{13,1},{2,6},{6,10},{... | collective-permute-start | bytes 6152 | tf_op jit(solution)/shard_map/ppermute | solution.py:29
  518.5 2.7 collective-permute-start.98
  526.8 3.0 collective-permute-done.93
  548.8 2.3 fusion.14
  (634 shorter events, 220.2 us)
Async XLA Ops:
  7.2 122.1 %all-gather.4.cloned.1.call-start = ((), (), s32[]{:S(2)}) async-start(), calls=%async_computation.4 | async-start | bytes 5013504 | tf_op jit(solution)/shard_map/all_gather | solution.py:352
  9.9 11.5 %collective-permute-start = (bf16[128,1024]{1,0:T(8,128)(2,1)S(1)}, bf16[128,1024]{1,0:T(8,128)(2,1)S(1)}, u32[]{:S(2)}, u32[]{:S(2)}) collective-permute-start(bf16[128,1024]{1,0:T(8,128)(2,1)S(1)} %fusion.131), channel_id=1, source_target_pairs={{0,16},{16,0},{1,17},{17,1},{2,18},{18,2},{3,19},{19,3},{4,20},{20... | collective-permute-start | bytes 786440 | tf_op jit(solution)/shard_map/ppermute | solution.py:33
  22.2 11.1 %collective-permute-start.5 = (bf16[128,1024]{1,0:T(8,128)(2,1)S(1)}, bf16[128,1024]{1,0:T(8,128)(2,1)S(1)}, u32[]{:S(2)}, u32[]{:S(2)}) collective-permute-start(bf16[128,1024]{1,0:T(8,128)(2,1)S(1)} %get-tuple-element.179), channel_id=1, source_target_pairs={{0,4},{4,8},{8,12},{12,0},{1,5},{5,9},{9,13},{13,1},{2,6},{6,10},{... | collective-permute-start | bytes 786440 | tf_op jit(solution)/shard_map/ppermute | solution.py:29
  22.3 19.8 %collective-permute-start.6 = (bf16[128,1024]{1,0:T(8,128)(2,1)S(1)}, bf16[128,1024]{1,0:T(8,128)(2,1)S(1)}, u32[]{:S(2)}, u32[]{:S(2)}) collective-permute-start(bf16[128,1024]{1,0:T(8,128)(2,1)S(1)} %get-tuple-element.179), channel_id=1, source_target_pairs={{0,8},{4,12},{8,0},{12,4},{1,9},{5,13},{9,1},{13,5},{2,10},{6,14},... | collective-permute-start | bytes 786440 | tf_op jit(solution)/shard_map/ppermute | solution.py:29
  25.9 16.2 %collective-permute-start.7 = (bf16[128,1024]{1,0:T(8,128)(2,1)S(1)}, bf16[128,1024]{1,0:T(8,128)(2,1)S(1)}, u32[]{:S(2)}, u32[]{:S(2)}) collective-permute-start(bf16[128,1024]{1,0:T(8,128)(2,1)S(1)} %get-tuple-element.179), channel_id=1, source_target_pairs={{0,12},{4,0},{8,4},{12,8},{1,13},{5,1},{9,5},{13,9},{2,14},{6,2},{... | collective-permute-start | bytes 786440 | tf_op jit(solution)/shard_map/ppermute | solution.py:29
  27.7 27.7 %collective-permute-start.15 = (bf16[128,2112]{0,1:T(8,128)(2,1)}, bf16[128,2112]{0,1:T(8,128)(2,1)}, u32[]{:S(2)}, u32[]{:S(2)}) collective-permute-start(bf16[128,2112]{0,1:T(8,128)(2,1)} %copy.93), channel_id=1, source_target_pairs={{0,16},{16,0},{1,17},{17,1},{2,18},{18,2},{3,19},{19,3},{4,20},{20... | collective-permute-start | bytes 1622024 | tf_op jit(solution)/shard_map/ppermute | solution.py:33
  49.6 11.4 %collective-permute-start.9 = (bf16[3,64,512]{2,1,0:T(8,128)(2,1)}, bf16[3,64,512]{2,1,0:T(8,128)(2,1)S(1)}, u32[]{:S(2)}, u32[]{:S(2)}) collective-permute-start(bf16[3,64,512]{2,1,0:T(8,128)(2,1)} %get-tuple-element.469), channel_id=1, source_target_pairs={{0,4},{4,8},{8,12},{12,0},{1,5},{5,9},{9,13},{13,1},{2,6},{6,10},{... | collective-permute-start | bytes 589832 | tf_op jit(solution)/shard_map/ppermute | solution.py:29
  58.3 13.7 %collective-permute-start.13 = (bf16[4,128,256]{2,1,0:T(8,128)(2,1)S(1)}, bf16[4,128,256]{2,1,0:T(8,128)(2,1)S(1)}, u32[]{:S(2)}, u32[]{:S(2)}) collective-permute-start(bf16[4,128,256]{2,1,0:T(8,128)(2,1)S(1)} %pad_maximum_fusion.26), channel_id=1, source_target_pairs={{0,2},{1,3},{2,0},{3,1},{4,6},{5,7},{6,4},{7,5},{8,10},{9,11},{10,... | collective-permute-start | bytes 786440 | tf_op jit(solution)/shard_map/ppermute | solution.py:24
  59.9 12.2 %collective-permute-start.14 = (bf16[4,128,256]{2,1,0:T(8,128)(2,1)S(1)}, bf16[4,128,256]{2,1,0:T(8,128)(2,1)S(1)}, u32[]{:S(2)}, u32[]{:S(2)}) collective-permute-start(bf16[4,128,256]{2,1,0:T(8,128)(2,1)S(1)} %pad_maximum_fusion.26), channel_id=1, source_target_pairs={{0,3},{1,2},{2,1},{3,0},{4,7},{5,6},{6,5},{7,4},{8,11},{9,10},{10,... | collective-permute-start | bytes 786440 | tf_op jit(solution)/shard_map/ppermute | solution.py:24
  60.3 11.9 %collective-permute-start.10 = (bf16[3,64,512]{2,1,0:T(8,128)(2,1)}, bf16[3,64,512]{2,1,0:T(8,128)(2,1)S(1)}, u32[]{:S(2)}, u32[]{:S(2)}) collective-permute-start(bf16[3,64,512]{2,1,0:T(8,128)(2,1)} %get-tuple-element.468), channel_id=1, source_target_pairs={{0,8},{4,12},{8,0},{12,4},{1,9},{5,13},{9,1},{13,5},{2,10},{6,14},... | collective-permute-start | bytes 589832 | tf_op jit(solution)/shard_map/ppermute | solution.py:29
  61.0 11.2 %collective-permute-start.11 = (bf16[3,64,512]{2,1,0:T(8,128)(2,1)}, bf16[3,64,512]{2,1,0:T(8,128)(2,1)S(1)}, u32[]{:S(2)}, u32[]{:S(2)}) collective-permute-start(bf16[3,64,512]{2,1,0:T(8,128)(2,1)} %get-tuple-element.467), channel_id=1, source_target_pairs={{0,12},{4,0},{8,4},{12,8},{1,13},{5,1},{9,5},{13,9},{2,14},{6,2},{... | collective-permute-start | bytes 589832 | tf_op jit(solution)/shard_map/ppermute | solution.py:29
  73.1 86.2 %all-gather.6.cloned.1.call-start = ((), (), s32[]{:S(2)}) async-start(), calls=%async_computation.5 | async-start | bytes 2359296 | tf_op jit(solution)/shard_map/all_gather | solution.py:352
  85.9 16.2 %collective-permute-start.17 = (bf16[64,512]{1,0:T(8,128)(2,1)}, bf16[64,512]{1,0:T(8,128)(2,1)S(1)}, u32[]{:S(2)}, u32[]{:S(2)}) collective-permute-start(bf16[64,512]{1,0:T(8,128)(2,1)} %get-tuple-element.530), channel_id=1, source_target_pairs={{0,8},{4,12},{8,0},{12,4},{1,9},{5,13},{9,1},{13,5},{2,10},{6,14},... | collective-permute-start | bytes 196616 | tf_op jit(solution)/shard_map/ppermute | solution.py:29
  87.5 14.6 %collective-permute-start.18 = (bf16[64,512]{1,0:T(8,128)(2,1)}, bf16[64,512]{1,0:T(8,128)(2,1)S(1)}, u32[]{:S(2)}, u32[]{:S(2)}) collective-permute-start(bf16[64,512]{1,0:T(8,128)(2,1)} %get-tuple-element.529), channel_id=1, source_target_pairs={{0,4},{4,8},{8,12},{12,0},{1,5},{5,9},{9,13},{13,1},{2,6},{6,10},{... | collective-permute-start | bytes 196616 | tf_op jit(solution)/shard_map/ppermute | solution.py:29
  104.7 13.2 %collective-permute-start.21 = (bf16[256,512]{1,0:T(8,128)(2,1)S(1)}, bf16[256,512]{1,0:T(8,128)(2,1)S(1)}, u32[]{:S(2)}, u32[]{:S(2)}) collective-permute-start(bf16[256,512]{1,0:T(8,128)(2,1)S(1)} %bitcast.475), channel_id=1, source_target_pairs={{0,2},{1,3},{2,0},{3,1},{4,6},{5,7},{6,4},{7,5},{8,10},{9,11},{10,... | collective-permute-start | bytes 786440 | tf_op jit(solution)/shard_map/ppermute | solution.py:24
  106.2 11.7 %collective-permute-start.22 = (bf16[256,512]{1,0:T(8,128)(2,1)S(1)}, bf16[256,512]{1,0:T(8,128)(2,1)S(1)}, u32[]{:S(2)}, u32[]{:S(2)}) collective-permute-start(bf16[256,512]{1,0:T(8,128)(2,1)S(1)} %bitcast.476), channel_id=1, source_target_pairs={{0,3},{1,2},{2,1},{3,0},{4,7},{5,6},{6,5},{7,4},{8,11},{9,10},{10,... | collective-permute-start | bytes 786440 | tf_op jit(solution)/shard_map/ppermute | solution.py:24
  106.7 140.0 %all-gather.8.cloned.1.call-start = ((), (), s32[]{:S(2)}) async-start(), calls=%async_computation.6 | async-start | bytes 5013504 | tf_op jit(solution)/shard_map/all_gather | solution.py:352
  138.3 13.8 %collective-permute-start.24 = (bf16[128,1024]{1,0:T(8,128)(2,1)S(1)}, bf16[128,1024]{1,0:T(8,128)(2,1)S(1)}, u32[]{:S(2)}, u32[]{:S(2)}) collective-permute-start(bf16[128,1024]{1,0:T(8,128)(2,1)S(1)} %get-tuple-element.438), channel_id=1, source_target_pairs={{0,2},{1,3},{2,0},{3,1},{4,6},{5,7},{6,4},{7,5},{8,10},{9,11},{10,... | collective-permute-start | bytes 786440 | tf_op jit(solution)/shard_map/ppermute | solution.py:24
  139.8 12.3 %collective-permute-start.25 = (bf16[128,1024]{1,0:T(8,128)(2,1)S(1)}, bf16[128,1024]{1,0:T(8,128)(2,1)S(1)}, u32[]{:S(2)}, u32[]{:S(2)}) collective-permute-start(bf16[128,1024]{1,0:T(8,128)(2,1)S(1)} %get-tuple-element.437), channel_id=1, source_target_pairs={{0,3},{1,2},{2,1},{3,0},{4,7},{5,6},{6,5},{7,4},{8,11},{9,10},{10,... | collective-permute-start | bytes 786440 | tf_op jit(solution)/shard_map/ppermute | solution.py:24
  155.2 13.0 %collective-permute-start.27 = (bf16[128,1024]{1,0:T(8,128)(2,1)S(1)}, bf16[128,1024]{1,0:T(8,128)(2,1)S(1)}, u32[]{:S(2)}, u32[]{:S(2)}) collective-permute-start(bf16[128,1024]{1,0:T(8,128)(2,1)S(1)} %get-tuple-element.377), channel_id=1, source_target_pairs={{0,2},{1,3},{2,0},{3,1},{4,6},{5,7},{6,4},{7,5},{8,10},{9,11},{10,... | collective-permute-start | bytes 786440 | tf_op jit(solution)/shard_map/ppermute | solution.py:24
  156.0 12.3 %collective-permute-start.28 = (bf16[128,1024]{1,0:T(8,128)(2,1)S(1)}, bf16[128,1024]{1,0:T(8,128)(2,1)S(1)}, u32[]{:S(2)}, u32[]{:S(2)}) collective-permute-start(bf16[128,1024]{1,0:T(8,128)(2,1)S(1)} %get-tuple-element.377), channel_id=1, source_target_pairs={{0,3},{1,2},{2,1},{3,0},{4,7},{5,6},{6,5},{7,4},{8,11},{9,10},{10,... | collective-permute-start | bytes 786440 | tf_op jit(solution)/shard_map/ppermute | solution.py:24
  171.5 13.4 %collective-permute-start.32 = (bf16[4,128,256]{2,1,0:T(8,128)(2,1)S(1)}, bf16[4,128,256]{2,1,0:T(8,128)(2,1)S(1)}, u32[]{:S(2)}, u32[]{:S(2)}) collective-permute-start(bf16[4,128,256]{2,1,0:T(8,128)(2,1)S(1)} %dynamic-slice_bitcast_fusion.12), channel_id=1, source_target_pairs={{0,1},{1,0},{2,3},{3,2},{4,5},{5,4},{6,7},{7,6},{8,9},{9,8},{10,11... | collective-permute-start | bytes 786440 | tf_op jit(solution)/shard_map/ppermute | solution.py:24
  172.1 12.7 %collective-permute-start.33 = (bf16[4,128,256]{2,1,0:T(8,128)(2,1)S(1)}, bf16[4,128,256]{2,1,0:T(8,128)(2,1)S(1)}, u32[]{:S(2)}, u32[]{:S(2)}) collective-permute-start(bf16[4,128,256]{2,1,0:T(8,128)(2,1)S(1)} %dynamic-slice_bitcast_fusion.12), channel_id=1, source_target_pairs={{0,2},{1,3},{2,0},{3,1},{4,6},{5,7},{6,4},{7,5},{8,10},{9,11},{10,... | collective-permute-start | bytes 786440 | tf_op jit(solution)/shard_map/ppermute | solution.py:24
  173.5 11.3 %collective-permute-start.34 = (bf16[4,128,256]{2,1,0:T(8,128)(2,1)S(1)}, bf16[4,128,256]{2,1,0:T(8,128)(2,1)S(1)}, u32[]{:S(2)}, u32[]{:S(2)}) collective-permute-start(bf16[4,128,256]{2,1,0:T(8,128)(2,1)S(1)} %dynamic-slice_bitcast_fusion.12), channel_id=1, source_target_pairs={{0,3},{1,2},{2,1},{3,0},{4,7},{5,6},{6,5},{7,4},{8,11},{9,10},{10,... | collective-permute-start | bytes 786440 | tf_op jit(solution)/shard_map/ppermute | solution.py:24
  175.1 14.4 %collective-permute-start.30 = (bf16[3,64,512]{2,1,0:T(8,128)(2,1)S(1)}, bf16[3,64,512]{2,1,0:T(8,128)(2,1)S(1)}, u32[]{:S(2)}, u32[]{:S(2)}) collective-permute-start(bf16[3,64,512]{2,1,0:T(8,128)(2,1)S(1)} %get-tuple-element.462), channel_id=1, source_target_pairs={{0,8},{4,12},{8,0},{12,4},{1,9},{5,13},{9,1},{13,5},{2,10},{6,14},... | collective-permute-start | bytes 589832 | tf_op jit(solution)/shard_map/ppermute | solution.py:29
  191.2 261.5 %reduce-scatter.7.cloned.1.call-start = ((), (), s32[]{:S(2)}) async-start(), calls=%async_computation.8 | async-start | bytes 2359296 | tf_op jit(solution)/shard_map/reduce_scatter | solution.py:391
  201.9 14.7 %collective-permute-start.36 = (bf16[64,512]{1,0:T(8,128)(2,1)S(1)}, bf16[64,512]{1,0:T(8,128)(2,1)S(1)}, u32[]{:S(2)}, u32[]{:S(2)}) collective-permute-start(bf16[64,512]{1,0:T(8,128)(2,1)S(1)} %get-tuple-element.512), channel_id=1, source_target_pairs={{0,8},{4,12},{8,0},{12,4},{1,9},{5,13},{9,1},{13,5},{2,10},{6,14},... | collective-permute-start | bytes 196616 | tf_op jit(solution)/shard_map/ppermute | solution.py:29
  202.9 13.8 %collective-permute-start.37 = (bf16[64,512]{1,0:T(8,128)(2,1)S(1)}, bf16[64,512]{1,0:T(8,128)(2,1)S(1)}, u32[]{:S(2)}, u32[]{:S(2)}) collective-permute-start(bf16[64,512]{1,0:T(8,128)(2,1)S(1)} %get-tuple-element.511), channel_id=1, source_target_pairs={{0,4},{4,8},{8,12},{12,0},{1,5},{5,9},{9,13},{13,1},{2,6},{6,10},{... | collective-permute-start | bytes 196616 | tf_op jit(solution)/shard_map/ppermute | solution.py:29
  216.8 17.5 %collective-permute-start.42 = (bf16[512,1024]{1,0:T(8,128)(2,1)S(1)}, bf16[512,1024]{1,0:T(8,128)(2,1)S(1)}, u32[]{:S(2)}, u32[]{:S(2)}) collective-permute-start(bf16[512,1024]{1,0:T(8,128)(2,1)S(1)} %copy-done.1), channel_id=1, source_target_pairs={{16,0},{17,1},{18,2},{19,3},{20,4},{21,5},{22,6},{23,7},{24,8},{25... | collective-permute-start | bytes 3145736 | tf_op jit(solution)/shard_map/ppermute | solution.py:542
  219.5 14.7 %collective-permute-start.40 = (bf16[256,512]{1,0:T(8,128)(2,1)S(1)}, bf16[256,512]{1,0:T(8,128)(2,1)S(1)}, u32[]{:S(2)}, u32[]{:S(2)}) collective-permute-start(bf16[256,512]{1,0:T(8,128)(2,1)S(1)} %bitcast.480), channel_id=1, source_target_pairs={{0,2},{1,3},{2,0},{3,1},{4,6},{5,7},{6,4},{7,5},{8,10},{9,11},{10,... | collective-permute-start | bytes 786440 | tf_op jit(solution)/shard_map/ppermute | solution.py:24
  221.2 13.1 %collective-permute-start.41 = (bf16[256,512]{1,0:T(8,128)(2,1)S(1)}, bf16[256,512]{1,0:T(8,128)(2,1)S(1)}, u32[]{:S(2)}, u32[]{:S(2)}) collective-permute-start(bf16[256,512]{1,0:T(8,128)(2,1)S(1)} %bitcast.481), channel_id=1, source_target_pairs={{0,3},{1,2},{2,1},{3,0},{4,7},{5,6},{6,5},{7,4},{8,11},{9,10},{10,... | collective-permute-start | bytes 786440 | tf_op jit(solution)/shard_map/ppermute | solution.py:24
  262.7 13.8 %collective-permute-start.44 = (bf16[128,1024]{1,0:T(8,128)(2,1)S(1)}, bf16[128,1024]{1,0:T(8,128)(2,1)S(1)}, u32[]{:S(2)}, u32[]{:S(2)}) collective-permute-start(bf16[128,1024]{1,0:T(8,128)(2,1)S(1)} %get-tuple-element.434), channel_id=1, source_target_pairs={{0,2},{1,3},{2,0},{3,1},{4,6},{5,7},{6,4},{7,5},{8,10},{9,11},{10,... | collective-permute-start | bytes 786440 | tf_op jit(solution)/shard_map/ppermute | solution.py:24
  264.3 12.2 %collective-permute-start.45 = (bf16[128,1024]{1,0:T(8,128)(2,1)S(1)}, bf16[128,1024]{1,0:T(8,128)(2,1)S(1)}, u32[]{:S(2)}, u32[]{:S(2)}) collective-permute-start(bf16[128,1024]{1,0:T(8,128)(2,1)S(1)} %get-tuple-element.433), channel_id=1, source_target_pairs={{0,3},{1,2},{2,1},{3,0},{4,7},{5,6},{6,5},{7,4},{8,11},{9,10},{10,... | collective-permute-start | bytes 786440 | tf_op jit(solution)/shard_map/ppermute | solution.py:24
  279.9 13.0 %collective-permute-start.47 = (bf16[128,1024]{1,0:T(8,128)(2,1)S(1)}, bf16[128,1024]{1,0:T(8,128)(2,1)S(1)}, u32[]{:S(2)}, u32[]{:S(2)}) collective-permute-start(bf16[128,1024]{1,0:T(8,128)(2,1)S(1)} %get-tuple-element.237), channel_id=1, source_target_pairs={{0,2},{1,3},{2,0},{3,1},{4,6},{5,7},{6,4},{7,5},{8,10},{9,11},{10,... | collective-permute-start | bytes 786440 | tf_op jit(solution)/shard_map/ppermute | solution.py:24
  280.6 12.2 %collective-permute-start.48 = (bf16[128,1024]{1,0:T(8,128)(2,1)S(1)}, bf16[128,1024]{1,0:T(8,128)(2,1)S(1)}, u32[]{:S(2)}, u32[]{:S(2)}) collective-permute-start(bf16[128,1024]{1,0:T(8,128)(2,1)S(1)} %get-tuple-element.237), channel_id=1, source_target_pairs={{0,3},{1,2},{2,1},{3,0},{4,7},{5,6},{6,5},{7,4},{8,11},{9,10},{10,... | collective-permute-start | bytes 786440 | tf_op jit(solution)/shard_map/ppermute | solution.py:24
  301.4 151.3 %reduce-scatter.5.cloned.1.call-start = ((), (), s32[]{:S(2)}) async-start(), calls=%async_computation.7 | async-start | bytes 3244032 | tf_op jit(solution)/shard_map/reduce_scatter | solution.py:391
  302.6 13.7 %collective-permute-start.52 = (bf16[128,1024]{1,0:T(8,128)(2,1)S(1)}, bf16[128,1024]{1,0:T(8,128)(2,1)S(1)}, u32[]{:S(2)}, u32[]{:S(2)}) collective-permute-start(bf16[128,1024]{1,0:T(8,128)(2,1)S(1)} %get-tuple-element.430), channel_id=1, source_target_pairs={{0,1},{1,0},{2,3},{3,2},{4,5},{5,4},{6,7},{7,6},{8,9},{9,8},{10,11... | collective-permute-start | bytes 786440 | tf_op jit(solution)/shard_map/ppermute | solution.py:24
  303.2 13.1 %collective-permute-start.53 = (bf16[128,1024]{1,0:T(8,128)(2,1)S(1)}, bf16[128,1024]{1,0:T(8,128)(2,1)S(1)}, u32[]{:S(2)}, u32[]{:S(2)}) collective-permute-start(bf16[128,1024]{1,0:T(8,128)(2,1)S(1)} %get-tuple-element.432), channel_id=1, source_target_pairs={{0,2},{1,3},{2,0},{3,1},{4,6},{5,7},{6,4},{7,5},{8,10},{9,11},{10,... | collective-permute-start | bytes 786440 | tf_op jit(solution)/shard_map/ppermute | solution.py:24
  305.0 11.3 %collective-permute-start.54 = (bf16[128,1024]{1,0:T(8,128)(2,1)S(1)}, bf16[128,1024]{1,0:T(8,128)(2,1)S(1)}, u32[]{:S(2)}, u32[]{:S(2)}) collective-permute-start(bf16[128,1024]{1,0:T(8,128)(2,1)S(1)} %get-tuple-element.431), channel_id=1, source_target_pairs={{0,3},{1,2},{2,1},{3,0},{4,7},{5,6},{6,5},{7,4},{8,11},{9,10},{10,... | collective-permute-start | bytes 786440 | tf_op jit(solution)/shard_map/ppermute | solution.py:24
  333.5 15.0 %collective-permute-start.56 = (bf16[3,64,512]{2,1,0:T(8,128)(2,1)}, bf16[3,64,512]{2,1,0:T(8,128)(2,1)}, u32[]{:S(2)}, u32[]{:S(2)}) collective-permute-start(bf16[3,64,512]{2,1,0:T(8,128)(2,1)} %get-tuple-element.460), channel_id=1, source_target_pairs={{0,8},{4,12},{8,0},{12,4},{1,9},{5,13},{9,1},{13,5},{2,10},{6,14},... | collective-permute-start | bytes 589832 | tf_op jit(solution)/shard_map/ppermute | solution.py:29
  335.4 13.1 %collective-permute-start.57 = (bf16[3,64,512]{2,1,0:T(8,128)(2,1)S(1)}, bf16[3,64,512]{2,1,0:T(8,128)(2,1)}, u32[]{:S(2)}, u32[]{:S(2)}) collective-permute-start(bf16[3,64,512]{2,1,0:T(8,128)(2,1)S(1)} %get-tuple-element.457), channel_id=1, source_target_pairs={{0,4},{4,8},{8,12},{12,0},{1,5},{5,9},{9,13},{13,1},{2,6},{6,10},{... | collective-permute-start | bytes 589832 | tf_op jit(solution)/shard_map/ppermute | solution.py:29
  337.7 156.0 %reduce-scatter.9.cloned.1.call-start = ((), (), s32[]{:S(2)}) async-start(), calls=%async_computation.9 | async-start | bytes 5013504 | tf_op jit(solution)/shard_map/reduce_scatter | solution.py:391
  353.3 12.1 %collective-permute-start.62 = (bf16[128,1024]{1,0:T(8,128)(2,1)S(1)}, bf16[128,1024]{1,0:T(8,128)(2,1)S(1)}, u32[]{:S(2)}, u32[]{:S(2)}) collective-permute-start(bf16[128,1024]{1,0:T(8,128)(2,1)S(1)} %get-tuple-element.424), channel_id=1, source_target_pairs={{0,2},{1,3},{2,0},{3,1},{4,6},{5,7},{6,4},{7,5},{8,10},{9,11},{10,... | collective-permute-start | bytes 786440 | tf_op jit(solution)/shard_map/ppermute | solution.py:24
  355.0 10.5 %collective-permute-start.63 = (bf16[128,1024]{1,0:T(8,128)(2,1)S(1)}, bf16[128,1024]{1,0:T(8,128)(2,1)S(1)}, u32[]{:S(2)}, u32[]{:S(2)}) collective-permute-start(bf16[128,1024]{1,0:T(8,128)(2,1)S(1)} %get-tuple-element.423), channel_id=1, source_target_pairs={{0,3},{1,2},{2,1},{3,0},{4,7},{5,6},{6,5},{7,4},{8,11},{9,10},{10,... | collective-permute-start | bytes 786440 | tf_op jit(solution)/shard_map/ppermute | solution.py:24
  367.5 11.3 %collective-permute-start.65 = (bf16[128,1024]{1,0:T(8,128)(2,1)S(1)}, bf16[128,1024]{1,0:T(8,128)(2,1)S(1)}, u32[]{:S(2)}, u32[]{:S(2)}) collective-permute-start(bf16[128,1024]{1,0:T(8,128)(2,1)S(1)} %fusion.90), channel_id=1, source_target_pairs={{0,2},{1,3},{2,0},{3,1},{4,6},{5,7},{6,4},{7,5},{8,10},{9,11},{10,... | collective-permute-start | bytes 786440 | tf_op jit(solution)/shard_map/ppermute | solution.py:24
  368.3 10.5 %collective-permute-start.66 = (bf16[128,1024]{1,0:T(8,128)(2,1)S(1)}, bf16[128,1024]{1,0:T(8,128)(2,1)S(1)}, u32[]{:S(2)}, u32[]{:S(2)}) collective-permute-start(bf16[128,1024]{1,0:T(8,128)(2,1)S(1)} %fusion.90), channel_id=1, source_target_pairs={{0,3},{1,2},{2,1},{3,0},{4,7},{5,6},{6,5},{7,4},{8,11},{9,10},{10,... | collective-permute-start | bytes 786440 | tf_op jit(solution)/shard_map/ppermute | solution.py:24
  370.3 26.3 %collective-permute-start.70 = (bf16[512,1024]{1,0:T(8,128)(2,1)}, bf16[512,1024]{1,0:T(8,128)(2,1)}, u32[]{:S(2)}, u32[]{:S(2)}) collective-permute-start(bf16[512,1024]{1,0:T(8,128)(2,1)} %pad_maximum_fusion.15), channel_id=1, source_target_pairs={{0,16},{1,17},{2,18},{3,19},{4,20},{5,21},{6,22},{7,23},{8,24},{9,... | collective-permute-start | bytes 3145736 | tf_op jit(solution)/shard_map/ppermute | solution.py:545
  400.5 126.3 %reduce-scatter.11.cloned.1.call-start = ((), (), s32[]{:S(2)}) async-start(), calls=%async_computation.10 | async-start | bytes 2359296 | tf_op jit(solution)/shard_map/reduce_scatter | solution.py:391
  401.6 14.5 %collective-permute-start.74 = (bf16[512,1024]{1,0:T(8,128)(2,1)S(1)}, bf16[512,1024]{1,0:T(8,128)(2,1)S(1)}, u32[]{:S(2)}, u32[]{:S(2)}) collective-permute-start(bf16[512,1024]{1,0:T(8,128)(2,1)S(1)} %pad_maximum_fusion.16), channel_id=1, source_target_pairs={{0,16},{1,17},{2,18},{3,19},{4,20},{5,21},{6,22},{7,23},{8,24},{9,... | collective-permute-start | bytes 3145736 | tf_op jit(solution)/shard_map/ppermute | solution.py:545
  453.4 17.5 %collective-permute-start.81 = (bf16[128,1408]{1,0:T(8,128)(2,1)}, bf16[128,1408]{1,0:T(8,128)(2,1)S(1)}, u32[]{:S(2)}, u32[]{:S(2)}) collective-permute-start(bf16[128,1408]{1,0:T(8,128)(2,1)} %reduce-scatter.5.cloned.1.call-done), channel_id=1, source_target_pairs={{0,16},{1,17},{2,18},{3,19},{4,20},{5,21},{6,22},{7,23},{8,24},{9,... | collective-permute-start | bytes 1081352 | tf_op jit(solution)/shard_map/ppermute | solution.py:545
  455.0 15.8 %collective-permute-start.79 = (bf16[3,64,512]{2,1,0:T(8,128)(2,1)}, bf16[3,64,512]{2,1,0:T(8,128)(2,1)S(1)}, u32[]{:S(2)}, u32[]{:S(2)}) collective-permute-start(bf16[3,64,512]{2,1,0:T(8,128)(2,1)} %get-tuple-element.452), channel_id=1, source_target_pairs={{0,8},{4,12},{8,0},{12,4},{1,9},{5,13},{9,1},{13,5},{2,10},{6,14},... | collective-permute-start | bytes 589832 | tf_op jit(solution)/shard_map/ppermute | solution.py:29
  455.1 15.7 %collective-permute-start.80 = (bf16[3,64,512]{2,1,0:T(8,128)(2,1)}, bf16[3,64,512]{2,1,0:T(8,128)(2,1)S(1)}, u32[]{:S(2)}, u32[]{:S(2)}) collective-permute-start(bf16[3,64,512]{2,1,0:T(8,128)(2,1)} %get-tuple-element.449), channel_id=1, source_target_pairs={{0,4},{4,8},{8,12},{12,0},{1,5},{5,9},{9,13},{13,1},{2,6},{6,10},{... | collective-permute-start | bytes 589832 | tf_op jit(solution)/shard_map/ppermute | solution.py:29
  458.9 11.9 %collective-permute-start.82 = (bf16[128,960]{1,0:T(8,128)(2,1)}, bf16[128,960]{1,0:T(8,128)(2,1)S(1)}, u32[]{:S(2)}, u32[]{:S(2)}) collective-permute-start(bf16[128,960]{1,0:T(8,128)(2,1)} %reduce-scatter.7.cloned.1.call-done), channel_id=1, source_target_pairs={{0,16},{1,17},{2,18},{3,19},{4,20},{5,21},{6,22},{7,23},{8,24},{9,... | collective-permute-start | bytes 737288 | tf_op jit(solution)/shard_map/ppermute | solution.py:545
  475.4 12.3 %collective-permute-start.84 = (bf16[144,1024]{1,0:T(8,128)(2,1)S(1)}, bf16[144,1024]{1,0:T(8,128)(2,1)S(1)}, u32[]{:S(2)}, u32[]{:S(2)}) collective-permute-start(bf16[144,1024]{1,0:T(8,128)(2,1)S(1)} %get-tuple-element.407), channel_id=1, source_target_pairs={{0,2},{1,3},{2,0},{3,1},{4,6},{5,7},{6,4},{7,5},{8,10},{9,11},{10,... | collective-permute-start | bytes 884744 | tf_op jit(solution)/shard_map/ppermute | solution.py:24
  476.9 10.8 %collective-permute-start.85 = (bf16[144,1024]{1,0:T(8,128)(2,1)S(1)}, bf16[144,1024]{1,0:T(8,128)(2,1)S(1)}, u32[]{:S(2)}, u32[]{:S(2)}) collective-permute-start(bf16[144,1024]{1,0:T(8,128)(2,1)S(1)} %get-tuple-element.406), channel_id=1, source_target_pairs={{0,3},{1,2},{2,1},{3,0},{4,7},{5,6},{6,5},{7,4},{8,11},{9,10},{10,... | collective-permute-start | bytes 884744 | tf_op jit(solution)/shard_map/ppermute | solution.py:24
  488.7 14.0 %collective-permute-start.88 = (bf16[128,768]{1,0:T(8,128)(2,1)S(1)}, bf16[128,768]{1,0:T(8,128)(2,1)S(1)}, u32[]{:S(2)}, u32[]{:S(2)}) collective-permute-start(bf16[128,768]{1,0:T(8,128)(2,1)S(1)} %get-tuple-element.443), channel_id=1, source_target_pairs={{0,4},{4,8},{8,12},{12,0},{1,5},{5,9},{9,13},{13,1},{2,6},{6,10},{... | collective-permute-start | bytes 589832 | tf_op jit(solution)/shard_map/ppermute | solution.py:29
  489.0 22.2 %collective-permute-start.89 = (bf16[128,768]{1,0:T(8,128)(2,1)S(1)}, bf16[128,768]{1,0:T(8,128)(2,1)S(1)}, u32[]{:S(2)}, u32[]{:S(2)}) collective-permute-start(bf16[128,768]{1,0:T(8,128)(2,1)S(1)} %get-tuple-element.442), channel_id=1, source_target_pairs={{0,8},{4,12},{8,0},{12,4},{1,9},{5,13},{9,1},{13,5},{2,10},{6,14},... | collective-permute-start | bytes 589832 | tf_op jit(solution)/shard_map/ppermute | solution.py:29
  490.9 20.3 %collective-permute-start.90 = (bf16[128,768]{1,0:T(8,128)(2,1)S(1)}, bf16[128,768]{1,0:T(8,128)(2,1)}, u32[]{:S(2)}, u32[]{:S(2)}) collective-permute-start(bf16[128,768]{1,0:T(8,128)(2,1)S(1)} %get-tuple-element.441), channel_id=1, source_target_pairs={{0,12},{4,0},{8,4},{12,8},{1,13},{5,1},{9,5},{13,9},{2,14},{6,2},{... | collective-permute-start | bytes 589832 | tf_op jit(solution)/shard_map/ppermute | solution.py:29
  493.8 17.4 %collective-permute-start.86 = (bf16[128,1024]{1,0:T(8,128)(2,1)S(1)}, bf16[128,1024]{1,0:T(8,128)(2,1)S(1)}, u32[]{:S(2)}, u32[]{:S(2)}) collective-permute-start(bf16[128,1024]{1,0:T(8,128)(2,1)S(1)} %fusion.85), channel_id=1, source_target_pairs={{0,1},{1,0},{2,3},{3,2},{4,5},{5,4},{6,7},{7,6},{8,9},{9,8},{10,11... | collective-permute-start | bytes 786440 | tf_op jit(solution)/shard_map/ppermute | solution.py:24
  498.0 28.8 %collective-permute-start.92 = (bf16[128,1024]{1,0:T(8,128)(2,1)S(1)}, bf16[128,1024]{1,0:T(8,128)(2,1)}, u32[]{:S(2)}, u32[]{:S(2)}) collective-permute-start(bf16[128,1024]{1,0:T(8,128)(2,1)S(1)} %fusion.85), channel_id=1, source_target_pairs={{0,2},{1,3},{2,0},{3,1},{4,6},{5,7},{6,4},{7,5},{8,10},{9,11},{10,... | collective-permute-start | bytes 786440 | tf_op jit(solution)/shard_map/ppermute | solution.py:24
  502.7 23.8 %collective-permute-start.94 = (bf16[128,1408]{1,0:T(8,128)(2,1)S(1)}, bf16[128,1408]{1,0:T(8,128)(2,1)S(1)}, u32[]{:S(2)}, u32[]{:S(2)}) collective-permute-start(bf16[128,1408]{1,0:T(8,128)(2,1)S(1)} %get-tuple-element.480), channel_id=1, source_target_pairs={{16,0},{17,1},{18,2},{19,3},{20,4},{21,5},{22,6},{23,7},{24,8},{25... | collective-permute-start | bytes 1081352 | tf_op jit(solution)/shard_map/ppermute | solution.py:542
  511.3 11.0 %collective-permute-start.97 = (f32[2,256]{1,0:T(2,128)S(1)}, f32[2,256]{1,0:T(2,128)S(1)}, u32[]{:S(2)}, u32[]{:S(2)}) collective-permute-start(f32[2,256]{1,0:T(2,128)S(1)} %get-tuple-element.553), channel_id=1, source_target_pairs={{0,4},{4,8},{8,12},{12,0},{1,5},{5,9},{9,13},{13,1},{2,6},{6,10},{... | collective-permute-start | bytes 6152 | tf_op jit(solution)/shard_map/ppermute | solution.py:29
  529.8 14.1 %collective-permute-start.101 = (bf16[128,960]{1,0:T(8,128)(2,1)}, bf16[128,960]{1,0:T(8,128)(2,1)}, u32[]{:S(2)}, u32[]{:S(2)}) collective-permute-start(bf16[128,960]{1,0:T(8,128)(2,1)} %reduce-scatter.11.cloned.1.call-done), channel_id=1, source_target_pairs={{16,0},{17,1},{18,2},{19,3},{20,4},{21,5},{22,6},{23,7},{24,8},{25... | collective-permute-start | bytes 737288 | tf_op jit(solution)/shard_map/ppermute | solution.py:542
  535.2 11.7 %collective-permute-start.100 = (bf16[512,1024]{1,0:T(8,128)(2,1)}, bf16[512,1024]{1,0:T(8,128)(2,1)}, u32[]{:S(2)}, u32[]{:S(2)}) collective-permute-start(bf16[512,1024]{1,0:T(8,128)(2,1)} %constant_dynamic-update-slice_fusion.8), channel_id=1, source_target_pairs={{16,0},{17,1},{18,2},{19,3},{20,4},{21,5},{22,6},{23,7},{24,8},{25... | collective-permute-start | bytes 3145736 | tf_op jit(solution)/shard_map/ppermute | solution.py:542
  (148 other events, 1161.3 us)
Sparse Core Ops, SparseCore 0:
  73.3 56.0 all-gather.3
  131.5 27.7 all-gather.5
  191.3 55.3 all-gather.7
  301.6 38.7 reduce-scatter.6
  342.5 44.5 reduce-scatter.4
  400.6 61.2 reduce-scatter.8
  464.8 51.0 reduce-scatter.10

commit v3 on v2

--- a/solution.py
+++ b/solution.py
@@ -61,23 +61,14 @@
     return total if work is None else (total, done)
 
 
-def gather_tokens(own, work=None, operands=(), second=None, second_operands=()):
+def gather_tokens(own, work=lambda: (), operands=()):
     n = lax.axis_size("head")
 
     def exchange(x):
         return [head_peer(x, k) for k in range(1, n)]
 
-    if work is None:
-        return jnp.concatenate([own] + exchange(own), axis=0)
-    if second is None:
-        got, done = beside(exchange, own, work, operands)
-        return jnp.concatenate([own] + got, axis=0), done
-    own, operands = barrier((own, operands))
-    got = exchange(own)
-    done = work(*operands)
-    got[0], second_operands = barrier((got[0], second_operands))
-    got, done, also = barrier((got, done, second(*second_operands)))
-    return jnp.concatenate([own] + got, axis=0), done, also
+    got, done = beside(exchange, own, work, operands)
+    return jnp.concatenate([own] + got, axis=0), done
 
 
 def gather_features(own, work=lambda: (), operands=()):
@@ -116,7 +107,7 @@
     return jnp.stack(seq_blocks(x), axis=0)
 
 
-def to_heads(x, work, operands=(), held=()):
+def to_heads(x, work, operands=()):
     n = lax.axis_size("seq")
     me = lax.axis_index("seq")
 
@@ -126,28 +117,21 @@
 
         return [block(0)] + [seq_shift(block(k), k) for k in range(1, n)]
 
-    x, operands = barrier((x, operands))
-    got = exchange(x)
-    got[1], held = barrier((got[1], held))
-    got, done = barrier((got, work(*operands)))
-    return jnp.stack(got, axis=0), done, held
-
-
-def to_tokens(x, work, operands=(), second=lambda: (), second_operands=()):
+    got, done = beside(exchange, x, work, operands)
+    return jnp.stack(got, axis=0), done
+
+
+def to_tokens(x, work, operands=()):
     n = lax.axis_size("seq")
     me = lax.axis_index("seq")
 
     def exchange(x):
         return [x[0]] + [seq_shift(x[k], -k) for k in range(1, n)]
 
-    x, operands = barrier((x, operands))
-    got = exchange(x)
-    done = work(*operands)
-    got[1], second_operands = barrier((got[1], second_operands))
-    got, done, also = barrier((got, done, second(*second_operands)))
+    got, done = beside(exchange, x, work, operands)
     parts = jnp.stack(got, axis=0)
     out = [lax.dynamic_index_in_dim(parts, (h - me) % n, 0, keepdims=False) for h in range(n)]
-    return jnp.stack(out, axis=0), done, also
+    return jnp.stack(out, axis=0), done
 
 
 def visible(block, xor, lo_token, queries, size):
@@ -391,29 +375,6 @@
     return lax.psum_scatter(by_rows(grad), ("seq", "section"), scatter_dimension=0, tiled=True)
 
 
-def add_cores(grad):
-    core = lax.axis_index("section")
-    n = lax.axis_size("seq")
-    grad = grad.reshape(n, 2, grad.shape[0] // (2 * n), grad.shape[1])
-    mine = lax.dynamic_index_in_dim(grad, core, 1, keepdims=False)
-    other = core_swap(lax.dynamic_index_in_dim(grad, 1 - core, 1, keepdims=False))
-    return (mine.astype(F32) + other.astype(F32)).astype(BF16)
-
-
-def scatter_devices(total):
-    seq = lax.axis_index("seq")
-    n = lax.axis_size("seq")
-
-    def block(k):
-        return lax.dynamic_index_in_dim(total, (seq + k) % n, 0, keepdims=False)
-
-    return [block(0)] + [seq_shift(block(k), k) for k in range(1, n)]
-
-
-def add_up(parts):
-    return sum((p.astype(F32) for p in parts[1:]), parts[0].astype(F32)).astype(BF16)
-
-
 def on_device(
     inputs, positions, cotangent, qkv_weight, out_weight, gate_up_weight, down_weight,
     attn_gain, ffn_gain,
@@ -435,16 +396,18 @@
     )
     attn_shard = jnp.concatenate([qkv_shard, out_weight[0]], axis=1)
     attn_half, attn_later = split_layers(attn_shard)
+    (
+        attn_half, inputs, cotangent, positions, gate_up_weight, down_weight, attn_gain, ffn_gain,
+    ) = barrier(
+        (attn_half, inputs, cotangent, positions, gate_up_weight, down_weight, attn_gain, ffn_gain)
+    )
+    first = seq_blocks(attn_half)
     pos = lax.dynamic_index_in_dim(positions, core, 0, keepdims=False)
     gain = jnp.stack([attn_gain[0], ffn_gain[0]]).astype(F32)
     gain_other = core_swap(gain)
     small = jnp.where(core == 0, jnp.stack([gain, gain_other]), jnp.stack([gain_other, gain]))
     small = jnp.concatenate([peer_order(pos).astype(F32), small.reshape(4 * own)])
     small = seq_slots(small)
-    attn_half, inputs, cotangent, gate_up_weight, down_weight = barrier(
-        (attn_half, inputs, cotangent, gate_up_weight, down_weight)
-    )
-    first = seq_blocks(attn_half)
     ffn_shard = jnp.concatenate(
         [gate_up_weight[0].reshape(own, 2 * hidden), down_weight[0]], axis=1
     )
@@ -509,7 +472,7 @@
 
     def mix(packed, out_mine, in_slots, held):
         if by_head:
-            query, out_all, _ = to_heads(packed, gather_peers, (out_mine,))
+            query, out_all = to_heads(packed, gather_peers, (out_mine,))
             query = query[None]
             key_value = query
         else:
@@ -524,7 +487,7 @@
             return join_halves(out_all, in_slots)
 
         if by_head:
-            ob, w_out, _ = to_tokens(ob[0], join, (out_all,))
+            ob, w_out = to_tokens(ob[0], join, (out_all,))
         else:
             ob, w_out = ob[:, 0], join(out_all)
         return ob.reshape(local, rows), w_out, (query, key_value, o, lse), held
@@ -578,8 +541,7 @@
             g_gate_up, g_gain = grad_rows(n2, dgu), gain_rows(dn, n2, gain[layer, 1])
             if layer:
                 return g_gate_up, g_gain
-            g_gate_up = by_rows(jnp.concatenate([g_gate_up, before[1]], axis=1))
-            return g_gate_up, g_gain, to_second(before[3])
+            return g_gate_up, g_gain, to_second(before[2])
 
         dn2 = dot(dgu, w_gate_up, ((1,), (1,))).astype(BF16)
         dn2, (g_gate_up, g_ffn_gain, *y_other) = reduce_tokens(dn2, beside_ffn, (dn2, n2, dgu))
@@ -601,15 +563,13 @@
             return jnp.concatenate([g_out, g_down], axis=1)
 
         if by_head:
-            dob, g_rest, late = to_heads(dob, grad_rest, (ghb, ob, g_down), late)
+            dob, g_rest = to_heads(dob, grad_rest, (ghb, ob, g_down))
             dob = dob[None]
         else:
             g_rest = grad_rest(ghb, ob, g_down)
             dob = dob[:, None]
-        dob, g_rest = barrier((dob, g_rest))
-        rest_rows = scatter_rows(g_rest)
         if layer:
-            y_part, y_hid = late
+            dob, (y_part, y_hid) = barrier((dob, late))
             y_own = (y_hid + reduce_tokens(y_part)).astype(BF16)
         dq, dk, dv = attend_grad(scalars, query, key_value, pos_rows, o, dob, lse)
         if layer:
@@ -628,14 +588,15 @@
         else:
             dv = (dv + gfirst.astype(F32)).astype(BF16)
         packed = jnp.stack([dq, dk, dv], axis=1)
-        if by_head and layer:
-            packed, _, y = to_tokens(packed, lambda: (), (), gather_tokens, (y_own,))
-        elif by_head:
-            packed, _, rows_other = to_tokens(packed, lambda: (), (), to_second_all, before[0])
-        elif layer:
-            y = gather_tokens(y_own)
+
+        def beside_packed(*values):
+            return gather_tokens(*values)[0] if layer else to_second_all(*values)
+
+        values = (y_own,) if layer else before[0]
+        if by_head:
+            packed, moved = to_tokens(packed, beside_packed, values)
         else:
-            rows_other = to_second_all(*before[0])
+            moved = beside_packed(*values)
         dqkv = packed.reshape(3 * local, rows)
 
         dn1 = dot(dqkv, w_qkv, ((0,), (1,))).astype(BF16)
@@ -644,20 +605,20 @@
 
         def grad_qkv(n1, dqkv):
             g_qkv = dot(n1, dqkv, ((0,), (1,))).astype(BF16)
-            return g_qkv if layer else scatter_devices(add_cores(g_qkv))
-
+            return by_rows(jnp.concatenate([g_rest, g_qkv], axis=1))
+
+        dn1, n1, dqkv = barrier((dn1, n1, dqkv))
+        g_last = grad_qkv(n1, dqkv)
         if layer:
-            dn1, g_qkv = reduce_tokens(dn1, grad_qkv, (n1, dqkv))
+            dn1 = reduce_tokens(dn1)
         else:
-            gains = jnp.concatenate([gains, before[2]], axis=0)
+            gains = jnp.concatenate([gains, before[1]], axis=0)
             high = gains.astype(BF16)
             low = (gains - high.astype(F32)).astype(BF16)
             tail = jnp.concatenate([high, low, jnp.zeros((8, width), BF16)], axis=0)
             dn1 = jnp.concatenate([dn1.reshape(peers, part, width)] + [
                 jnp.broadcast_to(tail[None], (peers, 16, width))
             ], axis=1).reshape(peers * (part + 16), width)
-            dn1, n1, dqkv = barrier((dn1, n1, dqkv))
-            qkv_parts = grad_qkv(n1, dqkv)
             dn1 = reduce_tokens(dn1)
             gains = dn1[part : part + 4] + dn1[part + 4 : part + 8]
             dn1 = dn1[:part]
@@ -666,32 +627,16 @@
         e1 = dn1 * gain[layer, 0]
         gx = gh + r1 * (e1 - c1 * jnp.mean(e1 * c1, axis=-1, keepdims=True))
         gx = gx.astype(BF16)
+        g_last, gate_up_rows = barrier((g_last, gate_up_rows))
+        last_rows = scatter_rows(g_last)
         if layer:
-            return gather_tokens(gx), dv, (gate_up_rows, rest_rows), g_qkv, gains, y
-
-        def beside_last(gate_up_rows, gains):
-            gains = gains.reshape(2, 2, width)
-            mine = lax.dynamic_index_in_dim(gains, core, 0, keepdims=False)
-            other = lax.dynamic_index_in_dim(gains, 1 - core, 0, keepdims=False)
-            gate_up, qkv = columns(gate_up_rows, 2 * hidden, 3 * local)
-            gate_up = settle(gate_up, to_first(gate_up), before[0][0], rows_other[0])
-            return rows_of(gate_up), qkv, to_second(qkv), mine + core_swap(other)
-
-        def then(qkv_parts, gains):
-            qkv = add_up(qkv_parts)
-            return qkv, to_first(qkv), add_devices(gains)
-
-        n = peers
-        gx, gate_up_rows, gains = barrier((gx, gate_up_rows, gains))
-        got = [head_peer(gx, k) for k in range(1, n)]
-        gate_up, qkv1, qkv1_other, gains = beside_last(gate_up_rows, gains)
-        got[0], qkv_parts, gains = barrier((got[0], qkv_parts, gains))
-        qkv0, qkv0_other, gains = then(qkv_parts, gains)
-        got, gate_up, qkv, gains, rest_rows = barrier(
-            (got, gate_up, (qkv0, qkv0_other, qkv1, qkv1_other), gains, rest_rows)
-        )
-        gx = jnp.concatenate([gx] + got, axis=0)
-        return gx, gate_up, qkv, gains, rest_rows, y_other[0], gx_other[0], rows_other[1]
+            return gather_tokens(gx)[0], dv, (gate_up_rows, last_rows), gains, moved
+
+        def beside_last(gate_up):
+            return rows_of(settle(gate_up, to_first(gate_up), before[0][0], moved[0]))
+
+        gx, gate_up = gather_tokens(gx, beside_last, (gate_up_rows,))
+        return gx, gate_up, last_rows, gains, y_other[0], gx_other[0], moved[1]
 
     def rows_of(pair):
         return jnp.concatenate(pair, axis=0).astype(F32)
@@ -710,7 +655,7 @@
     ob0, attn_later = barrier((ob0, attn_later))
     attn_later = gather_rows(attn_later)
     y_part, fed0 = feed(0, x0, gather_features(ob0)[0], w_out0, gate_up0, down0)
-    y0 = gather_tokens((fed0[0] + reduce_tokens(y_part)).astype(BF16))
+    y0, _ = gather_tokens((fed0[0] + reduce_tokens(y_part)).astype(BF16))
     qkv1, out1 = columns(attn_later, 3 * local, local)
     out1 = lax.dynamic_index_in_dim(
         out1.reshape(devices, 2, own // 2, local), core, 1, keepdims=False
@@ -722,32 +667,31 @@
     y_part, fed1 = feed(1, y0, ob_all, w_out1, gate_up1, down1)
     kept0 = (x0[:part].astype(F32), n1_0, attn0, ob0, w_out0, fed0, w_qkv_first, gate_up0, down0)
     kept1 = (y0[:part].astype(F32), n1_1, attn1, ob1, w_out1, fed1, qkv1, gate_up1, down1)
-    gx1, gfirst, rows1, g_qkv1, gains1, y1 = backward(
-        1, gy1, None, kept1, (y_part, fed1[0]), ()
-    )
-    gx0, gate_up_grad, qkv, gains, rest_rows, y1_second, gx1_second, rest_second = backward(
-        0, gx1, gfirst, kept0, (), (rows1, g_qkv1, gains1, y1)
+    gx1, gfirst, rows1, gains1, y1 = backward(1, gy1, None, kept1, (y_part, fed1[0]), ())
+    gx0, gate_up_grad, last_rows, gains, y1_second, gx1_second, last_second = backward(
+        0, gx1, gfirst, kept0, (), (rows1, gains1, y1)
     )
 
     def tokens_of(pair, dtype):
         return jnp.stack([peer_order(m).astype(dtype) for m in pair])[None]
 
     activations = tokens_of(settle(y0, y0_first, y1, y1_second), BF16)
-    gx0_first, rest_first = to_first(gx0), to_first(rest_rows)
+    gx0_first = to_first(gx0)
     input_grads = tokens_of(settle(gx0, gx0_first, gx1, gx1_second), F32)
+    gains = gains.reshape(2, 2, width)
+    gains = lax.dynamic_index_in_dim(gains, core, 0, keepdims=False) + core_swap(
+        lax.dynamic_index_in_dim(gains, 1 - core, 0, keepdims=False)
+    )
+    gains = add_devices(gains)
     gate_up_grad = gate_up_grad.reshape(1, own, 2, hidden)
+    last = rows_of(settle(last_rows, to_first(last_rows), rows1[1], last_second))
+    out_grad, down_grad, qkv_grad = columns(last, local, hidden, 3 * local)
+    out_grad, down_grad = out_grad[None], down_grad[None]
     qkv_grad = (
-        rows_of(settle(*qkv))
-        .reshape(1, own, heads, 3, HEAD_DIM)
+        qkv_grad.reshape(1, own, heads, 3, HEAD_DIM)
         .transpose(0, 1, 3, 2, 4)
         .reshape(1, own, 3, local)
     )
-    out_grad, down_grad = [
-        g[None]
-        for g in columns(
-            rows_of(settle(rest_rows, rest_first, rows1[1], rest_second)), local, hidden
-        )
-    ]
     return (
         activations,
         input_grads,

time: 568 us -> 545 us (0.960)
  starting transfers between devices: 138 us -> 127 us
  waiting for transfers between devices: 223 us -> 215 us
  local copies, waits for them, and re-layouts: 41.5 us -> 34.1 us
    ppermute x36 -> x33, waiting for transfers between devices: 103 us -> 76.8 us  [seq_shift(): return lax.ppermute(x, 'seq', [(i, (i + k) % n) for i in range(n)])]
    ppermute x48, waiting for transfers between devices: 104 us -> 115 us  [head_peer(): return lax.ppermute(x, 'head', [(i, i ^ k) for i in range(n)])]
    ppermute x36 -> x33, starting transfers between devices: 64.1 us -> 56 us  [seq_shift(): return lax.ppermute(x, 'seq', [(i, (i + k) % n) for i in range(n)])]
    unnamed x240 -> x187, local copies, waits for them, and re-layouts: 18.7 us -> 17.9 us
  transfers between devices with their start and end apart: 109 -> 103, of which waited for: 49 -> 53; matrix products, arithmetic and copies ran while one was open for 19% -> 20% of each run, Pallas kernels for 6% -> 7%
where the time goes in v3:
time: 545 us; the launch traced here: 536 us
  waiting for transfers between devices  215 us (39%)
  starting transfers between devices  127 us (23%)
  other arithmetic  60.7 us (11%)
  matrix products  47.3 us (9%)
  Pallas kernels  35.6 us (7%)
  local copies, waits for them, and re-layouts  34.1 us (6%)
  between operations  17 us (3%)
    ppermute x48, waiting for transfers between devices, head_peer(): return lax.ppermute(x, 'head', [(i, i ^ k) for i in range(n)])  115 us
    ppermute x33, waiting for transfers between devices, seq_shift(): return lax.ppermute(x, 'seq', [(i, (i + k) % n) for i in range(n)])  76.8 us
    ppermute x48, starting transfers between devices, head_peer(): return lax.ppermute(x, 'head', [(i, i ^ k) for i in range(n)])  57.2 us
    ppermute x33, starting transfers between devices, seq_shift(): return lax.ppermute(x, 'seq', [(i, (i + k) % n) for i in range(n)])  56 us
    dot_general x24, matrix products, dot(): return lax.dot_general(a, b, (dims, ((), ())), preferred_element_type=F32)  47.3 us
    pallas_call x2, Pallas kernels, attend_grad(): pl.pallas_call(grad_kernel, grid_spec=pltpu.PrefetchScalarGridSpec(num_sc...  20.1 us
    unnamed x187, local copies, waits for them, and re-layouts  17.9 us
    all_gather x3, waiting for transfers between devices, gather_rows(): return lax.all_gather(by_rows(half), ('seq', 'section'), axis=0, tiled=True)  17 us
  transfers between devices with their start and end apart: 103, of which 53 were waited for; matrix products, arithmetic and copies ran while one was open for 20% of the time, Pallas kernels for 7%

profile of v3, /device:TPU:0, one launch (start us, length us, event | category | flops | bytes accessed | tf_op | source)
XLA Modules:
  0.0 536.2 jit_solution(13819892296159050519)
XLA Ops:
  11.2 2.9 collective-permute-start.5
  14.1 2.6 collective-permute-start.6
  28.8 5.8 %collective-permute-done.3 = f32[1536]{0:T(1024)S(1)} collective-permute-done((f32[1536]{0:T(1024)S(1)}, f32[1536]{0:T(1024)S(1)}, u32[]{:S(2)}, u32[]{:S(2)}) %collective-permute-start.3) | collective-permute-done | bytes 6176 | tf_op jit(solution)/shard_map/ppermute | solution.py:29
  35.9 8.8 %collective-permute-done.7 = bf16[128,1024]{1,0:T(8,128)(2,1)S(1)} collective-permute-done((bf16[128,1024]{1,0:T(8,128)(2,1)S(1)}, bf16[128,1024]{1,0:T(8,128)(2,1)S(1)}, u32[]{:S(2)}, u32[]{:S(2)}) %collective-permute-start.7) | collective-permute-done | bytes 262176 | tf_op jit(solution)/shard_map/ppermute | solution.py:29
  56.3 3.4 collective-permute-start.10
  64.2 4.1 collective-permute-done.13
  71.1 2.6 collective-permute-done.9
  74.9 7.8 %attend.2 = (f32[1,4,64,512]{3,2,1,0:T(8,128)S(1)}, bf16[1,4,64,512]{3,2,1,0:T(8,128)(2,1)S(1)}, f32[1,4,1,512]{3,2,1,0:T(1,128)S(1)}) custom-call(s32[4]{0:T(128)S(1)} %gather_fusion, s32[4]{0:T(128)S(1)} %get-tuple-element.555.qslot.kslot, s32[4]{0:T(128)S(1)} %get-tuple-element.555.qslot.kslot, s32[2]{0:T(128)S(1)} %pad_add_fusion.base, ...), custom_call_target="tpu_custom_call" | custom-call | flops 1073741824 | bytes 1572864 | tf_op jit(solution)/shard_map/attend/pallas_call | solution.py:260
  85.1 2.9 collective-permute-start.17
  92.2 9.0 %collective-permute-done.17 = bf16[64,512]{1,0:T(8,128)(2,1)S(1)} collective-permute-done((bf16[64,512]{1,0:T(8,128)(2,1)S(1)}, bf16[64,512]{1,0:T(8,128)(2,1)S(1)}, u32[]{:S(2)}, u32[]{:S(2)}) %collective-permute-start.17) | collective-permute-done | bytes 65568 | tf_op jit(solution)/shard_map/ppermute | solution.py:29
  105.2 5.4 %collective-permute-done.20 = bf16[256,512]{1,0:T(8,128)(2,1)S(1)} collective-permute-done((bf16[256,512]{1,0:T(8,128)(2,1)S(1)}, bf16[256,512]{1,0:T(8,128)(2,1)S(1)}, u32[]{:S(2)}, u32[]{:S(2)}) %collective-permute-start.20) | collective-permute-done | bytes 262176 | tf_op jit(solution)/shard_map/ppermute | solution.py:24
  110.6 5.5 %collective-permute-done.21 = bf16[256,512]{1,0:T(8,128)(2,1)S(1)} collective-permute-done((bf16[256,512]{1,0:T(8,128)(2,1)S(1)}, bf16[256,512]{1,0:T(8,128)(2,1)S(1)}, u32[]{:S(2)}, u32[]{:S(2)}) %collective-permute-start.21) | collective-permute-done | bytes 262176 | tf_op jit(solution)/shard_map/ppermute | solution.py:24
  116.3 3.1 multiply_reduce_fusion.5
  121.0 9.6 %all-gather.4.cloned.1.call-done = bf16[1024,2112]{1,0:T(8,128)(2,1)} async-done(((bf16[128,2112]{1,0:T(8,128)(2,1)}), bf16[1024,2112]{1,0:T(8,128)(2,1)}) %all-gather.4.cloned.1.call-update) | async-done | bytes 4325392 | tf_op jit(solution)/shard_map/all_gather | solution.py:336
  130.6 3.6 fusion.6
  134.8 3.2 convolution_convert_fusion.9
  141.6 5.7 %collective-permute-done.23 = bf16[128,1024]{1,0:T(8,128)(2,1)S(1)} collective-permute-done((bf16[128,1024]{1,0:T(8,128)(2,1)S(1)}, bf16[128,1024]{1,0:T(8,128)(2,1)S(1)}, u32[]{:S(2)}, u32[]{:S(2)}) %collective-permute-start.23) | collective-permute-done | bytes 262176 | tf_op jit(solution)/shard_map/ppermute | solution.py:24
  147.3 6.1 %collective-permute-done.24 = bf16[128,1024]{1,0:T(8,128)(2,1)S(1)} collective-permute-done((bf16[128,1024]{1,0:T(8,128)(2,1)S(1)}, bf16[128,1024]{1,0:T(8,128)(2,1)S(1)}, u32[]{:S(2)}, u32[]{:S(2)}) %collective-permute-start.24) | collective-permute-done | bytes 262176 | tf_op jit(solution)/shard_map/ppermute | solution.py:24
  161.7 2.8 collective-permute-done.26
  164.5 5.0 collective-permute-done.27
  178.0 3.8 collective-permute-done.32
  186.2 4.6 collective-permute-done.30
  191.0 7.8 %attend.3 = (f32[1,4,64,512]{3,2,1,0:T(8,128)S(1)}, bf16[1,4,64,512]{3,2,1,0:T(8,128)(2,1)S(1)}, f32[1,4,1,512]{3,2,1,0:T(1,128)S(1)}) custom-call(s32[4]{0:T(128)S(1)} %gather_fusion, s32[4]{0:T(128)S(1)} %get-tuple-element.555.qslot.kslot, s32[4]{0:T(128)S(1)} %get-tuple-element.555.qslot.kslot, s32[2]{0:T(128)S(1)} %pad_add_fusion.base, ...), custom_call_target="tpu_custom_call" | custom-call | flops 1073741824 | bytes 1572864 | tf_op jit(solution)/shard_map/attend/pallas_call | solution.py:260
  198.9 4.4 collective-permute-start.35
  208.1 9.9 %collective-permute-done.36 = bf16[64,512]{1,0:T(8,128)(2,1)S(1)} collective-permute-done((bf16[64,512]{1,0:T(8,128)(2,1)S(1)}, bf16[64,512]{1,0:T(8,128)(2,1)S(1)}, u32[]{:S(2)}, u32[]{:S(2)}) %collective-permute-start.36) | collective-permute-done | bytes 65568 | tf_op jit(solution)/shard_map/ppermute | solution.py:29
  219.8 2.4 collective-permute-start.39
  224.9 4.1 collective-permute-done.39
  228.9 8.0 %collective-permute-done.40 = bf16[256,512]{1,0:T(8,128)(2,1)S(1)} collective-permute-done((bf16[256,512]{1,0:T(8,128)(2,1)S(1)}, bf16[256,512]{1,0:T(8,128)(2,1)S(1)}, u32[]{:S(2)}, u32[]{:S(2)}) %collective-permute-start.40) | collective-permute-done | bytes 262176 | tf_op jit(solution)/shard_map/ppermute | solution.py:24
  241.9 5.5 %all-gather.8.cloned.1.call-done = bf16[1024,2112]{1,0:T(8,128)(2,1)} async-done(((bf16[128,2112]{1,0:T(8,128)(2,1)}), bf16[1024,2112]{1,0:T(8,128)(2,1)}) %all-gather.8.cloned.1.call-update) | async-done | bytes 4325392 | tf_op jit(solution)/shard_map/all_gather | solution.py:336
  247.5 4.1 fusion.2
  261.4 3.4 convolution_convert_fusion.1
  264.8 2.6 collective-permute-done.43
  267.4 6.1 %collective-permute-done.44 = bf16[128,1024]{1,0:T(8,128)(2,1)} collective-permute-done((bf16[128,1024]{1,0:T(8,128)(2,1)}, bf16[128,1024]{1,0:T(8,128)(2,1)}, u32[]{:S(2)}, u32[]{:S(2)}) %collective-permute-start.44) | collective-permute-done | bytes 262176 | tf_op jit(solution)/shard_map/ppermute | solution.py:24
  273.5 2.3 fusion.177
  275.8 2.5 fusion.175
  279.8 2.5 convolution_convert_fusion.8
  286.9 4.7 collective-permute-done.46
  291.6 4.9 collective-permute-done.47
  303.0 3.5 collective-permute-done.49
  312.1 10.1 %attend_grad.2 = (f32[1,4,64,512]{3,2,1,0:T(8,128)S(1)}, f32[1,4,64,512]{3,2,1,0:T(8,128)S(1)}, f32[1,4,64,512]{3,2,1,0:T(8,128)S(1)}) custom-call(s32[4]{0:T(128)S(1)} %gather_fusion, s32[4]{0:T(128)S(1)} %get-tuple-element.555.qslot.kslot, s32[4]{0:T(128)S(1)} %get-tuple-element.555.qslot.kslot, s32[2]{0:T(128)S(1)} %pad_add_fusion.base, ...), custom_call_target="tpu_custom_call" | custom-call | flops 2684354560 | bytes 3145728 | tf_op jit(solution)/shard_map/attend_grad/pallas_call | solution.py:287
  327.7 3.1 collective-permute-start.55
  332.2 3.0 collective-permute-start.57
  337.3 8.4 %collective-permute-done.56 = bf16[3,64,512]{2,1,0:T(8,128)(2,1)S(1)} collective-permute-done((bf16[3,64,512]{2,1,0:T(8,128)(2,1)S(1)}, bf16[3,64,512]{2,1,0:T(8,128)(2,1)S(1)}, u32[]{:S(2)}, u32[]{:S(2)}) %collective-permute-start.56) | collective-permute-done | bytes 196640 | tf_op jit(solution)/shard_map/ppermute | solution.py:29
  350.8 2.9 pad_maximum_fusion
  358.6 5.7 %collective-permute-done.61 = bf16[128,1024]{1,0:T(8,128)(2,1)S(1)} collective-permute-done((bf16[128,1024]{1,0:T(8,128)(2,1)S(1)}, bf16[128,1024]{1,0:T(8,128)(2,1)S(1)}, u32[]{:S(2)}, u32[]{:S(2)}) %collective-permute-start.61) | collective-permute-done | bytes 262176 | tf_op jit(solution)/shard_map/ppermute | solution.py:24
  364.3 4.7 collective-permute-done.62
  375.3 2.6 collective-permute-start.70
  377.9 2.6 collective-permute-done.64
  380.5 4.1 collective-permute-done.65
  384.6 3.0 multiply_convert_fusion.3
  394.8 3.5 convolution_convert_fusion
  398.6 3.6 collective-permute-done.68
  403.7 2.4 fusion.174
  415.5 4.5 collective-permute-done.72
  422.1 3.7 collective-permute-start.77
  431.5 10.1 %attend_grad.3 = (f32[1,4,64,512]{3,2,1,0:T(8,128)S(1)}, f32[1,4,64,512]{3,2,1,0:T(8,128)S(1)}, f32[1,4,64,512]{3,2,1,0:T(8,128)S(1)}) custom-call(s32[4]{0:T(128)S(1)} %gather_fusion, s32[4]{0:T(128)S(1)} %get-tuple-element.555.qslot.kslot, s32[4]{0:T(128)S(1)} %get-tuple-element.555.qslot.kslot, s32[2]{0:T(128)S(1)} %pad_add_fusion.base, ...), custom_call_target="tpu_custom_call" | custom-call | flops 2684354560 | bytes 3145728 | tf_op jit(solution)/shard_map/attend_grad/pallas_call | solution.py:287
  444.4 3.0 collective-permute-start.78
  452.3 10.3 %collective-permute-done.79 = bf16[3,64,512]{2,1,0:T(8,128)(2,1)S(1)} collective-permute-done((bf16[3,64,512]{2,1,0:T(8,128)(2,1)S(1)}, bf16[3,64,512]{2,1,0:T(8,128)(2,1)S(1)}, u32[]{:S(2)}, u32[]{:S(2)}) %collective-permute-start.79) | collective-permute-done | bytes 196640 | tf_op jit(solution)/shard_map/ppermute | solution.py:29
  467.8 2.9 pad_maximum_fusion.1
  478.3 5.2 collective-permute-done.83
  483.4 5.6 %collective-permute-done.84 = bf16[144,1024]{1,0:T(8,128)(2,1)S(1)} collective-permute-done((bf16[144,1024]{1,0:T(8,128)(2,1)S(1)}, bf16[144,1024]{1,0:T(8,128)(2,1)S(1)}, u32[]{:S(2)}, u32[]{:S(2)}) %collective-permute-start.84) | collective-permute-done | bytes 294944 | tf_op jit(solution)/shard_map/ppermute | solution.py:24
  499.0 4.3 collective-permute-done.87
  504.1 2.6 broadcast_select_fusion.1
  510.5 2.8 collective-permute-start.95
  (563 shorter events, 217.4 us)
Async XLA Ops:
  7.2 123.4 %all-gather.4.cloned.1.call-start = ((), (), s32[]{:S(2)}) async-start(), calls=%async_computation.4 | async-start | bytes 5013504 | tf_op jit(solution)/shard_map/all_gather | solution.py:336
  11.2 24.7 %collective-permute-start.5 = (bf16[128,1024]{1,0:T(8,128)(2,1)S(1)}, bf16[128,1024]{1,0:T(8,128)(2,1)S(1)}, u32[]{:S(2)}, u32[]{:S(2)}) collective-permute-start(bf16[128,1024]{1,0:T(8,128)(2,1)S(1)} %get-tuple-element.177), channel_id=1, source_target_pairs={{0,4},{4,8},{8,12},{12,0},{1,5},{5,9},{9,13},{13,1},{2,6},{6,10},{... | collective-permute-start | bytes 786440 | tf_op jit(solution)/shard_map/ppermute | solution.py:29
  14.1 21.8 %collective-permute-start.6 = (bf16[128,1024]{1,0:T(8,128)(2,1)S(1)}, bf16[128,1024]{1,0:T(8,128)(2,1)}, u32[]{:S(2)}, u32[]{:S(2)}) collective-permute-start(bf16[128,1024]{1,0:T(8,128)(2,1)S(1)} %get-tuple-element.177), channel_id=1, source_target_pairs={{0,8},{4,12},{8,0},{12,4},{1,9},{5,13},{9,1},{13,5},{2,10},{6,14},... | collective-permute-start | bytes 786440 | tf_op jit(solution)/shard_map/ppermute | solution.py:29
  22.0 12.6 %collective-permute-start.3 = (f32[1536]{0:T(1024)S(1)}, f32[1536]{0:T(1024)S(1)}, u32[]{:S(2)}, u32[]{:S(2)}) collective-permute-start(f32[1536]{0:T(1024)S(1)} %pad_maximum_fusion.37), channel_id=1, source_target_pairs={{0,8},{4,12},{8,0},{12,4},{1,9},{5,13},{9,1},{13,5},{2,10},{6,14},... | collective-permute-start | bytes 18440 | tf_op jit(solution)/shard_map/ppermute | solution.py:29
  23.9 10.7 %collective-permute-start.4 = (f32[1536]{0:T(1024)S(1)}, f32[1536]{0:T(1024)S(1)}, u32[]{:S(2)}, u32[]{:S(2)}) collective-permute-start(f32[1536]{0:T(1024)S(1)} %pad_maximum_fusion.37), channel_id=1, source_target_pairs={{0,12},{4,0},{8,4},{12,8},{1,13},{5,1},{9,5},{13,9},{2,14},{6,2},{... | collective-permute-start | bytes 18440 | tf_op jit(solution)/shard_map/ppermute | solution.py:29
  28.8 16.0 %collective-permute-start.7 = (bf16[128,1024]{1,0:T(8,128)(2,1)S(1)}, bf16[128,1024]{1,0:T(8,128)(2,1)S(1)}, u32[]{:S(2)}, u32[]{:S(2)}) collective-permute-start(bf16[128,1024]{1,0:T(8,128)(2,1)S(1)} %get-tuple-element.177), channel_id=1, source_target_pairs={{0,12},{4,0},{8,4},{12,8},{1,13},{5,1},{9,5},{13,9},{2,14},{6,2},{... | collective-permute-start | bytes 786440 | tf_op jit(solution)/shard_map/ppermute | solution.py:29
  34.6 18.3 %collective-permute-start.15 = (bf16[128,2112]{0,1:T(8,128)(2,1)}, bf16[128,2112]{0,1:T(8,128)(2,1)}, u32[]{:S(2)}, u32[]{:S(2)}) collective-permute-start(bf16[128,2112]{0,1:T(8,128)(2,1)} %copy.94), channel_id=1, source_target_pairs={{0,16},{16,0},{1,17},{17,1},{2,18},{18,2},{3,19},{19,3},{4,20},{20... | collective-permute-start | bytes 1622024 | tf_op jit(solution)/shard_map/ppermute | solution.py:33
  54.2 14.1 %collective-permute-start.13 = (bf16[4,128,256]{2,1,0:T(8,128)(2,1)}, bf16[4,128,256]{2,1,0:T(8,128)(2,1)S(1)}, u32[]{:S(2)}, u32[]{:S(2)}) collective-permute-start(bf16[4,128,256]{2,1,0:T(8,128)(2,1)} %pad_maximum_fusion.27), channel_id=1, source_target_pairs={{0,2},{1,3},{2,0},{3,1},{4,6},{5,7},{6,4},{7,5},{8,10},{9,11},{10,... | collective-permute-start | bytes 786440 | tf_op jit(solution)/shard_map/ppermute | solution.py:24
  55.8 12.5 %collective-permute-start.14 = (bf16[4,128,256]{2,1,0:T(8,128)(2,1)}, bf16[4,128,256]{2,1,0:T(8,128)(2,1)S(1)}, u32[]{:S(2)}, u32[]{:S(2)}) collective-permute-start(bf16[4,128,256]{2,1,0:T(8,128)(2,1)} %pad_maximum_fusion.27), channel_id=1, source_target_pairs={{0,3},{1,2},{2,1},{3,0},{4,7},{5,6},{6,5},{7,4},{8,11},{9,10},{10,... | collective-permute-start | bytes 786440 | tf_op jit(solution)/shard_map/ppermute | solution.py:24
  56.3 14.7 %collective-permute-start.10 = (bf16[3,64,512]{2,1,0:T(8,128)(2,1)S(1)}, bf16[3,64,512]{2,1,0:T(8,128)(2,1)S(1)}, u32[]{:S(2)}, u32[]{:S(2)}) collective-permute-start(bf16[3,64,512]{2,1,0:T(8,128)(2,1)S(1)} %get-tuple-element.454), channel_id=1, source_target_pairs={{0,8},{4,12},{8,0},{12,4},{1,9},{5,13},{9,1},{13,5},{2,10},{6,14},... | collective-permute-start | bytes 589832 | tf_op jit(solution)/shard_map/ppermute | solution.py:29
  59.8 11.3 %collective-permute-start.11 = (bf16[3,64,512]{2,1,0:T(8,128)(2,1)S(1)}, bf16[3,64,512]{2,1,0:T(8,128)(2,1)S(1)}, u32[]{:S(2)}, u32[]{:S(2)}) collective-permute-start(bf16[3,64,512]{2,1,0:T(8,128)(2,1)S(1)} %get-tuple-element.453), channel_id=1, source_target_pairs={{0,12},{4,0},{8,4},{12,8},{1,13},{5,1},{9,5},{13,9},{2,14},{6,2},{... | collective-permute-start | bytes 589832 | tf_op jit(solution)/shard_map/ppermute | solution.py:29
  61.0 12.8 %collective-permute-start.9 = (bf16[3,64,512]{2,1,0:T(8,128)(2,1)S(1)}, bf16[3,64,512]{2,1,0:T(8,128)(2,1)S(1)}, u32[]{:S(2)}, u32[]{:S(2)}) collective-permute-start(bf16[3,64,512]{2,1,0:T(8,128)(2,1)S(1)} %get-tuple-element.455), channel_id=1, source_target_pairs={{0,4},{4,8},{8,12},{12,0},{1,5},{5,9},{9,13},{13,1},{2,6},{6,10},{... | collective-permute-start | bytes 589832 | tf_op jit(solution)/shard_map/ppermute | solution.py:29
  73.9 86.7 %all-gather.6.cloned.1.call-start = ((), (), s32[]{:S(2)}) async-start(), calls=%async_computation.5 | async-start | bytes 2359296 | tf_op jit(solution)/shard_map/all_gather | solution.py:336
  85.1 16.1 %collective-permute-start.17 = (bf16[64,512]{1,0:T(8,128)(2,1)S(1)}, bf16[64,512]{1,0:T(8,128)(2,1)S(1)}, u32[]{:S(2)}, u32[]{:S(2)}) collective-permute-start(bf16[64,512]{1,0:T(8,128)(2,1)S(1)} %get-tuple-element.514), channel_id=1, source_target_pairs={{0,8},{4,12},{8,0},{12,4},{1,9},{5,13},{9,1},{13,5},{2,10},{6,14},... | collective-permute-start | bytes 196616 | tf_op jit(solution)/shard_map/ppermute | solution.py:29
  88.1 13.1 %collective-permute-start.18 = (bf16[64,512]{1,0:T(8,128)(2,1)S(1)}, bf16[64,512]{1,0:T(8,128)(2,1)S(1)}, u32[]{:S(2)}, u32[]{:S(2)}) collective-permute-start(bf16[64,512]{1,0:T(8,128)(2,1)S(1)} %get-tuple-element.513), channel_id=1, source_target_pairs={{0,4},{4,8},{8,12},{12,0},{1,5},{5,9},{9,13},{13,1},{2,6},{6,10},{... | collective-permute-start | bytes 196616 | tf_op jit(solution)/shard_map/ppermute | solution.py:29
  102.9 13.2 %collective-permute-start.21 = (bf16[256,512]{1,0:T(8,128)(2,1)S(1)}, bf16[256,512]{1,0:T(8,128)(2,1)S(1)}, u32[]{:S(2)}, u32[]{:S(2)}) collective-permute-start(bf16[256,512]{1,0:T(8,128)(2,1)S(1)} %bitcast.455), channel_id=1, source_target_pairs={{0,2},{1,3},{2,0},{3,1},{4,6},{5,7},{6,4},{7,5},{8,10},{9,11},{10,... | collective-permute-start | bytes 786440 | tf_op jit(solution)/shard_map/ppermute | solution.py:24
  104.4 11.7 %collective-permute-start.22 = (bf16[256,512]{1,0:T(8,128)(2,1)S(1)}, bf16[256,512]{1,0:T(8,128)(2,1)S(1)}, u32[]{:S(2)}, u32[]{:S(2)}) collective-permute-start(bf16[256,512]{1,0:T(8,128)(2,1)S(1)} %bitcast.456), channel_id=1, source_target_pairs={{0,3},{1,2},{2,1},{3,0},{4,7},{5,6},{6,5},{7,4},{8,11},{9,10},{10,... | collective-permute-start | bytes 786440 | tf_op jit(solution)/shard_map/ppermute | solution.py:24
  104.9 142.5 %all-gather.8.cloned.1.call-start = ((), (), s32[]{:S(2)}) async-start(), calls=%async_computation.6 | async-start | bytes 5013504 | tf_op jit(solution)/shard_map/all_gather | solution.py:336
  139.6 13.8 %collective-permute-start.24 = (bf16[128,1024]{1,0:T(8,128)(2,1)S(1)}, bf16[128,1024]{1,0:T(8,128)(2,1)S(1)}, u32[]{:S(2)}, u32[]{:S(2)}) collective-permute-start(bf16[128,1024]{1,0:T(8,128)(2,1)S(1)} %get-tuple-element.430), channel_id=1, source_target_pairs={{0,2},{1,3},{2,0},{3,1},{4,6},{5,7},{6,4},{7,5},{8,10},{9,11},{10,... | collective-permute-start | bytes 786440 | tf_op jit(solution)/shard_map/ppermute | solution.py:24
  141.1 12.3 %collective-permute-start.25 = (bf16[128,1024]{1,0:T(8,128)(2,1)S(1)}, bf16[128,1024]{1,0:T(8,128)(2,1)S(1)}, u32[]{:S(2)}, u32[]{:S(2)}) collective-permute-start(bf16[128,1024]{1,0:T(8,128)(2,1)S(1)} %get-tuple-element.429), channel_id=1, source_target_pairs={{0,3},{1,2},{2,1},{3,0},{4,7},{5,6},{6,5},{7,4},{8,11},{9,10},{10,... | collective-permute-start | bytes 786440 | tf_op jit(solution)/shard_map/ppermute | solution.py:24
  156.4 13.1 %collective-permute-start.27 = (bf16[128,1024]{1,0:T(8,128)(2,1)S(1)}, bf16[128,1024]{1,0:T(8,128)(2,1)S(1)}, u32[]{:S(2)}, u32[]{:S(2)}) collective-permute-start(bf16[128,1024]{1,0:T(8,128)(2,1)S(1)} %get-tuple-element.367), channel_id=1, source_target_pairs={{0,2},{1,3},{2,0},{3,1},{4,6},{5,7},{6,4},{7,5},{8,10},{9,11},{10,... | collective-permute-start | bytes 786440 | tf_op jit(solution)/shard_map/ppermute | solution.py:24
  157.3 12.2 %collective-permute-start.28 = (bf16[128,1024]{1,0:T(8,128)(2,1)S(1)}, bf16[128,1024]{1,0:T(8,128)(2,1)S(1)}, u32[]{:S(2)}, u32[]{:S(2)}) collective-permute-start(bf16[128,1024]{1,0:T(8,128)(2,1)S(1)} %get-tuple-element.367), channel_id=1, source_target_pairs={{0,3},{1,2},{2,1},{3,0},{4,7},{5,6},{6,5},{7,4},{8,11},{9,10},{10,... | collective-permute-start | bytes 786440 | tf_op jit(solution)/shard_map/ppermute | solution.py:24
  173.4 11.7 %collective-permute-start.33 = (bf16[4,128,256]{2,1,0:T(8,128)(2,1)S(1)}, bf16[4,128,256]{2,1,0:T(8,128)(2,1)S(1)}, u32[]{:S(2)}, u32[]{:S(2)}) collective-permute-start(bf16[4,128,256]{2,1,0:T(8,128)(2,1)S(1)} %dynamic-slice_bitcast_fusion.11), channel_id=1, source_target_pairs={{0,2},{1,3},{2,0},{3,1},{4,6},{5,7},{6,4},{7,5},{8,10},{9,11},{10,... | collective-permute-start | bytes 786440 | tf_op jit(solution)/shard_map/ppermute | solution.py:24
  174.8 10.3 %collective-permute-start.34 = (bf16[4,128,256]{2,1,0:T(8,128)(2,1)S(1)}, bf16[4,128,256]{2,1,0:T(8,128)(2,1)S(1)}, u32[]{:S(2)}, u32[]{:S(2)}) collective-permute-start(bf16[4,128,256]{2,1,0:T(8,128)(2,1)S(1)} %dynamic-slice_bitcast_fusion.11), channel_id=1, source_target_pairs={{0,3},{1,2},{2,1},{3,0},{4,7},{5,6},{6,5},{7,4},{8,11},{9,10},{10,... | collective-permute-start | bytes 786440 | tf_op jit(solution)/shard_map/ppermute | solution.py:24
  176.4 14.3 %collective-permute-start.30 = (bf16[3,64,512]{2,1,0:T(8,128)(2,1)S(1)}, bf16[3,64,512]{2,1,0:T(8,128)(2,1)S(1)}, u32[]{:S(2)}, u32[]{:S(2)}) collective-permute-start(bf16[3,64,512]{2,1,0:T(8,128)(2,1)S(1)} %get-tuple-element.448), channel_id=1, source_target_pairs={{0,8},{4,12},{8,0},{12,4},{1,9},{5,13},{9,1},{13,5},{2,10},{6,14},... | collective-permute-start | bytes 589832 | tf_op jit(solution)/shard_map/ppermute | solution.py:29
  190.9 162.8 %reduce-scatter.5.cloned.1.call-start = ((), (), s32[]{:S(2)}) async-start(), calls=%async_computation.7 | async-start | bytes 3244032 | tf_op jit(solution)/shard_map/reduce_scatter | solution.py:375
  203.3 14.7 %collective-permute-start.36 = (bf16[64,512]{1,0:T(8,128)(2,1)S(1)}, bf16[64,512]{1,0:T(8,128)(2,1)S(1)}, u32[]{:S(2)}, u32[]{:S(2)}) collective-permute-start(bf16[64,512]{1,0:T(8,128)(2,1)S(1)} %get-tuple-element.496), channel_id=1, source_target_pairs={{0,8},{4,12},{8,0},{12,4},{1,9},{5,13},{9,1},{13,5},{2,10},{6,14},... | collective-permute-start | bytes 196616 | tf_op jit(solution)/shard_map/ppermute | solution.py:29
  204.2 13.8 %collective-permute-start.37 = (bf16[64,512]{1,0:T(8,128)(2,1)S(1)}, bf16[64,512]{1,0:T(8,128)(2,1)S(1)}, u32[]{:S(2)}, u32[]{:S(2)}) collective-permute-start(bf16[64,512]{1,0:T(8,128)(2,1)S(1)} %get-tuple-element.495), channel_id=1, source_target_pairs={{0,4},{4,8},{8,12},{12,0},{1,5},{5,9},{9,13},{13,1},{2,6},{6,10},{... | collective-permute-start | bytes 196616 | tf_op jit(solution)/shard_map/ppermute | solution.py:29
  218.1 18.9 %collective-permute-start.42 = (bf16[512,1024]{1,0:T(8,128)(2,1)S(1)}, bf16[512,1024]{1,0:T(8,128)(2,1)S(1)}, u32[]{:S(2)}, u32[]{:S(2)}) collective-permute-start(bf16[512,1024]{1,0:T(8,128)(2,1)S(1)} %copy-done.1), channel_id=1, source_target_pairs={{16,0},{17,1},{18,2},{19,3},{20,4},{21,5},{22,6},{23,7},{24,8},{25... | collective-permute-start | bytes 3145736 | tf_op jit(solution)/shard_map/ppermute | solution.py:505
  222.2 14.7 %collective-permute-start.40 = (bf16[256,512]{1,0:T(8,128)(2,1)S(1)}, bf16[256,512]{1,0:T(8,128)(2,1)S(1)}, u32[]{:S(2)}, u32[]{:S(2)}) collective-permute-start(bf16[256,512]{1,0:T(8,128)(2,1)S(1)} %bitcast.460), channel_id=1, source_target_pairs={{0,2},{1,3},{2,0},{3,1},{4,6},{5,7},{6,4},{7,5},{8,10},{9,11},{10,... | collective-permute-start | bytes 786440 | tf_op jit(solution)/shard_map/ppermute | solution.py:24
  223.8 13.1 %collective-permute-start.41 = (bf16[256,512]{1,0:T(8,128)(2,1)S(1)}, bf16[256,512]{1,0:T(8,128)(2,1)S(1)}, u32[]{:S(2)}, u32[]{:S(2)}) collective-permute-start(bf16[256,512]{1,0:T(8,128)(2,1)S(1)} %bitcast.461), channel_id=1, source_target_pairs={{0,3},{1,2},{2,1},{3,0},{4,7},{5,6},{6,5},{7,4},{8,11},{9,10},{10,... | collective-permute-start | bytes 786440 | tf_op jit(solution)/shard_map/ppermute | solution.py:24
  259.4 14.1 %collective-permute-start.44 = (bf16[128,1024]{1,0:T(8,128)(2,1)}, bf16[128,1024]{1,0:T(8,128)(2,1)}, u32[]{:S(2)}, u32[]{:S(2)}) collective-permute-start(bf16[128,1024]{1,0:T(8,128)(2,1)} %get-tuple-element.426), channel_id=1, source_target_pairs={{0,2},{1,3},{2,0},{3,1},{4,6},{5,7},{6,4},{7,5},{8,10},{9,11},{10,... | collective-permute-start | bytes 786440 | tf_op jit(solution)/shard_map/ppermute | solution.py:24
  260.9 12.6 %collective-permute-start.45 = (bf16[128,1024]{1,0:T(8,128)(2,1)}, bf16[128,1024]{1,0:T(8,128)(2,1)}, u32[]{:S(2)}, u32[]{:S(2)}) collective-permute-start(bf16[128,1024]{1,0:T(8,128)(2,1)} %get-tuple-element.425), channel_id=1, source_target_pairs={{0,3},{1,2},{2,1},{3,0},{4,7},{5,6},{6,5},{7,4},{8,11},{9,10},{10,... | collective-permute-start | bytes 786440 | tf_op jit(solution)/shard_map/ppermute | solution.py:24
  278.4 164.7 %reduce-scatter.7.cloned.1.call-start = ((), (), s32[]{:S(2)}) async-start(), calls=%async_computation.8 | async-start | bytes 4128768 | tf_op jit(solution)/shard_map/reduce_scatter | solution.py:375
  283.5 13.0 %collective-permute-start.47 = (bf16[128,1024]{1,0:T(8,128)(2,1)S(1)}, bf16[128,1024]{1,0:T(8,128)(2,1)S(1)}, u32[]{:S(2)}, u32[]{:S(2)}) collective-permute-start(bf16[128,1024]{1,0:T(8,128)(2,1)S(1)} %copy-done.32), channel_id=1, source_target_pairs={{0,2},{1,3},{2,0},{3,1},{4,6},{5,7},{6,4},{7,5},{8,10},{9,11},{10,... | collective-permute-start | bytes 786440 | tf_op jit(solution)/shard_map/ppermute | solution.py:24
  284.4 12.1 %collective-permute-start.48 = (bf16[128,1024]{1,0:T(8,128)(2,1)S(1)}, bf16[128,1024]{1,0:T(8,128)(2,1)S(1)}, u32[]{:S(2)}, u32[]{:S(2)}) collective-permute-start(bf16[128,1024]{1,0:T(8,128)(2,1)S(1)} %copy-done.32), channel_id=1, source_target_pairs={{0,3},{1,2},{2,1},{3,0},{4,7},{5,6},{6,5},{7,4},{8,11},{9,10},{10,... | collective-permute-start | bytes 786440 | tf_op jit(solution)/shard_map/ppermute | solution.py:24
  298.4 10.1 %collective-permute-start.50 = (bf16[64,512]{1,0:T(8,128)(2,1)S(1)}, bf16[64,512]{1,0:T(8,128)(2,1)S(1)}, u32[]{:S(2)}, u32[]{:S(2)}) collective-permute-start(bf16[64,512]{1,0:T(8,128)(2,1)S(1)} %get-tuple-element.478), channel_id=1, source_target_pairs={{0,8},{4,12},{8,0},{12,4},{1,9},{5,13},{9,1},{13,5},{2,10},{6,14},... | collective-permute-start | bytes 196616 | tf_op jit(solution)/shard_map/ppermute | solution.py:29
  308.5 13.7 %collective-permute-start.52 = (bf16[128,1024]{1,0:T(8,128)(2,1)S(1)}, bf16[128,1024]{1,0:T(8,128)(2,1)S(1)}, u32[]{:S(2)}, u32[]{:S(2)}) collective-permute-start(bf16[128,1024]{1,0:T(8,128)(2,1)S(1)} %get-tuple-element.422), channel_id=1, source_target_pairs={{0,1},{1,0},{2,3},{3,2},{4,5},{5,4},{6,7},{7,6},{8,9},{9,8},{10,11... | collective-permute-start | bytes 786440 | tf_op jit(solution)/shard_map/ppermute | solution.py:24
  309.4 12.8 %collective-permute-start.53 = (bf16[128,1024]{1,0:T(8,128)(2,1)S(1)}, bf16[128,1024]{1,0:T(8,128)(2,1)S(1)}, u32[]{:S(2)}, u32[]{:S(2)}) collective-permute-start(bf16[128,1024]{1,0:T(8,128)(2,1)S(1)} %get-tuple-element.424), channel_id=1, source_target_pairs={{0,2},{1,3},{2,0},{3,1},{4,6},{5,7},{6,4},{7,5},{8,10},{9,11},{10,... | collective-permute-start | bytes 786440 | tf_op jit(solution)/shard_map/ppermute | solution.py:24
  310.9 11.4 %collective-permute-start.54 = (bf16[128,1024]{1,0:T(8,128)(2,1)S(1)}, bf16[128,1024]{1,0:T(8,128)(2,1)S(1)}, u32[]{:S(2)}, u32[]{:S(2)}) collective-permute-start(bf16[128,1024]{1,0:T(8,128)(2,1)S(1)} %get-tuple-element.423), channel_id=1, source_target_pairs={{0,3},{1,2},{2,1},{3,0},{4,7},{5,6},{6,5},{7,4},{8,11},{9,10},{10,... | collective-permute-start | bytes 786440 | tf_op jit(solution)/shard_map/ppermute | solution.py:24
  324.9 11.3 %collective-permute-start.59 = (bf16[128,1024]{1,0:T(8,128)(2,1)S(1)}, bf16[128,1024]{1,0:T(8,128)(2,1)S(1)}, u32[]{:S(2)}, u32[]{:S(2)}) collective-permute-start(bf16[128,1024]{1,0:T(8,128)(2,1)S(1)} %add_convert_fusion), channel_id=1, source_target_pairs={{0,2},{1,3},{2,0},{3,1},{4,6},{5,7},{6,4},{7,5},{8,10},{9,11},{10,... | collective-permute-start | bytes 786440 | tf_op jit(solution)/shard_map/ppermute | solution.py:24
  326.4 9.8 %collective-permute-start.60 = (bf16[128,1024]{1,0:T(8,128)(2,1)S(1)}, bf16[128,1024]{1,0:T(8,128)(2,1)S(1)}, u32[]{:S(2)}, u32[]{:S(2)}) collective-permute-start(bf16[128,1024]{1,0:T(8,128)(2,1)S(1)} %add_convert_fusion), channel_id=1, source_target_pairs={{0,3},{1,2},{2,1},{3,0},{4,7},{5,6},{6,5},{7,4},{8,11},{9,10},{10,... | collective-permute-start | bytes 786440 | tf_op jit(solution)/shard_map/ppermute | solution.py:24
  330.8 15.0 %collective-permute-start.56 = (bf16[3,64,512]{2,1,0:T(8,128)(2,1)S(1)}, bf16[3,64,512]{2,1,0:T(8,128)(2,1)S(1)}, u32[]{:S(2)}, u32[]{:S(2)}) collective-permute-start(bf16[3,64,512]{2,1,0:T(8,128)(2,1)S(1)} %get-tuple-element.444), channel_id=1, source_target_pairs={{0,8},{4,12},{8,0},{12,4},{1,9},{5,13},{9,1},{13,5},{2,10},{6,14},... | collective-permute-start | bytes 589832 | tf_op jit(solution)/shard_map/ppermute | solution.py:29
  332.2 13.6 %collective-permute-start.57 = (bf16[3,64,512]{2,1,0:T(8,128)(2,1)S(1)}, bf16[3,64,512]{2,1,0:T(8,128)(2,1)S(1)}, u32[]{:S(2)}, u32[]{:S(2)}) collective-permute-start(bf16[3,64,512]{2,1,0:T(8,128)(2,1)S(1)} %slice_bitcast_fusion.11), channel_id=1, source_target_pairs={{0,4},{4,8},{8,12},{12,0},{1,5},{5,9},{9,13},{13,1},{2,6},{6,10},{... | collective-permute-start | bytes 589832 | tf_op jit(solution)/shard_map/ppermute | solution.py:29
  353.7 117.0 %reduce-scatter.9.cloned.1.call-start = ((), (), s32[]{:S(2)}) async-start(), calls=%async_computation.9 | async-start | bytes 3244032 | tf_op jit(solution)/shard_map/reduce_scatter | solution.py:375
  356.7 12.3 %collective-permute-start.62 = (bf16[128,1024]{1,0:T(8,128)(2,1)S(1)}, bf16[128,1024]{1,0:T(8,128)(2,1)S(1)}, u32[]{:S(2)}, u32[]{:S(2)}) collective-permute-start(bf16[128,1024]{1,0:T(8,128)(2,1)S(1)} %get-tuple-element.417), channel_id=1, source_target_pairs={{0,2},{1,3},{2,0},{3,1},{4,6},{5,7},{6,4},{7,5},{8,10},{9,11},{10,... | collective-permute-start | bytes 786440 | tf_op jit(solution)/shard_map/ppermute | solution.py:24
  358.3 10.7 %collective-permute-start.63 = (bf16[128,1024]{1,0:T(8,128)(2,1)S(1)}, bf16[128,1024]{1,0:T(8,128)(2,1)S(1)}, u32[]{:S(2)}, u32[]{:S(2)}) collective-permute-start(bf16[128,1024]{1,0:T(8,128)(2,1)S(1)} %get-tuple-element.416), channel_id=1, source_target_pairs={{0,3},{1,2},{2,1},{3,0},{4,7},{5,6},{6,5},{7,4},{8,11},{9,10},{10,... | collective-permute-start | bytes 786440 | tf_op jit(solution)/shard_map/ppermute | solution.py:24
  373.1 11.5 %collective-permute-start.65 = (bf16[128,1024]{1,0:T(8,128)(2,1)S(1)}, bf16[128,1024]{1,0:T(8,128)(2,1)S(1)}, u32[]{:S(2)}, u32[]{:S(2)}) collective-permute-start(bf16[128,1024]{1,0:T(8,128)(2,1)S(1)} %fusion.91), channel_id=1, source_target_pairs={{0,2},{1,3},{2,0},{3,1},{4,6},{5,7},{6,4},{7,5},{8,10},{9,11},{10,... | collective-permute-start | bytes 786440 | tf_op jit(solution)/shard_map/ppermute | solution.py:24
  373.8 10.7 %collective-permute-start.66 = (bf16[128,1024]{1,0:T(8,128)(2,1)S(1)}, bf16[128,1024]{1,0:T(8,128)(2,1)S(1)}, u32[]{:S(2)}, u32[]{:S(2)}) collective-permute-start(bf16[128,1024]{1,0:T(8,128)(2,1)S(1)} %fusion.91), channel_id=1, source_target_pairs={{0,3},{1,2},{2,1},{3,0},{4,7},{5,6},{6,5},{7,4},{8,11},{9,10},{10,... | collective-permute-start | bytes 786440 | tf_op jit(solution)/shard_map/ppermute | solution.py:24
  375.3 26.9 %collective-permute-start.70 = (bf16[512,1024]{1,0:T(8,128)(2,1)}, bf16[512,1024]{1,0:T(8,128)(2,1)}, u32[]{:S(2)}, u32[]{:S(2)}) collective-permute-start(bf16[512,1024]{1,0:T(8,128)(2,1)} %pad_maximum_fusion.15), channel_id=1, source_target_pairs={{0,16},{1,17},{2,18},{3,19},{4,20},{5,21},{6,22},{7,23},{8,24},{9,... | collective-permute-start | bytes 3145736 | tf_op jit(solution)/shard_map/ppermute | solution.py:508
  391.8 10.4 %collective-permute-start.68 = (bf16[128,1024]{1,0:T(8,128)(2,1)}, bf16[128,1024]{1,0:T(8,128)(2,1)}, u32[]{:S(2)}, u32[]{:S(2)}) collective-permute-start(bf16[128,1024]{1,0:T(8,128)(2,1)} %get-tuple-element.413), channel_id=1, source_target_pairs={{0,2},{1,3},{2,0},{3,1},{4,6},{5,7},{6,4},{7,5},{8,10},{9,11},{10,... | collective-permute-start | bytes 786440 | tf_op jit(solution)/shard_map/ppermute | solution.py:24
  406.2 115.0 %reduce-scatter.11.cloned.1.call-start = ((), (), s32[]{:S(2)}) async-start(), calls=%async_computation.10 | async-start | bytes 4128768 | tf_op jit(solution)/shard_map/reduce_scatter | solution.py:375
  407.3 12.6 %collective-permute-start.74 = (bf16[512,1024]{1,0:T(8,128)(2,1)S(1)}, bf16[512,1024]{1,0:T(8,128)(2,1)S(1)}, u32[]{:S(2)}, u32[]{:S(2)}) collective-permute-start(bf16[512,1024]{1,0:T(8,128)(2,1)S(1)} %pad_maximum_fusion.16), channel_id=1, source_target_pairs={{0,16},{1,17},{2,18},{3,19},{4,20},{5,21},{6,22},{7,23},{8,24},{9,... | collective-permute-start | bytes 3145736 | tf_op jit(solution)/shard_map/ppermute | solution.py:508
  443.0 19.6 %collective-permute-start.82 = (bf16[128,1728]{1,0:T(8,128)(2,1)}, bf16[128,1728]{1,0:T(8,128)(2,1)S(1)}, u32[]{:S(2)}, u32[]{:S(2)}) collective-permute-start(bf16[128,1728]{1,0:T(8,128)(2,1)} %reduce-scatter.7.cloned.1.call-done), channel_id=1, source_target_pairs={{0,16},{1,17},{2,18},{3,19},{4,20},{5,21},{6,22},{7,23},{8,24},{9,... | collective-permute-start | bytes 1327112 | tf_op jit(solution)/shard_map/ppermute | solution.py:508
  447.4 15.2 %collective-permute-start.81 = (bf16[128,1408]{1,0:T(8,128)(2,1)S(1)}, bf16[128,1408]{1,0:T(8,128)(2,1)S(1)}, u32[]{:S(2)}, u32[]{:S(2)}) collective-permute-start(bf16[128,1408]{1,0:T(8,128)(2,1)S(1)} %copy-done.57), channel_id=1, source_target_pairs={{0,16},{1,17},{2,18},{3,19},{4,20},{5,21},{6,22},{7,23},{8,24},{9,... | collective-permute-start | bytes 1081352 | tf_op jit(solution)/shard_map/ppermute | solution.py:508
  448.7 13.9 %collective-permute-start.79 = (bf16[3,64,512]{2,1,0:T(8,128)(2,1)S(1)}, bf16[3,64,512]{2,1,0:T(8,128)(2,1)S(1)}, u32[]{:S(2)}, u32[]{:S(2)}) collective-permute-start(bf16[3,64,512]{2,1,0:T(8,128)(2,1)S(1)} %get-tuple-element.437), channel_id=1, source_target_pairs={{0,8},{4,12},{8,0},{12,4},{1,9},{5,13},{9,1},{13,5},{2,10},{6,14},... | collective-permute-start | bytes 589832 | tf_op jit(solution)/shard_map/ppermute | solution.py:29
  449.4 13.2 %collective-permute-start.80 = (bf16[3,64,512]{2,1,0:T(8,128)(2,1)S(1)}, bf16[3,64,512]{2,1,0:T(8,128)(2,1)S(1)}, u32[]{:S(2)}, u32[]{:S(2)}) collective-permute-start(bf16[3,64,512]{2,1,0:T(8,128)(2,1)S(1)} %slice_bitcast_fusion.10), channel_id=1, source_target_pairs={{0,4},{4,8},{8,12},{12,0},{1,5},{5,9},{9,13},{13,1},{2,6},{6,10},{... | collective-permute-start | bytes 589832 | tf_op jit(solution)/shard_map/ppermute | solution.py:29
  473.4 10.0 %collective-permute-start.83 = (bf16[144,1024]{1,0:T(8,128)(2,1)S(1)}, bf16[144,1024]{1,0:T(8,128)(2,1)S(1)}, u32[]{:S(2)}, u32[]{:S(2)}) collective-permute-start(bf16[144,1024]{1,0:T(8,128)(2,1)S(1)} %get-tuple-element.395), channel_id=1, source_target_pairs={{0,1},{1,0},{2,3},{3,2},{4,5},{5,4},{6,7},{7,6},{8,9},{9,8},{10,11... | collective-permute-start | bytes 884744 | tf_op jit(solution)/shard_map/ppermute | solution.py:24
  475.0 14.1 %collective-permute-start.84 = (bf16[144,1024]{1,0:T(8,128)(2,1)S(1)}, bf16[144,1024]{1,0:T(8,128)(2,1)S(1)}, u32[]{:S(2)}, u32[]{:S(2)}) collective-permute-start(bf16[144,1024]{1,0:T(8,128)(2,1)S(1)} %get-tuple-element.397), channel_id=1, source_target_pairs={{0,2},{1,3},{2,0},{3,1},{4,6},{5,7},{6,4},{7,5},{8,10},{9,11},{10,... | collective-permute-start | bytes 884744 | tf_op jit(solution)/shard_map/ppermute | solution.py:24
  476.4 12.6 %collective-permute-start.85 = (bf16[144,1024]{1,0:T(8,128)(2,1)S(1)}, bf16[144,1024]{1,0:T(8,128)(2,1)S(1)}, u32[]{:S(2)}, u32[]{:S(2)}) collective-permute-start(bf16[144,1024]{1,0:T(8,128)(2,1)S(1)} %get-tuple-element.396), channel_id=1, source_target_pairs={{0,3},{1,2},{2,1},{3,0},{4,7},{5,6},{6,5},{7,4},{8,11},{9,10},{10,... | collective-permute-start | bytes 884744 | tf_op jit(solution)/shard_map/ppermute | solution.py:24
  491.2 12.1 %collective-permute-start.87 = (bf16[128,1024]{1,0:T(8,128)(2,1)S(1)}, bf16[128,1024]{1,0:T(8,128)(2,1)S(1)}, u32[]{:S(2)}, u32[]{:S(2)}) collective-permute-start(bf16[128,1024]{1,0:T(8,128)(2,1)S(1)} %fusion.86), channel_id=1, source_target_pairs={{0,2},{1,3},{2,0},{3,1},{4,6},{5,7},{6,4},{7,5},{8,10},{9,11},{10,... | collective-permute-start | bytes 786440 | tf_op jit(solution)/shard_map/ppermute | solution.py:24
  491.9 12.2 %collective-permute-start.88 = (bf16[128,1024]{1,0:T(8,128)(2,1)S(1)}, bf16[128,1024]{1,0:T(8,128)(2,1)}, u32[]{:S(2)}, u32[]{:S(2)}) collective-permute-start(bf16[128,1024]{1,0:T(8,128)(2,1)S(1)} %fusion.86), channel_id=1, source_target_pairs={{0,3},{1,2},{2,1},{3,0},{4,7},{5,6},{6,5},{7,4},{8,11},{9,10},{10,... | collective-permute-start | bytes 786440 | tf_op jit(solution)/shard_map/ppermute | solution.py:24
  493.3 14.6 %collective-permute-start.92 = (f32[2,1024]{1,0:T(2,128)S(1)}, f32[2,1024]{1,0:T(2,128)S(1)}, u32[]{:S(2)}, u32[]{:S(2)}) collective-permute-start(f32[2,1024]{1,0:T(2,128)S(1)} %fusion.159), channel_id=1, source_target_pairs={{0,16},{16,0},{1,17},{17,1},{2,18},{18,2},{3,19},{19,3},{4,20},{20... | collective-permute-start | bytes 24584 | tf_op jit(solution)/shard_map/ppermute | solution.py:33
  506.6 10.5 %collective-permute-start.90 = (bf16[512,1024]{1,0:T(8,128)(2,1)}, bf16[512,1024]{1,0:T(8,128)(2,1)}, u32[]{:S(2)}, u32[]{:S(2)}) collective-permute-start(bf16[512,1024]{1,0:T(8,128)(2,1)} %get-tuple-element.403), channel_id=1, source_target_pairs={{16,0},{17,1},{18,2},{19,3},{20,4},{21,5},{22,6},{23,7},{24,8},{25... | collective-permute-start | bytes 3145736 | tf_op jit(solution)/shard_map/ppermute | solution.py:505
  (117 other events, 888.8 us)
Sparse Core Ops, SparseCore 0:
  74.0 56.6 all-gather.3
  132.8 27.7 all-gather.5
  191.1 56.3 all-gather.7
  278.5 40.0 reduce-scatter.4
  353.8 43.4 reduce-scatter.6
  406.3 41.1 reduce-scatter.8
  470.8 43.6 reduce-scatter.10
